TPU v7x, 32 devices: a whole 2x2x4 slice. The times are simulated.
32 devices in a mesh: seq: 16 (over z, y, x), tp: 2 (over core).
Axes of the slice: x: 2, y: 2, z: 4, core: 2. Of those that a mesh axis runs over, the one named last changes fastest.
Arguments:
- inputs: bfloat16 [16384, 768], P('seq'), may hold values from -6 to 6
- cotangent: bfloat16 [16384, 768], P('seq'), may hold values from -6 to 6
- query_weight: bfloat16 [768, 768], P(None, 'tp'), may hold values from -0.21875 to 0.21875
- key_weight: bfloat16 [768, 768], P(None, 'tp'), may hold values from -0.21875 to 0.21875
- value_weight: bfloat16 [768, 768], P(None, 'tp'), may hold values from -0.21875 to 0.21875
- out_weight: bfloat16 [768, 768], P('tp'), may hold values from -0.21875 to 0.21875
- up_weight: bfloat16 [768, 3072], P(None, 'tp'), may hold values from -0.21875 to 0.21875
- down_weight: bfloat16 [3072, 768], P('tp'), may hold values from -0.21875 to 0.21875
- conv_taps: float32 [12, 33], P('tp'), may hold values from -1 to 1
- attn_gain: float32 [768], replicated, may hold values from 0.5 to 1.5
- attn_shift: float32 [768], replicated, may hold values from -1 to 1
- ffn_gain: float32 [768], replicated, may hold values from 0.5 to 1.5
- ffn_shift: float32 [768], replicated, may hold values from -1 to 1
- hyperplanes: bfloat16 [32, 8, 64], replicated, may hold values from -6 to 6
- lengths: int32 [32], replicated, may hold values from 1 to 4096, 16384 in all
Outputs:
- output: bfloat16 [16384, 768], P('seq')
- grad_inputs: float32 [16384, 768], P('seq')
- grad_query: float32 [768, 768], P(None, 'tp')
- grad_key: float32 [768, 768], P(None, 'tp')
- grad_value: float32 [768, 768], P(None, 'tp')
- grad_out: float32 [768, 768], P('tp')
- grad_up: float32 [768, 3072], P(None, 'tp')
- grad_down: float32 [3072, 768], P('tp')
- grad_taps: float32 [12, 33], P('tp')
- grad_attn_gain: float32 [768], replicated
- grad_attn_shift: float32 [768], replicated
- grad_ffn_gain: float32 [768], replicated
- grad_ffn_shift: float32 [768], replicated
- occupancy: float32 [12, 32, 256], P('tp')
Inputs may be any that keep to these rules, and one draw needn't show every extreme that they name: The 32 lengths sum to 16384, and the longest is exactly 4096; sequences lie one after another along the tokens.
All inputs are finite; a program needn't handle non-finite values.
Results may differ from a plain program's by a relative error of at most 0.018.
Values may be sent and summed in bfloat16 or wider, within the bound.
A program may use at most 256 MiB of HBM per device.

v0:
```python
from functools import partial
import math

import jax
import jax.numpy as jnp
from jax import lax
from jax.sharding import PartitionSpec as P

TAU = 8
BITS = 8
CONV = 33
MOST = 4096


EPS_UNIT = 1e-06
EPS_LAYER = 1e-05
SHARP = 4.0
CLIP_EDGE = 0.999


def from_behind(block, axis, distance):
    devices = range(lax.axis_size(axis))
    route = [((i - distance) % len(devices), i) for i in devices]
    return lax.ppermute(block, axis, route)


def padded(block, sides, width):
    for axis, dim in sides:
        count = lax.axis_size(axis)
        forward = [(i, i + 1) for i in range(count - 1)]
        backward = [(target, source) for source, target in forward]
        low = lax.ppermute(
            lax.slice_in_dim(block, block.shape[dim] - width, None, axis=dim), axis, forward
        )
        high = lax.ppermute(lax.slice_in_dim(block, 0, width, axis=dim), axis, backward)
        block = jnp.concatenate([low, block, high], axis=dim)
    return block


def doc_ids(lengths, positions, all_tokens):
    doc_ends = jnp.cumsum(lengths)
    doc_index = jnp.sum((doc_ends[None, :] <= positions[:, None]).astype(jnp.int32), axis=1)
    inside = (positions >= 0) & (positions < all_tokens)
    return jnp.where(inside, doc_index, -1)


def unit_rows(vectors):
    return (
        vectors
        * lax.rsqrt(jnp.mean(vectors * vectors, axis=-1, keepdims=True) + EPS_UNIT)
        * (1.0 / math.sqrt(vectors.shape[-1]))
    )


def layer_norm(vectors, gain_row, shift_row):
    center = vectors - jnp.mean(vectors, axis=-1, keepdims=True)
    spread = jnp.mean(center * center, axis=-1, keepdims=True)
    return center * lax.rsqrt(spread + EPS_LAYER) * gain_row + shift_row


def collide_parts(scores):
    clipped = jnp.clip(scores, -CLIP_EDGE, CLIP_EDGE)
    return (clipped, 1.0 - jnp.arccos(clipped) * (1.0 / math.pi))


def inner_sum(left, right):
    return lax.dot_general(
        left, right, (((0,), (0,)), ((), ())), preferred_element_type=jnp.float32
    )


def back_dot(left, weight):
    return lax.dot_general(
        left, weight, (((1,), (1,)), ((), ())), preferred_element_type=jnp.float32
    )


def bucket_probs(bit_prob, bit_table):
    running = jnp.ones(bit_prob.shape[:-1] + (bit_table.shape[0],), jnp.float32)
    for bit_index in range(bit_table.shape[1]):
        chosen = bit_table[:, bit_index] == 1
        running = running * jnp.where(
            chosen,
            bit_prob[..., bit_index : bit_index + 1],
            1.0 - bit_prob[..., bit_index : bit_index + 1],
        )
    return running


def bucket_counts(key_unit, hyperplanes):
    half_bits = hyperplanes.shape[1] // 2
    bit_table = jnp.arange(2**half_bits)[:, None] // (2 ** jnp.arange(half_bits))[None, :] % 2
    projected = jnp.einsum(
        "thd,mbd->thmb", key_unit, hyperplanes, preferred_element_type=jnp.float32
    )
    bit_prob = jax.nn.sigmoid(SHARP * projected)
    low_half = bucket_probs(bit_prob[..., :half_bits], bit_table)
    high_half = bucket_probs(bit_prob[..., half_bits:], bit_table)
    counts = jnp.einsum("thmc,thme->hmec", low_half, high_half, precision=lax.Precision.HIGHEST)
    return counts.reshape(counts.shape[0], counts.shape[1], -1)


def attend_block(query_unit, key_unit, values, same_doc):

    def attend_compute(unused):
        scores = jnp.einsum(
            "qhd,khd->hqk", query_unit, key_unit, preferred_element_type=jnp.float32
        )
        clipped, collide = collide_parts(scores)
        weights = jnp.where(same_doc[None], collide**TAU, 0.0).astype(jnp.bfloat16)
        return jnp.einsum("hqk,khd->qhd", weights, values, preferred_element_type=jnp.float32)

    def attend_nothing(unused):
        return jnp.zeros(query_unit.shape, jnp.float32)

    return lax.cond(jnp.any(same_doc), attend_compute, attend_nothing, 0)


def back_block(query_unit, grad_rows, key_unit, values, same_doc):

    def back_compute(unused):
        scores = jnp.einsum(
            "qhd,khd->hqk", query_unit, key_unit, preferred_element_type=jnp.float32
        )
        clipped, collide = collide_parts(scores)
        inside = same_doc[None] & (jnp.abs(scores) <= CLIP_EDGE)
        kernel_slope = (
            TAU * collide ** (TAU - 1) * lax.rsqrt(1.0 - clipped * clipped) * (1.0 / math.pi)
        )
        grad_weights = jnp.einsum(
            "qhd,khd->hqk", grad_rows, values, preferred_element_type=jnp.float32
        )
        grad_scores = jnp.where(inside, grad_weights * kernel_slope, 0.0).astype(jnp.bfloat16)
        results = []
        results.append(
            jnp.einsum("hqk,khd->qhd", grad_scores, key_unit, preferred_element_type=jnp.float32)
        )
        weights = jnp.where(same_doc[None], collide**TAU, 0.0).astype(jnp.bfloat16)
        results.append(
            jnp.einsum("hqk,qhd->khd", grad_scores, query_unit, preferred_element_type=jnp.float32)
        )
        results.append(
            jnp.einsum("hqk,qhd->khd", weights, grad_rows, preferred_element_type=jnp.float32)
        )
        return tuple(results)

    def back_nothing(unused):
        results = []
        results.append(jnp.zeros(query_unit.shape, jnp.float32))
        results.append(jnp.zeros(key_unit.shape, jnp.float32))
        results.append(jnp.zeros(key_unit.shape, jnp.float32))
        return tuple(results)

    return lax.cond(jnp.any(same_doc), back_compute, back_nothing, 0)


def body(
    inputs,
    cotangent,
    query_weight,
    key_weight,
    value_weight,
    out_weight,
    up_weight,
    down_weight,
    conv_taps,
    attn_gain,
    attn_shift,
    ffn_gain,
    ffn_shift,
    hyperplanes,
    lengths,
):
    tokens = inputs.shape[0]
    head_count = conv_taps.shape[0]
    head_dim = hyperplanes.shape[2]
    head_shape = (tokens, head_count, head_dim)
    cycle_size = lax.axis_size("seq")
    my_index = lax.axis_index("seq")
    all_tokens = tokens * cycle_size
    far_reach = (MOST + tokens - 2) // tokens
    rim_width = (CONV - 1) // 2
    local_rows = jnp.arange(tokens, dtype=jnp.int32)
    own_ids = doc_ids(lengths, my_index * tokens + local_rows, all_tokens)
    own_same = own_ids[:, None] == own_ids[None, :]
    queries = jnp.dot(inputs, query_weight, preferred_element_type=jnp.float32).reshape(head_shape)
    keys_raw = jnp.dot(inputs, key_weight, preferred_element_type=jnp.float32).reshape(head_shape)
    values = (
        jnp.dot(inputs, value_weight, preferred_element_type=jnp.float32)
        .astype(jnp.bfloat16)
        .reshape(head_shape)
    )
    query_unit = unit_rows(queries).astype(jnp.bfloat16)
    key_unit = unit_rows(keys_raw).astype(jnp.bfloat16)
    occ_local = bucket_counts(key_unit, hyperplanes) * (2.0**BITS / all_tokens)
    gathered = attend_block(query_unit, key_unit, values, own_same)
    stored = []
    for direction in (1, -1):

        def forward_step(carried, travel):
            key_far, value_far, running = carried
            key_far, value_far = from_behind((key_far, value_far), "seq", direction)
            anchor = (my_index - direction * travel) % cycle_size
            far_ids = doc_ids(lengths, anchor * tokens + local_rows, all_tokens)
            running = running + attend_block(
                query_unit, key_far, value_far, own_ids[:, None] == far_ids[None, :]
            )
            return ((key_far, value_far, running), None)

        (unused_key, unused_value, gathered), saved = lax.scan(
            forward_step,
            (key_unit, values, gathered),
            jnp.arange(1, far_reach + 1, dtype=jnp.int32),
        )
        stored.append(saved)
    inv_norm = lax.rsqrt(jnp.mean(gathered * gathered, axis=-1, keepdims=True) + EPS_UNIT)
    normed = gathered * inv_norm
    value_rim = padded(values.reshape(tokens, head_count * head_dim), (("seq", 0),), rim_width)
    rim_values = value_rim.reshape(tokens + 2 * rim_width, head_count, head_dim)
    rim_ids = doc_ids(
        lengths,
        my_index * tokens - rim_width + jnp.arange(tokens + 2 * rim_width, dtype=jnp.int32),
        all_tokens,
    )
    convolved = jnp.zeros(head_shape, jnp.float32)
    for offset in range(CONV):
        same_doc = (rim_ids[offset : offset + tokens] == own_ids)[:, None, None]
        convolved = convolved + jnp.where(
            same_doc, conv_taps[None, :, offset, None] * rim_values[offset : offset + tokens], 0.0
        )
    mixed_heads = (normed + convolved).reshape(tokens, head_count * head_dim).astype(jnp.bfloat16)
    attn_out = lax.psum(jnp.dot(mixed_heads, out_weight, preferred_element_type=jnp.float32), "tp")
    first_norm, first_back = jax.vjp(
        layer_norm, inputs.astype(jnp.float32) + attn_out, attn_gain, attn_shift
    )
    first_low = first_norm.astype(jnp.bfloat16)
    hidden = jnp.dot(first_low, up_weight, preferred_element_type=jnp.float32)
    active = jax.nn.gelu(hidden, approximate=False).astype(jnp.bfloat16)
    ffn_out = lax.psum(
        jnp.dot(active, down_weight, preferred_element_type=jnp.float32).astype(jnp.bfloat16), "tp"
    ).astype(jnp.float32)
    result, second_back = jax.vjp(layer_norm, first_norm + ffn_out, ffn_gain, ffn_shift)
    output = result.astype(jnp.bfloat16)
    grad_second, grad_ffn_gain, grad_ffn_shift = second_back(cotangent.astype(jnp.float32))
    grad_ffn = grad_second.astype(jnp.bfloat16)
    grad_down = inner_sum(active, grad_ffn)
    grad_active = back_dot(grad_ffn, down_weight)
    unused_gelu, gelu_back = jax.vjp(partial(jax.nn.gelu, approximate=False), hidden)
    grad_hidden = gelu_back(grad_active)[0].astype(jnp.bfloat16)
    grad_up = inner_sum(first_low, grad_hidden)
    grad_first = grad_second + lax.psum(
        back_dot(grad_hidden, up_weight).astype(jnp.bfloat16), "tp"
    ).astype(jnp.float32)
    grad_residual, grad_attn_gain, grad_attn_shift = first_back(grad_first)
    grad_attn = grad_residual.astype(jnp.bfloat16)
    grad_out = inner_sum(mixed_heads, grad_attn)
    grad_mixed = back_dot(grad_attn, out_weight).astype(jnp.bfloat16)
    grad_heads = grad_mixed.reshape(head_shape).astype(jnp.float32)
    grad_rows = (
        inv_norm * grad_heads
        - inv_norm**3 * gathered * jnp.mean(grad_heads * gathered, axis=-1, keepdims=True)
    ).astype(jnp.bfloat16)
    grad_rim = padded(grad_mixed, (("seq", 0),), rim_width)
    grad_rim = grad_rim.reshape(tokens + 2 * rim_width, head_count, head_dim)
    grad_conv_values = jnp.zeros(head_shape, jnp.float32)
    tap_grads = []
    for offset in range(CONV):
        same_doc = (rim_ids[offset : offset + tokens] == own_ids)[:, None, None]
        tap_grads.append(
            jnp.sum(
                jnp.where(same_doc, grad_heads * rim_values[offset : offset + tokens], 0.0),
                axis=(0, 2),
            )
        )
        mirror = 2 * rim_width - offset
        back_same = (rim_ids[mirror : mirror + tokens] == own_ids)[:, None, None]
        grad_conv_values = grad_conv_values + jnp.where(
            back_same, conv_taps[None, :, offset, None] * grad_rim[mirror : mirror + tokens], 0.0
        )
    grad_taps = jnp.stack(tap_grads, axis=1)
    grad_query_unit, grad_key_unit, grad_value_att = back_block(
        query_unit, grad_rows, key_unit, values, own_same
    )
    for index_dir, direction in enumerate((1, -1)):

        def back_step(carried, sliced):
            travel, packet = sliced
            key_far, value_far, acc_key, acc_value, acc_query = carried
            key_far, value_far = from_behind((key_far, value_far), "seq", direction)
            acc_key, acc_value = (
                from_behind(acc_key.astype(jnp.bfloat16), "seq", direction).astype(acc_key.dtype),
                from_behind(acc_value.astype(jnp.bfloat16), "seq", direction).astype(
                    acc_value.dtype
                ),
            )
            anchor = (my_index - direction * travel) % cycle_size
            far_ids = doc_ids(lengths, anchor * tokens + local_rows, all_tokens)
            part_query, part_key, part_value = back_block(
                query_unit, grad_rows, key_far, value_far, own_ids[:, None] == far_ids[None, :]
            )
            return (
                (
                    key_far,
                    value_far,
                    acc_key + part_key,
                    acc_value + part_value,
                    acc_query + part_query,
                ),
                None,
            )

        zero_acc = jnp.zeros(head_shape, jnp.float32)
        (unused_key, unused_value, acc_key, acc_value, grad_query_unit), unused_ys = lax.scan(
            back_step,
            (key_unit, values, zero_acc, zero_acc, grad_query_unit),
            (jnp.arange(1, far_reach + 1, dtype=jnp.int32), stored[index_dir]),
        )
        home_key, home_value = (
            from_behind(acc_key.astype(jnp.bfloat16), "seq", -direction * far_reach).astype(
                acc_key.dtype
            ),
            from_behind(acc_value.astype(jnp.bfloat16), "seq", -direction * far_reach).astype(
                acc_value.dtype
            ),
        )
        grad_key_unit = grad_key_unit + home_key
        grad_value_att = grad_value_att + home_value
    unused_query, query_back = jax.vjp(unit_rows, queries)
    unused_keys, key_back = jax.vjp(unit_rows, keys_raw)
    grad_queries = query_back(grad_query_unit)[0].reshape(tokens, -1).astype(jnp.bfloat16)
    grad_keys = key_back(grad_key_unit)[0].reshape(tokens, -1).astype(jnp.bfloat16)
    grad_values = (grad_value_att + grad_conv_values).reshape(tokens, -1).astype(jnp.bfloat16)
    grad_query = inner_sum(inputs, grad_queries)
    grad_key = inner_sum(inputs, grad_keys)
    grad_value = inner_sum(inputs, grad_values)
    partial_inputs = (
        back_dot(grad_queries, query_weight)
        + back_dot(grad_keys, key_weight)
        + back_dot(grad_values, value_weight)
    )
    grad_inputs = grad_residual + lax.psum(partial_inputs.astype(jnp.bfloat16), "tp").astype(
        jnp.float32
    )
    summed = lax.psum(
        (
            grad_query,
            grad_key,
            grad_value,
            grad_out,
            grad_up,
            grad_down,
            grad_taps,
            grad_attn_gain,
            grad_attn_shift,
            grad_ffn_gain,
            grad_ffn_shift,
            occ_local,
        ),
        "seq",
    )
    return (
        output,
        grad_inputs,
        summed[0],
        summed[1],
        summed[2],
        summed[3],
        summed[4],
        summed[5],
        summed[6],
        summed[7],
        summed[8],
        summed[9],
        summed[10],
        summed[11],
    )


def solution(mesh):
    return jax.shard_map(
        body,
        mesh=mesh,
        in_specs=(
            P("seq", None),
            P("seq", None),
            P(None, "tp"),
            P(None, "tp"),
            P(None, "tp"),
            P("tp", None),
            P(None, "tp"),
            P("tp", None),
            P("tp", None),
            P(),
            P(),
            P(),
            P(),
            P(),
            P(),
        ),
        out_specs=(
            P("seq", None),
            P("seq", None),
            P(None, "tp"),
            P(None, "tp"),
            P(None, "tp"),
            P("tp", None),
            P(None, "tp"),
            P("tp", None),
            P("tp", None),
            P(),
            P(),
            P(),
            P(),
            P("tp", None, None),
        ),
        check_vma=False,
    )
```

profile of v0, /device:TPU:0, one launch (start us, length us, event | category | flops | bytes accessed | tf_op | source)
XLA Modules:
  0.0 3771.4 jit_solution(6675032514788774099)
XLA Ops:
  36.2 67.0 %conditional.6 = (f32[1024,6,64]{0,2,1:T(8,128)}) conditional(s32[]{:T(128)} %convert_element_type.803, () %tuple.98, (pred[1024,1024]{1,0:T(8,128)(4,1)}, bf16[1024,6,64]{0,2,1:T(8,128)(2,1)S(1)}, bf16[1024,6,64]{0,2,1:T(8,128)(2,1)}, bf16[1024,6,64]{0,2,1:T(8,128)(2,1)}) %tuple.419), branch_computations={%region_5.6_spmd, %region_6.7_spmd} | conditional | flops 1679818752 | bytes 4980744 | solution.py:116
  36.2 66.7 %fusion.11 = f32[1024,6,64]{0,2,1:T(8,128)} fusion(bf16[1024,6,64]{0,2,1:T(8,128)(2,1)} %get-tuple-element.602, pred[1024,1024]{1,0:T(8,128)(4,1)} %get-tuple-element.599, bf16[1024,6,64]{0,2,1:T(8,128)(2,1)S(1)} %get-tuple-element.600, bf16[1024,6,64]{0,2,1:T(8,128)(2,1)} %get-tuple-element.601), kind=kOutput, calls=%fused_computation.7 | convolution fusion | flops 1679818752 | bytes 4980736 | tf_op jit(solution)/shard_map/cond/branch_1_fun/hqk,khd->qhd/dot_general | solution.py:111
  103.2 376.0 %while.76 = (s32[]{:T(128)}, bf16[1024,6,64]{0,2,1:T(8,128)(2,1)}, bf16[1024,6,64]{0,2,1:T(8,128)(2,1)}, f32[1024,6,64]{0,2,1:T(8,128)}, s32[1024]{0:T(1024)S(1)...) while((s32[]{:T(128)}, bf16[1024,6,64]{0,2,1:T(8,128)(2,1)}, ...), condition=%wide.region_12.13_spmd.clone, body=%wide.region_7.12_spmd.clone.sunk | while | flops 1682412544 | bytes 20214300 | solution.py:210
  112.5 16.2 collective-permute-done.1
  128.7 15.4 collective-permute-done
  153.0 63.1 %collective-permute-start.1 = (bf16[1024,6,64]{0,2,1:T(8,128)(2,1)}, bf16[1024,6,64]{0,2,1:T(8,128)(2,1)}, u32[]{:S(2)}, u32[]{:S(2)}) collective-permute-start(bf16[1024,6,64]{0,2,1:T(8,128)(2,1)} %get-tuple-element.1594), channel_id=1, source_target_pairs={{30,0},{0,2},{2,4},{4,6},{6,8},{8,10},{10,12},{12,14},{14,16},{16,... | collective-permute-start | bytes 2359304 | tf_op jit(solution)/shard_map/while/body/eval_jaxpr/ppermute | solution.py:24
  223.5 15.3 collective-permute-done.1
  238.8 14.4 collective-permute-done
  268.3 79.8 %collective-permute-done.1 = bf16[1024,6,64]{0,2,1:T(8,128)(2,1)} collective-permute-done((bf16[1024,6,64]{0,2,1:T(8,128)(2,1)}, bf16[1024,6,64]{0,2,1:T(8,128)(2,1)}, u32[]{:S(2)}, u32[]{:S(2)}) %collective-permute-start.1) | collective-permute-done | bytes 786464 | tf_op jit(solution)/shard_map/while/body/eval_jaxpr/ppermute | solution.py:24
  348.1 13.7 collective-permute-done
  375.4 82.0 %collective-permute-done.1 = bf16[1024,6,64]{0,2,1:T(8,128)(2,1)} collective-permute-done((bf16[1024,6,64]{0,2,1:T(8,128)(2,1)}, bf16[1024,6,64]{0,2,1:T(8,128)(2,1)}, u32[]{:S(2)}, u32[]{:S(2)}) %collective-permute-start.1) | collective-permute-done | bytes 786464 | tf_op jit(solution)/shard_map/while/body/eval_jaxpr/ppermute | solution.py:24
  479.3 339.7 %while.77 = (s32[]{:T(128)}, bf16[1024,6,64]{0,2,1:T(8,128)(2,1)}, bf16[1024,6,64]{0,2,1:T(8,128)(2,1)}, f32[1024,6,64]{0,2,1:T(8,128)}, s32[1024]{0:T(1024)S(1)...) while((s32[]{:T(128)}, bf16[1024,6,64]{0,2,1:T(8,128)(2,1)}, ...), condition=%wide.region_18.19_spmd.clone, body=%wide.region_13.18_spmd.clone.sunk | while | flops 1682412544 | bytes 20214320 | solution.py:210
  479.3 67.6 %collective-permute-start.3 = (bf16[1024,6,64]{0,2,1:T(8,128)(2,1)}, bf16[1024,6,64]{0,2,1:T(8,128)(2,1)}, u32[]{:S(2)}, u32[]{:S(2)}) collective-permute-start(bf16[1024,6,64]{0,2,1:T(8,128)(2,1)} %get-tuple-element.1637), channel_id=1, source_target_pairs={{2,0},{4,2},{6,4},{8,6},{10,8},{12,10},{14,12},{16,14},{18,16},{20... | collective-permute-start | bytes 2359304 | tf_op jit(solution)/shard_map/while/body/eval_jaxpr/ppermute | solution.py:24
  576.9 66.7 %conditional.17 = (f32[1024,6,64]{0,2,1:T(8,128)}) conditional(s32[]{:T(128)} %convert_element_type.1505, () %tuple.369, (pred[1024,1024]{1,0:T(8,128)(4,1)}, bf16[1024,6,64]{0,2,1:T(8,128)(2,1)S(1)}, bf16[1024,6,64]{0,2,1:T(8,128)(2,1)}, bf16[1024,6,64]{0,2,1:T(8,128)(2,1)}) %tuple.370), branch_computations={%region_16.16_spmd, %region_17.17_spmd} | conditional | flops 1679818752 | bytes 4980744 | solution.py:116
  576.9 66.7 %fusion.29 = f32[1024,6,64]{0,2,1:T(8,128)} fusion(bf16[1024,6,64]{0,2,1:T(8,128)(2,1)} %get-tuple-element.621, pred[1024,1024]{1,0:T(8,128)(4,1)} %get-tuple-element.618, bf16[1024,6,64]{0,2,1:T(8,128)(2,1)S(1)} %get-tuple-element.619, bf16[1024,6,64]{0,2,1:T(8,128)(2,1)} %get-tuple-element.620), kind=kOutput, calls=%fused_computation.25 | convolution fusion | flops 1679818752 | bytes 4980736 | tf_op jit(solution)/shard_map/while/body/eval_jaxpr/cond/branch_1_fun/hqk,khd->qhd/dot_general | solution.py:111
  732.9 48.8 %collective-permute-start.3 = (bf16[1024,6,64]{0,2,1:T(8,128)(2,1)}, bf16[1024,6,64]{0,2,1:T(8,128)(2,1)}, u32[]{:S(2)}, u32[]{:S(2)}) collective-permute-start(bf16[1024,6,64]{0,2,1:T(8,128)(2,1)} %get-tuple-element.1637), channel_id=1, source_target_pairs={{2,0},{4,2},{6,4},{8,6},{10,8},{12,10},{14,12},{16,14},{18,16},{20... | collective-permute-start | bytes 2359304 | tf_op jit(solution)/shard_map/while/body/eval_jaxpr/ppermute | solution.py:24
  781.7 17.1 collective-permute-start.2
  946.6 19.9 add_convert_fusion.6
  970.4 168.4 %all-reduce.8.cloned.1.call-done = f32[1024,768]{1,0:T(8,128)} async-done(((f32[1024,768]{1,0:T(8,128)}), f32[1024,768]{1,0:T(8,128)}) %all-reduce.8.cloned.1.call-update) | async-done | bytes 3145744 | tf_op jit(solution)/shard_map/psum | solution.py:232
  1143.3 17.5 multiply_convert_fusion
  1211.3 25.2 fusion.201
  1269.1 173.6 %conditional.7 = (f32[1024,6,64]{0,2,1:T(8,128)S(1)}, f32[1024,6,64]{0,2,1:T(8,128)}, f32[1024,6,64]{0,2,1:T(8,128)}) conditional(s32[]{:T(128)} %convert_element_type.803, () %tuple.102, (pred[1024,1024]{1,0:T(8,128)(4,1)S(1)}, bf16[1024,6,64]{0,2,1:T(8,128)(2,1)S(1)}, bf16[1024,6,64]{0,2,1:T(8,128)(2,1)S(1)}, ...), branch_computations={%region_33.34_spmd, %region_34.35_spmd} | conditional | flops 4277141504 | bytes 177995840 | solution.py:154
  1281.3 56.6 %fusion.47 = f32[1024,6,64]{0,2,1:T(8,128)} fusion(bf16[1024,6,64]{0,2,1:T(8,128)(2,1)S(1)} %get-tuple-element.636, f32[6,1024,1024]{2,1,0:T(8,128)} %get-tuple-element.1138, pred[1024,1024]{1,0:T(8,128)(4,1)S(1)} %get-tuple-element.633), kind=kOutput, calls=%fused_computation.58 | convolution fusion | flops 874512384 | bytes 28573696 | tf_op jit(solution)/shard_map/cond/branch_1_fun/hqk,qhd->khd/dot_general | solution.py:143
  1338.0 65.9 %fusion.43 = bf16[6,1024,1024]{2,1,0:T(8,128)(2,1)S(1)} fusion(f32[6,1024,1024]{2,1,0:T(8,128)} %get-tuple-element.1138, pred[1024,1024]{1,0:T(8,128)(4,1)S(1)} %get-tuple-element.633, bf16[1024,6,64]{0,2,1:T(8,128)(2,1)S(1)} %get-tuple-element.636, bf16[1024,6,64]{0,2,1:T(8,128)(2,1)} %get-tuple-element.637, u8[1024,1024]{1,0:T(8,128)(4,1)S(1)} %get-tuple-element.1137), kind=kOutput, calls=%fused_computation.49 | convolution fusion | flops 950009856 | bytes 41418752 | tf_op jit(solution)/shard_map/cond/branch_1_fun/qhd,khd->hqk/dot_general | solution.py:130
  1442.8 749.7 %while.78 = (s32[]{:T(128)}, bf16[1024,6,64]{0,2,1:T(8,128)(2,1)S(1)}, bf16[1024,6,64]{0,2,1:T(8,128)(2,1)}, bf16[1024,6,64]{0,2,1:T(8,128)(2,1)}, bf16[1024,6,6...) while((s32[]{:T(128)}, ...), condition=%wide.region_40.41_spmd.clone, body=%wide.region_35.40_spmd.clone.sunk | while | flops 4282881024 | bytes 225735536 | solution.py:313
  1458.8 27.8 collective-permute-done.5
  1486.6 16.7 collective-permute-done.4
  1524.9 140.6 %collective-permute-start.6 = (bf16[1024,6,64]{0,2,1:T(8,128)(2,1)}, bf16[1024,6,64]{0,2,1:T(8,128)(2,1)}, u32[]{:S(2)}, u32[]{:S(2)}) collective-permute-start(bf16[1024,6,64]{0,2,1:T(8,128)(2,1)} %select_convert_fusion.32), channel_id=1, source_target_pairs={{30,0},{0,2},{2,4},{4,6},{6,8},{8,10},{10,12},{12,14},{14,16},{16,... | collective-permute-start | bytes 2359304 | tf_op jit(solution)/shard_map/while/body/eval_jaxpr/ppermute | solution.py:24
  1679.4 26.1 collective-permute-done.5
  1705.5 16.7 collective-permute-done.4
  1755.0 169.4 %collective-permute-done.5 = bf16[1024,6,64]{0,2,1:T(8,128)(2,1)} collective-permute-done((bf16[1024,6,64]{0,2,1:T(8,128)(2,1)}, bf16[1024,6,64]{0,2,1:T(8,128)(2,1)}, u32[]{:S(2)}, u32[]{:S(2)}) %collective-permute-start.5) | collective-permute-done | bytes 786464 | tf_op jit(solution)/shard_map/while/body/eval_jaxpr/ppermute | solution.py:24
  1924.3 16.7 collective-permute-done.4
  1964.0 180.0 %collective-permute-done.5 = bf16[1024,6,64]{0,2,1:T(8,128)(2,1)} collective-permute-done((bf16[1024,6,64]{0,2,1:T(8,128)(2,1)}, bf16[1024,6,64]{0,2,1:T(8,128)(2,1)}, u32[]{:S(2)}, u32[]{:S(2)}) %collective-permute-start.5) | collective-permute-done | bytes 786464 | tf_op jit(solution)/shard_map/while/body/eval_jaxpr/ppermute | solution.py:24
  2192.5 776.0 %while.79 = (s32[]{:T(128)}, bf16[1024,6,64]{0,2,1:T(8,128)(2,1)}, bf16[1024,6,64]{0,2,1:T(8,128)(2,1)}, bf16[1024,6,64]{0,2,1:T(8,128)(2,1)}, bf16[1024,6,64]{0...) while((s32[]{:T(128)}, bf16[1024,6,64]{0,2,1:T(8,128)(2,1)}, ...), condition=%wide.region_46.47_spmd.clone, body=%wide.region_41.46_spmd.clone.sunk | while | flops 4282881024 | bytes 219444032 | solution.py:313
  2193.6 149.7 %collective-permute-start.10 = (bf16[1024,6,64]{0,2,1:T(8,128)(2,1)}, bf16[1024,6,64]{0,2,1:T(8,128)(2,1)}, u32[]{:S(2)}, u32[]{:S(2)}) collective-permute-start(bf16[1024,6,64]{0,2,1:T(8,128)(2,1)} %select_convert_fusion.34), channel_id=1, source_target_pairs={{2,0},{4,2},{6,4},{8,6},{10,8},{12,10},{14,12},{16,14},{18,16},{20... | collective-permute-start | bytes 2359304 | tf_op jit(solution)/shard_map/while/body/eval_jaxpr/ppermute | solution.py:24
  2349.3 23.0 collective-permute-done.9
  2380.7 151.5 %conditional.19 = (f32[1024,6,64]{0,2,1:T(8,128)}, f32[1024,6,64]{0,2,1:T(8,128)}, f32[1024,6,64]{0,2,1:T(8,128)}) conditional(s32[]{:T(128)} %convert_element_type.1513, () %tuple.377, (pred[1024,1024]{1,0:T(8,128)(4,1)}, bf16[1024,6,64]{0,2,1:T(8,128)(2,1)S(1)}, bf16[1024,6,64]{0,2,1:T(8,128)(2,1)S(1)}, bf16[1024,6,64]{0,2,1:T(8,128)(2,1)}, ...), branch_computations={%region_44.44_spmd, %region_45.45_spmd} | conditional | flops 4277141504 | bytes 185335936 | solution.py:154
  2392.9 56.1 %fusion.80 = f32[1024,6,64]{0,2,1:T(8,128)} fusion(bf16[1024,6,64]{0,2,1:T(8,128)(2,1)S(1)} %copy-done.67, f32[6,1024,1024]{2,1,0:T(8,128)} %get-tuple-element.1144, pred[1024,1024]{1,0:T(8,128)(4,1)S(1)} %copy-done.28), kind=kOutput, calls=%fused_computation.117 | convolution fusion | flops 874512384 | bytes 28573696 | tf_op jit(solution)/shard_map/while/body/eval_jaxpr/cond/branch_1_fun/hqk,qhd->khd/dot_general | solution.py:143
  2449.0 65.5 %fusion.76 = bf16[6,1024,1024]{2,1,0:T(8,128)(2,1)S(1)} fusion(f32[6,1024,1024]{2,1,0:T(8,128)} %get-tuple-element.1144, pred[1024,1024]{1,0:T(8,128)(4,1)S(1)} %copy-done.28, bf16[1024,6,64]{0,2,1:T(8,128)(2,1)S(1)} %copy-done.67, bf16[1024,6,64]{0,2,1:T(8,128)(2,1)} %get-tuple-element.664, u8[1024,1024]{1,0:T(8,128)(4,1)S(1)} %get-tuple-element.1143), kind=kOutput, calls=%fused_computation.108 | convolution fusion | flops 950009856 | bytes 41418752 | tf_op jit(solution)/shard_map/while/body/eval_jaxpr/cond/branch_1_fun/qhd,khd->hqk/dot_general | solution.py:130
  2553.4 19.4 collective-permute-done.9
  2572.8 16.7 collective-permute-done.8
  2611.6 132.1 %collective-permute-start.8 = (bf16[1024,6,64]{0,2,1:T(8,128)(2,1)}, bf16[1024,6,64]{0,2,1:T(8,128)(2,1)S(1)}, u32[]{:S(2)}, u32[]{:S(2)}) collective-permute-start(bf16[1024,6,64]{0,2,1:T(8,128)(2,1)} %get-tuple-element.1741), channel_id=1, source_target_pairs={{2,0},{4,2},{6,4},{8,6},{10,8},{12,10},{14,12},{16,14},{18,16},{20... | collective-permute-start | bytes 2359304 | tf_op jit(solution)/shard_map/while/body/eval_jaxpr/ppermute | solution.py:24
  2799.9 138.1 %collective-permute-start.11 = (bf16[1024,6,64]{0,2,1:T(8,128)(2,1)}, bf16[1024,6,64]{0,2,1:T(8,128)(2,1)}, u32[]{:S(2)}, u32[]{:S(2)}) collective-permute-start(bf16[1024,6,64]{0,2,1:T(8,128)(2,1)} %select_convert_fusion.35), channel_id=1, source_target_pairs={{2,0},{4,2},{6,4},{8,6},{10,8},{12,10},{14,12},{16,14},{18,16},{20... | collective-permute-start | bytes 2359304 | tf_op jit(solution)/shard_map/while/body/eval_jaxpr/ppermute | solution.py:24
  2972.1 25.5 collective-permute-start.14
  3001.3 142.1 %collective-permute-start.16 = (bf16[1024,6,64]{0,2,1:T(8,128)(2,1)S(1)}, bf16[1024,6,64]{0,2,1:T(8,128)(2,1)}, u32[]{:S(2)}, u32[]{:S(2)}) collective-permute-start(bf16[1024,6,64]{0,2,1:T(8,128)(2,1)S(1)} %copy-done.35), channel_id=1, source_target_pairs={{8,0},{10,2},{12,4},{14,6},{16,8},{18,10},{20,12},{22,14},{24,16},... | collective-permute-start | bytes 2359304 | tf_op jit(solution)/shard_map/ppermute | solution.py:24
  3272.4 19.0 add_convert_fusion.5
  3341.5 82.6 %all-reduce = (f32[6,33]{1,0:T(8,128)}, f32[768]{0:T(1024)}, f32[768]{0:T(1024)}, f32[768]{0:T(1024)}, f32[768]{0:T(1024)}) all-reduce(f32[6,33]{1,0:T(8,128)S(1)} %stack.135, f32[768]{0:T(1024)S(1)} %copy-done.134, f32[768]{0:T(1024)S(1)} %copy-done.135, f32[768]{0:T(1024)S(1)} %copy-done.132, ...), channel_id=1, replica_groups=mesh['seq'=16,'tp'=2] {'seq'}, use_global_device_ids=true, to_apply=%region_122.123 | all-reduce | flops 3270 | bytes 26160 | tf_op jit(solution)/shard_map/psum | solution.py:344
  3428.6 319.7 %all-reduce.16.cloned.1.call-done = (f32[768,384]{0,1:T(8,128)}, f32[768,384]{0,1:T(8,128)}, f32[768,384]{0,1:T(8,128)}, f32[384,768]{1,0:T(8,128)}, f32[768,153...) async-done(((f32[768,384]{0,1:T(8,128)}, f32[768,384]{0,1:T(8,128)}, f32[768,384]{0,1:T(8,128)}, f32[384,768]{1,0:T(8,128)}, f32[768,1536]{1,0:T(8,128)}, ...) | async-done | bytes 14352400 | tf_op jit(solution)/shard_map/psum | solution.py:344
  (982 shorter events, 1011.3 us)
Async XLA Ops:
  7.2 1131.6 %all-reduce.8.cloned.1.call-start = ((), (), s32[]{:S(2)}) async-start(), calls=%async_computation | async-start | bytes 6291456 | tf_op jit(solution)/shard_map/psum | solution.py:232
  10.6 827.6 %collective-permute-start.12 = (bf16[16,384]{1,0:T(8,128)(2,1)}, bf16[16,384]{1,0:T(8,128)(2,1)}, u32[]{:S(2)}, u32[]{:S(2)}) collective-permute-start(bf16[16,384]{1,0:T(8,128)(2,1)} %get-tuple-element.1230), channel_id=1, source_target_pairs={{0,2},{2,4},{4,6},{6,8},{8,10},{10,12},{12,14},{14,16},{16,18},{18... | collective-permute-start | bytes 36872 | tf_op jit(solution)/shard_map/ppermute | solution.py:32
  16.0 806.3 %collective-permute-start.13 = (bf16[16,384]{1,0:T(8,128)(2,1)}, bf16[16,384]{1,0:T(8,128)(2,1)}, u32[]{:S(2)}, u32[]{:S(2)}) collective-permute-start(bf16[16,384]{1,0:T(8,128)(2,1)} %get-tuple-element.1231), channel_id=1, source_target_pairs={{2,0},{4,2},{6,4},{8,6},{10,8},{12,10},{14,12},{16,14},{18,16},{20... | collective-permute-start | bytes 36872 | tf_op jit(solution)/shard_map/ppermute | solution.py:35
  105.9 38.1 %collective-permute-start = (bf16[1024,6,64]{0,2,1:T(8,128)(2,1)}, bf16[1024,6,64]{0,2,1:T(8,128)(2,1)}, u32[]{:S(2)}, u32[]{:S(2)}) collective-permute-start(bf16[1024,6,64]{0,2,1:T(8,128)(2,1)} %get-tuple-element.1593), channel_id=1, source_target_pairs={{30,0},{0,2},{2,4},{4,6},{6,8},{8,10},{10,12},{12,14},{14,16},{16,... | collective-permute-start | bytes 2359304 | tf_op jit(solution)/shard_map/while/body/eval_jaxpr/ppermute | solution.py:24
  153.0 85.9 %collective-permute-start.1 = (bf16[1024,6,64]{0,2,1:T(8,128)(2,1)}, bf16[1024,6,64]{0,2,1:T(8,128)(2,1)}, u32[]{:S(2)}, u32[]{:S(2)}) collective-permute-start(bf16[1024,6,64]{0,2,1:T(8,128)(2,1)} %get-tuple-element.1594), channel_id=1, source_target_pairs={{30,0},{0,2},{2,4},{4,6},{6,8},{8,10},{10,12},{12,14},{14,16},{16,... | collective-permute-start | bytes 2359304 | tf_op jit(solution)/shard_map/while/body/eval_jaxpr/ppermute | solution.py:24
  262.2 85.9 %collective-permute-start.1 = (bf16[1024,6,64]{0,2,1:T(8,128)(2,1)}, bf16[1024,6,64]{0,2,1:T(8,128)(2,1)}, u32[]{:S(2)}, u32[]{:S(2)}) collective-permute-start(bf16[1024,6,64]{0,2,1:T(8,128)(2,1)} %get-tuple-element.1594), channel_id=1, source_target_pairs={{30,0},{0,2},{2,4},{4,6},{6,8},{8,10},{10,12},{12,14},{14,16},{16,... | collective-permute-start | bytes 2359304 | tf_op jit(solution)/shard_map/while/body/eval_jaxpr/ppermute | solution.py:24
  262.2 99.6 %collective-permute-start = (bf16[1024,6,64]{0,2,1:T(8,128)(2,1)}, bf16[1024,6,64]{0,2,1:T(8,128)(2,1)}, u32[]{:S(2)}, u32[]{:S(2)}) collective-permute-start(bf16[1024,6,64]{0,2,1:T(8,128)(2,1)} %get-tuple-element.1593), channel_id=1, source_target_pairs={{30,0},{0,2},{2,4},{4,6},{6,8},{8,10},{10,12},{12,14},{14,16},{16,... | collective-permute-start | bytes 2359304 | tf_op jit(solution)/shard_map/while/body/eval_jaxpr/ppermute | solution.py:24
  370.7 86.7 %collective-permute-start.1 = (bf16[1024,6,64]{0,2,1:T(8,128)(2,1)}, bf16[1024,6,64]{0,2,1:T(8,128)(2,1)}, u32[]{:S(2)}, u32[]{:S(2)}) collective-permute-start(bf16[1024,6,64]{0,2,1:T(8,128)(2,1)} %get-tuple-element.1594), channel_id=1, source_target_pairs={{30,0},{0,2},{2,4},{4,6},{6,8},{8,10},{10,12},{12,14},{14,16},{16,... | collective-permute-start | bytes 2359304 | tf_op jit(solution)/shard_map/while/body/eval_jaxpr/ppermute | solution.py:24
  370.7 99.6 %collective-permute-start = (bf16[1024,6,64]{0,2,1:T(8,128)(2,1)}, bf16[1024,6,64]{0,2,1:T(8,128)(2,1)}, u32[]{:S(2)}, u32[]{:S(2)}) collective-permute-start(bf16[1024,6,64]{0,2,1:T(8,128)(2,1)} %get-tuple-element.1593), channel_id=1, source_target_pairs={{30,0},{0,2},{2,4},{4,6},{6,8},{8,10},{10,12},{12,14},{14,16},{16,... | collective-permute-start | bytes 2359304 | tf_op jit(solution)/shard_map/while/body/eval_jaxpr/ppermute | solution.py:24
  479.3 85.9 %collective-permute-start.3 = (bf16[1024,6,64]{0,2,1:T(8,128)(2,1)}, bf16[1024,6,64]{0,2,1:T(8,128)(2,1)}, u32[]{:S(2)}, u32[]{:S(2)}) collective-permute-start(bf16[1024,6,64]{0,2,1:T(8,128)(2,1)} %get-tuple-element.1637), channel_id=1, source_target_pairs={{2,0},{4,2},{6,4},{8,6},{10,8},{12,10},{14,12},{16,14},{18,16},{20... | collective-permute-start | bytes 2359304 | tf_op jit(solution)/shard_map/while/body/eval_jaxpr/ppermute | solution.py:24
  732.9 70.7 %collective-permute-start.3 = (bf16[1024,6,64]{0,2,1:T(8,128)(2,1)}, bf16[1024,6,64]{0,2,1:T(8,128)(2,1)}, u32[]{:S(2)}, u32[]{:S(2)}) collective-permute-start(bf16[1024,6,64]{0,2,1:T(8,128)(2,1)} %get-tuple-element.1637), channel_id=1, source_target_pairs={{2,0},{4,2},{6,4},{8,6},{10,8},{12,10},{14,12},{16,14},{18,16},{20... | collective-permute-start | bytes 2359304 | tf_op jit(solution)/shard_map/while/body/eval_jaxpr/ppermute | solution.py:24
  970.1 217.8 %all-reduce.10.cloned.1.call-start = ((), (), s32[]{:S(2)}) async-start(), calls=%async_computation.1 | async-start | bytes 3145728 | tf_op jit(solution)/shard_map/psum | solution.py:239
  1166.2 82.9 %all-reduce.12.cloned.1.call-start = ((), (), s32[]{:S(2)}) async-start(), calls=%async_computation.2 | async-start | bytes 3145728 | tf_op jit(solution)/shard_map/psum | solution.py:251
  1210.2 2213.9 %all-reduce.14.cloned.1.call-start = ((), (), s32[]{:S(2)}) async-start(), calls=%async_computation.3 | async-start | bytes 3145728 | tf_op jit(solution)/shard_map/psum | solution.py:341
  1263.3 1890.2 %collective-permute-start.18 = (bf16[16,384]{1,0:T(8,128)(2,1)}, bf16[16,384]{1,0:T(8,128)(2,1)}, u32[]{:S(2)}, u32[]{:S(2)}) collective-permute-start(bf16[16,384]{1,0:T(8,128)(2,1)} %get-tuple-element.1228), channel_id=1, source_target_pairs={{2,0},{4,2},{6,4},{8,6},{10,8},{12,10},{14,12},{16,14},{18,16},{20... | collective-permute-start | bytes 36872 | tf_op jit(solution)/shard_map/ppermute | solution.py:35
  1443.9 68.4 %collective-permute-start.6 = (bf16[1024,6,64]{0,2,1:T(8,128)(2,1)}, bf16[1024,6,64]{0,2,1:T(8,128)(2,1)}, u32[]{:S(2)}, u32[]{:S(2)}) collective-permute-start(bf16[1024,6,64]{0,2,1:T(8,128)(2,1)} %select_convert_fusion.32), channel_id=1, source_target_pairs={{30,0},{0,2},{2,4},{4,6},{6,8},{8,10},{10,12},{12,14},{14,16},{16,... | collective-permute-start | bytes 2359304 | tf_op jit(solution)/shard_map/while/body/eval_jaxpr/ppermute | solution.py:24
  1446.5 40.0 %collective-permute-start.5 = (bf16[1024,6,64]{0,2,1:T(8,128)(2,1)}, bf16[1024,6,64]{0,2,1:T(8,128)(2,1)}, u32[]{:S(2)}, u32[]{:S(2)}) collective-permute-start(bf16[1024,6,64]{0,2,1:T(8,128)(2,1)} %get-tuple-element.1690), channel_id=1, source_target_pairs={{30,0},{0,2},{2,4},{4,6},{6,8},{8,10},{10,12},{12,14},{14,16},{16,... | collective-permute-start | bytes 2359304 | tf_op jit(solution)/shard_map/while/body/eval_jaxpr/ppermute | solution.py:24
  1449.1 54.1 %collective-permute-start.4 = (bf16[1024,6,64]{0,2,1:T(8,128)(2,1)}, bf16[1024,6,64]{0,2,1:T(8,128)(2,1)S(1)}, u32[]{:S(2)}, u32[]{:S(2)}) collective-permute-start(bf16[1024,6,64]{0,2,1:T(8,128)(2,1)} %copy-done.23), channel_id=1, source_target_pairs={{30,0},{0,2},{2,4},{4,6},{6,8},{8,10},{10,12},{12,14},{14,16},{16,... | collective-permute-start | bytes 2359304 | tf_op jit(solution)/shard_map/while/body/eval_jaxpr/ppermute | solution.py:24
  1450.8 68.8 %collective-permute-start.7 = (bf16[1024,6,64]{0,2,1:T(8,128)(2,1)}, bf16[1024,6,64]{0,2,1:T(8,128)(2,1)}, u32[]{:S(2)}, u32[]{:S(2)}) collective-permute-start(bf16[1024,6,64]{0,2,1:T(8,128)(2,1)} %select_convert_fusion.33), channel_id=1, source_target_pairs={{30,0},{0,2},{2,4},{4,6},{6,8},{8,10},{10,12},{12,14},{14,16},{16,... | collective-permute-start | bytes 2359304 | tf_op jit(solution)/shard_map/while/body/eval_jaxpr/ppermute | solution.py:24
  1524.9 206.2 %collective-permute-start.6 = (bf16[1024,6,64]{0,2,1:T(8,128)(2,1)}, bf16[1024,6,64]{0,2,1:T(8,128)(2,1)}, u32[]{:S(2)}, u32[]{:S(2)}) collective-permute-start(bf16[1024,6,64]{0,2,1:T(8,128)(2,1)} %select_convert_fusion.32), channel_id=1, source_target_pairs={{30,0},{0,2},{2,4},{4,6},{6,8},{8,10},{10,12},{12,14},{14,16},{16,... | collective-permute-start | bytes 2359304 | tf_op jit(solution)/shard_map/while/body/eval_jaxpr/ppermute | solution.py:24
  1665.6 39.9 %collective-permute-start.5 = (bf16[1024,6,64]{0,2,1:T(8,128)(2,1)}, bf16[1024,6,64]{0,2,1:T(8,128)(2,1)}, u32[]{:S(2)}, u32[]{:S(2)}) collective-permute-start(bf16[1024,6,64]{0,2,1:T(8,128)(2,1)} %get-tuple-element.1690), channel_id=1, source_target_pairs={{30,0},{0,2},{2,4},{4,6},{6,8},{8,10},{10,12},{12,14},{14,16},{16,... | collective-permute-start | bytes 2359304 | tf_op jit(solution)/shard_map/while/body/eval_jaxpr/ppermute | solution.py:24
  1668.8 53.4 %collective-permute-start.4 = (bf16[1024,6,64]{0,2,1:T(8,128)(2,1)}, bf16[1024,6,64]{0,2,1:T(8,128)(2,1)S(1)}, u32[]{:S(2)}, u32[]{:S(2)}) collective-permute-start(bf16[1024,6,64]{0,2,1:T(8,128)(2,1)} %copy-done.23), channel_id=1, source_target_pairs={{30,0},{0,2},{2,4},{4,6},{6,8},{8,10},{10,12},{12,14},{14,16},{16,... | collective-permute-start | bytes 2359304 | tf_op jit(solution)/shard_map/while/body/eval_jaxpr/ppermute | solution.py:24
  1670.5 66.1 %collective-permute-start.7 = (bf16[1024,6,64]{0,2,1:T(8,128)(2,1)}, bf16[1024,6,64]{0,2,1:T(8,128)(2,1)}, u32[]{:S(2)}, u32[]{:S(2)}) collective-permute-start(bf16[1024,6,64]{0,2,1:T(8,128)(2,1)} %select_convert_fusion.33), channel_id=1, source_target_pairs={{30,0},{0,2},{2,4},{4,6},{6,8},{8,10},{10,12},{12,14},{14,16},{16,... | collective-permute-start | bytes 2359304 | tf_op jit(solution)/shard_map/while/body/eval_jaxpr/ppermute | solution.py:24
  1741.9 208.1 %collective-permute-start.6 = (bf16[1024,6,64]{0,2,1:T(8,128)(2,1)}, bf16[1024,6,64]{0,2,1:T(8,128)(2,1)}, u32[]{:S(2)}, u32[]{:S(2)}) collective-permute-start(bf16[1024,6,64]{0,2,1:T(8,128)(2,1)} %select_convert_fusion.32), channel_id=1, source_target_pairs={{30,0},{0,2},{2,4},{4,6},{6,8},{8,10},{10,12},{12,14},{14,16},{16,... | collective-permute-start | bytes 2359304 | tf_op jit(solution)/shard_map/while/body/eval_jaxpr/ppermute | solution.py:24
  1741.9 182.4 %collective-permute-start.5 = (bf16[1024,6,64]{0,2,1:T(8,128)(2,1)}, bf16[1024,6,64]{0,2,1:T(8,128)(2,1)}, u32[]{:S(2)}, u32[]{:S(2)}) collective-permute-start(bf16[1024,6,64]{0,2,1:T(8,128)(2,1)} %get-tuple-element.1690), channel_id=1, source_target_pairs={{30,0},{0,2},{2,4},{4,6},{6,8},{8,10},{10,12},{12,14},{14,16},{16,... | collective-permute-start | bytes 2359304 | tf_op jit(solution)/shard_map/while/body/eval_jaxpr/ppermute | solution.py:24
  1743.6 197.5 %collective-permute-start.4 = (bf16[1024,6,64]{0,2,1:T(8,128)(2,1)}, bf16[1024,6,64]{0,2,1:T(8,128)(2,1)S(1)}, u32[]{:S(2)}, u32[]{:S(2)}) collective-permute-start(bf16[1024,6,64]{0,2,1:T(8,128)(2,1)} %copy-done.23), channel_id=1, source_target_pairs={{30,0},{0,2},{2,4},{4,6},{6,8},{8,10},{10,12},{12,14},{14,16},{16,... | collective-permute-start | bytes 2359304 | tf_op jit(solution)/shard_map/while/body/eval_jaxpr/ppermute | solution.py:24
  1746.0 206.8 %collective-permute-start.7 = (bf16[1024,6,64]{0,2,1:T(8,128)(2,1)}, bf16[1024,6,64]{0,2,1:T(8,128)(2,1)}, u32[]{:S(2)}, u32[]{:S(2)}) collective-permute-start(bf16[1024,6,64]{0,2,1:T(8,128)(2,1)} %select_convert_fusion.33), channel_id=1, source_target_pairs={{30,0},{0,2},{2,4},{4,6},{6,8},{8,10},{10,12},{12,14},{14,16},{16,... | collective-permute-start | bytes 2359304 | tf_op jit(solution)/shard_map/while/body/eval_jaxpr/ppermute | solution.py:24
  1958.1 206.7 %collective-permute-start.6 = (bf16[1024,6,64]{0,2,1:T(8,128)(2,1)}, bf16[1024,6,64]{0,2,1:T(8,128)(2,1)}, u32[]{:S(2)}, u32[]{:S(2)}) collective-permute-start(bf16[1024,6,64]{0,2,1:T(8,128)(2,1)} %select_convert_fusion.32), channel_id=1, source_target_pairs={{30,0},{0,2},{2,4},{4,6},{6,8},{8,10},{10,12},{12,14},{14,16},{16,... | collective-permute-start | bytes 2359304 | tf_op jit(solution)/shard_map/while/body/eval_jaxpr/ppermute | solution.py:24
  1958.1 185.8 %collective-permute-start.5 = (bf16[1024,6,64]{0,2,1:T(8,128)(2,1)}, bf16[1024,6,64]{0,2,1:T(8,128)(2,1)}, u32[]{:S(2)}, u32[]{:S(2)}) collective-permute-start(bf16[1024,6,64]{0,2,1:T(8,128)(2,1)} %get-tuple-element.1690), channel_id=1, source_target_pairs={{30,0},{0,2},{2,4},{4,6},{6,8},{8,10},{10,12},{12,14},{14,16},{16,... | collective-permute-start | bytes 2359304 | tf_op jit(solution)/shard_map/while/body/eval_jaxpr/ppermute | solution.py:24
  1958.1 197.8 %collective-permute-start.4 = (bf16[1024,6,64]{0,2,1:T(8,128)(2,1)}, bf16[1024,6,64]{0,2,1:T(8,128)(2,1)S(1)}, u32[]{:S(2)}, u32[]{:S(2)}) collective-permute-start(bf16[1024,6,64]{0,2,1:T(8,128)(2,1)} %copy-done.23), channel_id=1, source_target_pairs={{30,0},{0,2},{2,4},{4,6},{6,8},{8,10},{10,12},{12,14},{14,16},{16,... | collective-permute-start | bytes 2359304 | tf_op jit(solution)/shard_map/while/body/eval_jaxpr/ppermute | solution.py:24
  1959.3 208.3 %collective-permute-start.7 = (bf16[1024,6,64]{0,2,1:T(8,128)(2,1)}, bf16[1024,6,64]{0,2,1:T(8,128)(2,1)}, u32[]{:S(2)}, u32[]{:S(2)}) collective-permute-start(bf16[1024,6,64]{0,2,1:T(8,128)(2,1)} %select_convert_fusion.33), channel_id=1, source_target_pairs={{30,0},{0,2},{2,4},{4,6},{6,8},{8,10},{10,12},{12,14},{14,16},{16,... | collective-permute-start | bytes 2359304 | tf_op jit(solution)/shard_map/while/body/eval_jaxpr/ppermute | solution.py:24
  2193.6 343.5 %collective-permute-start.10 = (bf16[1024,6,64]{0,2,1:T(8,128)(2,1)}, bf16[1024,6,64]{0,2,1:T(8,128)(2,1)}, u32[]{:S(2)}, u32[]{:S(2)}) collective-permute-start(bf16[1024,6,64]{0,2,1:T(8,128)(2,1)} %select_convert_fusion.34), channel_id=1, source_target_pairs={{2,0},{4,2},{6,4},{8,6},{10,8},{12,10},{14,12},{16,14},{18,16},{20... | collective-permute-start | bytes 2359304 | tf_op jit(solution)/shard_map/while/body/eval_jaxpr/ppermute | solution.py:24
  2344.5 195.3 %collective-permute-start.11 = (bf16[1024,6,64]{0,2,1:T(8,128)(2,1)}, bf16[1024,6,64]{0,2,1:T(8,128)(2,1)}, u32[]{:S(2)}, u32[]{:S(2)}) collective-permute-start(bf16[1024,6,64]{0,2,1:T(8,128)(2,1)} %select_convert_fusion.35), channel_id=1, source_target_pairs={{2,0},{4,2},{6,4},{8,6},{10,8},{12,10},{14,12},{16,14},{18,16},{20... | collective-permute-start | bytes 2359304 | tf_op jit(solution)/shard_map/while/body/eval_jaxpr/ppermute | solution.py:24
  2544.9 53.6 %collective-permute-start.10 = (bf16[1024,6,64]{0,2,1:T(8,128)(2,1)}, bf16[1024,6,64]{0,2,1:T(8,128)(2,1)}, u32[]{:S(2)}, u32[]{:S(2)}) collective-permute-start(bf16[1024,6,64]{0,2,1:T(8,128)(2,1)} %select_convert_fusion.34), channel_id=1, source_target_pairs={{2,0},{4,2},{6,4},{8,6},{10,8},{12,10},{14,12},{16,14},{18,16},{20... | collective-permute-start | bytes 2359304 | tf_op jit(solution)/shard_map/while/body/eval_jaxpr/ppermute | solution.py:24
  2547.6 42.0 %collective-permute-start.8 = (bf16[1024,6,64]{0,2,1:T(8,128)(2,1)}, bf16[1024,6,64]{0,2,1:T(8,128)(2,1)S(1)}, u32[]{:S(2)}, u32[]{:S(2)}) collective-permute-start(bf16[1024,6,64]{0,2,1:T(8,128)(2,1)} %get-tuple-element.1741), channel_id=1, source_target_pairs={{2,0},{4,2},{6,4},{8,6},{10,8},{12,10},{14,12},{16,14},{18,16},{20... | collective-permute-start | bytes 2359304 | tf_op jit(solution)/shard_map/while/body/eval_jaxpr/ppermute | solution.py:24
  2548.7 57.8 %collective-permute-start.11 = (bf16[1024,6,64]{0,2,1:T(8,128)(2,1)}, bf16[1024,6,64]{0,2,1:T(8,128)(2,1)}, u32[]{:S(2)}, u32[]{:S(2)}) collective-permute-start(bf16[1024,6,64]{0,2,1:T(8,128)(2,1)} %select_convert_fusion.35), channel_id=1, source_target_pairs={{2,0},{4,2},{6,4},{8,6},{10,8},{12,10},{14,12},{16,14},{18,16},{20... | collective-permute-start | bytes 2359304 | tf_op jit(solution)/shard_map/while/body/eval_jaxpr/ppermute | solution.py:24
  2611.6 159.3 %collective-permute-start.10 = (bf16[1024,6,64]{0,2,1:T(8,128)(2,1)}, bf16[1024,6,64]{0,2,1:T(8,128)(2,1)}, u32[]{:S(2)}, u32[]{:S(2)}) collective-permute-start(bf16[1024,6,64]{0,2,1:T(8,128)(2,1)} %select_convert_fusion.34), channel_id=1, source_target_pairs={{2,0},{4,2},{6,4},{8,6},{10,8},{12,10},{14,12},{16,14},{18,16},{20... | collective-permute-start | bytes 2359304 | tf_op jit(solution)/shard_map/while/body/eval_jaxpr/ppermute | solution.py:24
  2611.6 138.0 %collective-permute-start.9 = (bf16[1024,6,64]{0,2,1:T(8,128)(2,1)}, bf16[1024,6,64]{0,2,1:T(8,128)(2,1)}, u32[]{:S(2)}, u32[]{:S(2)}) collective-permute-start(bf16[1024,6,64]{0,2,1:T(8,128)(2,1)} %get-tuple-element.1742), channel_id=1, source_target_pairs={{2,0},{4,2},{6,4},{8,6},{10,8},{12,10},{14,12},{16,14},{18,16},{20... | collective-permute-start | bytes 2359304 | tf_op jit(solution)/shard_map/while/body/eval_jaxpr/ppermute | solution.py:24
  2611.6 150.3 %collective-permute-start.8 = (bf16[1024,6,64]{0,2,1:T(8,128)(2,1)}, bf16[1024,6,64]{0,2,1:T(8,128)(2,1)S(1)}, u32[]{:S(2)}, u32[]{:S(2)}) collective-permute-start(bf16[1024,6,64]{0,2,1:T(8,128)(2,1)} %get-tuple-element.1741), channel_id=1, source_target_pairs={{2,0},{4,2},{6,4},{8,6},{10,8},{12,10},{14,12},{16,14},{18,16},{20... | collective-permute-start | bytes 2359304 | tf_op jit(solution)/shard_map/while/body/eval_jaxpr/ppermute | solution.py:24
  2783.9 167.9 %collective-permute-start.10 = (bf16[1024,6,64]{0,2,1:T(8,128)(2,1)}, bf16[1024,6,64]{0,2,1:T(8,128)(2,1)}, u32[]{:S(2)}, u32[]{:S(2)}) collective-permute-start(bf16[1024,6,64]{0,2,1:T(8,128)(2,1)} %select_convert_fusion.34), channel_id=1, source_target_pairs={{2,0},{4,2},{6,4},{8,6},{10,8},{12,10},{14,12},{16,14},{18,16},{20... | collective-permute-start | bytes 2359304 | tf_op jit(solution)/shard_map/while/body/eval_jaxpr/ppermute | solution.py:24
  2792.3 150.5 %collective-permute-start.9 = (bf16[1024,6,64]{0,2,1:T(8,128)(2,1)}, bf16[1024,6,64]{0,2,1:T(8,128)(2,1)}, u32[]{:S(2)}, u32[]{:S(2)}) collective-permute-start(bf16[1024,6,64]{0,2,1:T(8,128)(2,1)} %get-tuple-element.1742), channel_id=1, source_target_pairs={{2,0},{4,2},{6,4},{8,6},{10,8},{12,10},{14,12},{16,14},{18,16},{20... | collective-permute-start | bytes 2359304 | tf_op jit(solution)/shard_map/while/body/eval_jaxpr/ppermute | solution.py:24
  2795.6 147.2 %collective-permute-start.8 = (bf16[1024,6,64]{0,2,1:T(8,128)(2,1)}, bf16[1024,6,64]{0,2,1:T(8,128)(2,1)S(1)}, u32[]{:S(2)}, u32[]{:S(2)}) collective-permute-start(bf16[1024,6,64]{0,2,1:T(8,128)(2,1)} %get-tuple-element.1741), channel_id=1, source_target_pairs={{2,0},{4,2},{6,4},{8,6},{10,8},{12,10},{14,12},{16,14},{18,16},{20... | collective-permute-start | bytes 2359304 | tf_op jit(solution)/shard_map/while/body/eval_jaxpr/ppermute | solution.py:24
  2799.9 156.4 %collective-permute-start.11 = (bf16[1024,6,64]{0,2,1:T(8,128)(2,1)}, bf16[1024,6,64]{0,2,1:T(8,128)(2,1)}, u32[]{:S(2)}, u32[]{:S(2)}) collective-permute-start(bf16[1024,6,64]{0,2,1:T(8,128)(2,1)} %select_convert_fusion.35), channel_id=1, source_target_pairs={{2,0},{4,2},{6,4},{8,6},{10,8},{12,10},{14,12},{16,14},{18,16},{20... | collective-permute-start | bytes 2359304 | tf_op jit(solution)/shard_map/while/body/eval_jaxpr/ppermute | solution.py:24
  2971.9 292.4 %collective-permute-start.15 = (bf16[1024,6,64]{0,2,1:T(8,128)(2,1)S(1)}, bf16[1024,6,64]{0,2,1:T(8,128)(2,1)}, u32[]{:S(2)}, u32[]{:S(2)}) collective-permute-start(bf16[1024,6,64]{0,2,1:T(8,128)(2,1)S(1)} %copy-done.33), channel_id=1, source_target_pairs={{24,0},{26,2},{28,4},{30,6},{0,8},{2,10},{4,12},{6,14},{8,16},{10,... | collective-permute-start | bytes 2359304 | tf_op jit(solution)/shard_map/ppermute | solution.py:24
  2972.0 299.4 %collective-permute-start.17 = (bf16[1024,6,64]{0,2,1:T(8,128)(2,1)S(1)}, bf16[1024,6,64]{0,2,1:T(8,128)(2,1)}, u32[]{:S(2)}, u32[]{:S(2)}) collective-permute-start(bf16[1024,6,64]{0,2,1:T(8,128)(2,1)S(1)} %copy-done.32), channel_id=1, source_target_pairs={{24,0},{26,2},{28,4},{30,6},{0,8},{2,10},{4,12},{6,14},{8,16},{10,... | collective-permute-start | bytes 2359304 | tf_op jit(solution)/shard_map/ppermute | solution.py:24
  2972.1 292.3 %collective-permute-start.14 = (bf16[1024,6,64]{0,2,1:T(8,128)(2,1)}, bf16[1024,6,64]{0,2,1:T(8,128)(2,1)}, u32[]{:S(2)}, u32[]{:S(2)}) collective-permute-start(bf16[1024,6,64]{0,2,1:T(8,128)(2,1)} %get-tuple-element.713), channel_id=1, source_target_pairs={{8,0},{10,2},{12,4},{14,6},{16,8},{18,10},{20,12},{22,14},{24,16},... | collective-permute-start | bytes 2359304 | tf_op jit(solution)/shard_map/ppermute | solution.py:24
  3001.3 270.1 %collective-permute-start.16 = (bf16[1024,6,64]{0,2,1:T(8,128)(2,1)S(1)}, bf16[1024,6,64]{0,2,1:T(8,128)(2,1)}, u32[]{:S(2)}, u32[]{:S(2)}) collective-permute-start(bf16[1024,6,64]{0,2,1:T(8,128)(2,1)S(1)} %copy-done.35), channel_id=1, source_target_pairs={{8,0},{10,2},{12,4},{14,6},{16,8},{18,10},{20,12},{22,14},{24,16},... | collective-permute-start | bytes 2359304 | tf_op jit(solution)/shard_map/ppermute | solution.py:24
  3293.7 454.6 %all-reduce.16.cloned.1.call-start = ((), (), s32[]{:S(2)}) async-start(), calls=%async_computation.4 | async-start | bytes 29884416 | tf_op jit(solution)/shard_map/psum | solution.py:344
  (213 other events, 6019.8 us)
Sparse Core Ops, SparseCore 0:
  970.3 168.5 all-reduce.7
  1166.3 21.5 all-reduce.9
  1210.3 21.5 all-reduce.11
  3293.8 23.5 all-reduce.13
  3324.2 423.9 all-reduce.15
where the time goes:
time: 3780 us; the launch traced here: 3770 us
  waiting for transfers between devices  1390 us (37%)
  starting transfers between devices  992 us (26%)
  matrix products  528 us (14%)
  local copies, waits for them, and re-layouts  364 us (10%)
  other arithmetic  315 us (8%)
  blocking collectives  82.6 us (2%)
  loops' own time  76.5 us (2%)
    ppermute x52, starting transfers between devices, from_behind(): return lax.ppermute(block, axis, route)  983 us
    ppermute x52, waiting for transfers between devices, from_behind(): return lax.ppermute(block, axis, route)  894 us
    psum x1, waiting for transfers between devices, body(): lax.psum((grad_query, grad_key, grad_value, grad_out, grad_up, grad_down,...  320 us
    psum x1, waiting for transfers between devices, body(): lax.psum(jnp.dot(mixed_heads, out_weight, preferred_element_type=jnp.floa...  168 us
    dot_general x2, matrix products, attend_compute(): jnp.einsum('hqk,khd->qhd', weights, values, preferred_element_type=jnp.fl...  133 us
    dot_general x2, matrix products, back_compute(): jnp.einsum('qhd,khd->hqk', grad_rows, values, preferred_element_type=jnp....  131 us
    dot_general x2, matrix products, back_compute(): jnp.einsum('hqk,qhd->khd', weights, grad_rows, preferred_element_type=jnp...  113 us
    convert_element_type x32, local copies, waits for them, and re-layouts, body(): conv_taps[None, :, offset, None] * rim_values[offset:offset + tokens]  97.5 us
  transfers between devices with their start and end apart: 61, of which 36 were waited for; matrix products, arithmetic and copies ran while one was open for 25% of the time, Pallas kernels for 0%

commit v1 on v0

v1 whole, which is shorter than its diff:
```python
from functools import partial
import math

import jax
import jax.numpy as jnp
from jax import lax
from jax.experimental import pallas as pl
from jax.experimental.pallas import tpu as pltpu
from jax.sharding import PartitionSpec as P

TAU = 8
BITS = 8
CONV = 33
MOST = 4096
RIM = (CONV - 1) // 2

EPS_UNIT = 1e-06
EPS_LAYER = 1e-05
SHARP = 4.0
CLIP_EDGE = 0.999

TILE = 256
CHUNK = 512
PAIR = 128
STRIP = 128
FAR_ID = 1 << 20

F32 = jnp.float32
BF16 = jnp.bfloat16

ARC = (
    0.49999961256980896,
    -0.06828052550554276,
    0.027964841574430466,
    -0.014291195198893547,
    0.006136968266218901,
    -0.001371906721033156,
)


def params(**kwargs):
    return pltpu.CompilerParams(vmem_limit_bytes=56 << 20, **kwargs)


def nn(left, right):
    return lax.dot_general(left, right, (((1,), (0,)), ((), ())), preferred_element_type=F32)


def nt(left, right):
    return lax.dot_general(left, right, (((1,), (1,)), ((), ())), preferred_element_type=F32)


def tn(left, right):
    return lax.dot_general(left, right, (((0,), (0,)), ((), ())), preferred_element_type=F32)


def head_masks(head_dim):
    lanes = lax.broadcasted_iota(jnp.int32, (1, PAIR), 1)
    first = (lanes < head_dim).astype(F32)
    return first.astype(BF16), (1.0 - first).astype(BF16)


def head_sum(rows, head_dim):
    here = lax.broadcasted_iota(jnp.int32, (PAIR, PAIR), 0) // head_dim
    there = lax.broadcasted_iota(jnp.int32, (PAIR, PAIR), 1) // head_dim
    ones = (here == there).astype(F32).astype(BF16)
    sums = []
    for start in range(0, rows.shape[1], PAIR):
        part = rows[:, start : start + PAIR]
        high = part.astype(BF16)
        low = (part - high.astype(F32)).astype(BF16)
        sums.append(nn(high, ones) + nn(low, ones))
    return jnp.concatenate(sums, axis=1)


def project_kernel(units, head_dim, x_ref, w_ref, *out_refs):
    width = out_refs[-1].shape[1]
    whole = nn(x_ref[...], w_ref[...])
    for index in range(units):
        part = whole[:, index * width : (index + 1) * width]
        scale = lax.rsqrt(head_sum(part * part, head_dim) * (1.0 / head_dim) + EPS_UNIT)
        scale = scale * (1.0 / math.sqrt(head_dim))
        out_refs[2 * index][...] = (part * scale).astype(BF16)
        out_refs[2 * index + 1][...] = scale
    out_refs[-1][...] = whole[:, units * width :].astype(BF16)


def project(x, weight, units, head_dim):
    rows, depth = x.shape
    width = weight.shape[1] // (units + 1)
    row_spec = pl.BlockSpec((CHUNK, width), lambda i: (i, 0))
    unit_shapes = [
        jax.ShapeDtypeStruct((rows, width), BF16),
        jax.ShapeDtypeStruct((rows, width), F32),
    ]
    return pl.pallas_call(
        partial(project_kernel, units, head_dim),
        grid=(rows // CHUNK,),
        in_specs=[
            pl.BlockSpec((CHUNK, depth), lambda i: (i, 0)),
            pl.BlockSpec(weight.shape, lambda i: (0, 0)),
        ],
        out_specs=[row_spec] * (2 * units + 1),
        out_shape=unit_shapes * units + [jax.ShapeDtypeStruct((rows, width), BF16)],
        compiler_params=params(),
        cost_estimate=pl.CostEstimate(
            flops=2 * rows * depth * weight.shape[1],
            bytes_accessed=rows * (depth * 2 + width * (6 * units + 2)),
            transcendentals=0,
        ),
        name="project",
    )(x, weight)


def collide_parts(scores):
    size = jnp.minimum(jnp.abs(scores), CLIP_EDGE)
    rest = 1.0 - size
    root = lax.rsqrt(rest)
    poly = ARC[5]
    for factor in ARC[4::-1]:
        poly = poly * size + factor
    angle = (rest * root) * poly
    return size, root, jnp.where(scores < 0.0, angle, 1.0 - angle)


def tile_facts(table, tiles_q, tiles_k, qi, kt):
    q_low, q_high = table[qi], table[tiles_q + qi]
    k_low, k_high = table[2 * tiles_q + kt], table[2 * tiles_q + tiles_k + kt]
    needed = (k_high >= q_low) & (k_low <= q_high)
    whole = (q_low == q_high) & (k_low == k_high)
    return needed, whole


def attend_kernel(head_dim, seeded, table, q_ref, k_ref, v_ref, qcol_ref, krow_ref, *rest):
    out_ref = rest[-1]
    tiles_q, tiles_k = q_ref.shape[0] // TILE, k_ref.shape[0] // TILE
    masks = head_masks(head_dim)
    if seeded:
        out_ref[...] = rest[0][...]
    else:
        out_ref[...] = jnp.zeros_like(out_ref)

    def q_loop(qi, carry):
        rows = pl.ds(pl.multiple_of(qi * TILE, TILE), TILE)

        def k_loop(kt, inner):
            needed, whole = tile_facts(table, tiles_q, tiles_k, qi, kt)

            def part(same):
                cols = pl.ds(pl.multiple_of(kt * TILE, TILE), TILE)
                q, k, v = q_ref[rows, :], k_ref[cols, :], v_ref[cols, :]
                total = None
                for mask in masks:
                    chance = collide_parts(nt(q * mask, k))[2]
                    chance = chance * chance
                    chance = chance * chance
                    chance = chance * chance
                    if same is not None:
                        chance = jnp.where(same, chance, 0.0)
                    term = nn(chance.astype(BF16), v * mask)
                    total = term if total is None else total + term
                out_ref[rows, :] += total

            @pl.when(needed & whole)
            def _():
                part(None)

            @pl.when(needed & jnp.logical_not(whole))
            def _():
                ids = qcol_ref[rows, :]
                part(jnp.concatenate([ids, ids], axis=1) == krow_ref[pl.ds(kt, 1), :])

            return inner

        return lax.fori_loop(0, tiles_k, k_loop, carry)

    lax.fori_loop(0, tiles_q, q_loop, 0)


def attend(q, k, v, own_ids, key_ids, head_dim, seed=None):
    tokens, width = q.shape
    far = k.shape[0]
    table, qcol, krow = mask_tables(own_ids, key_ids)
    operands = [q, k, v, qcol, krow]
    q_spec = pl.BlockSpec((tokens, PAIR), lambda p, t: (0, p))
    k_spec = pl.BlockSpec((far, PAIR), lambda p, t: (0, p))
    specs = [
        q_spec,
        k_spec,
        k_spec,
        pl.BlockSpec(qcol.shape, lambda p, t: (0, 0)),
        pl.BlockSpec(krow.shape, lambda p, t: (0, 0)),
    ]
    if seed is not None:
        operands.append(seed)
        specs.append(q_spec)
    return pl.pallas_call(
        partial(attend_kernel, head_dim, seed is not None),
        grid_spec=pltpu.PrefetchScalarGridSpec(
            num_scalar_prefetch=1, grid=(width // PAIR,), in_specs=specs, out_specs=q_spec
        ),
        out_shape=jax.ShapeDtypeStruct((tokens, width), F32),
        compiler_params=params(),
        cost_estimate=pl.CostEstimate(
            flops=8 * tokens * far * width, bytes_accessed=far * width * 4, transcendentals=0
        ),
        name="attend",
    )(table, *operands)


def mask_tables(own_ids, key_ids):
    table = jnp.concatenate(
        [
            own_ids[::TILE],
            own_ids[TILE - 1 :: TILE],
            key_ids[::TILE],
            key_ids[TILE - 1 :: TILE],
        ]
    )
    qcol = jnp.broadcast_to(own_ids[:, None], (own_ids.shape[0], PAIR))
    return table, qcol, key_ids.reshape(-1, TILE)


def back_attend_kernel(
    head_dim,
    seeded,
    table,
    q_ref,
    g_ref,
    k_ref,
    v_ref,
    kcol_ref,
    qrow_ref,
    *rest,
):
    dk_ref, dv_ref, dq_ref, acc_k, acc_v = rest[-5:]
    tiles_q, tiles_k = q_ref.shape[0] // TILE, k_ref.shape[0] // TILE
    masks = head_masks(head_dim)
    if seeded:
        dq_ref[...] = rest[0][...]
    else:
        dq_ref[...] = jnp.zeros_like(dq_ref)

    def k_loop(kt, carry):
        cols = pl.ds(pl.multiple_of(kt * TILE, TILE), TILE)
        acc_k[...] = jnp.zeros_like(acc_k)
        acc_v[...] = jnp.zeros_like(acc_v)

        def q_loop(qi, inner):
            needed, whole = tile_facts(table, tiles_q, tiles_k, qi, kt)

            def part(same):
                rows = pl.ds(pl.multiple_of(qi * TILE, TILE), TILE)
                q, g, k, v = q_ref[rows, :], g_ref[rows, :], k_ref[cols, :], v_ref[cols, :]
                k_turned = k.T
                sum_k, sum_v = None, None
                for index, mask in enumerate(masks):
                    q_half, g_half = q * mask, g * mask
                    scores = nt(k, q_half)
                    size, root, chance = collide_parts(scores)
                    second = chance * chance
                    fourth = second * second
                    weights = fourth * fourth
                    slope = (fourth * second) * (chance * (root * lax.rsqrt(1.0 + size)))
                    inside = jnp.abs(scores) <= CLIP_EDGE
                    if same is not None:
                        inside = inside & same
                        weights = jnp.where(same, weights, 0.0)
                    slope = jnp.where(inside, nt(v, g_half) * slope, 0.0).astype(BF16)
                    term_v = nn(weights.astype(BF16), g_half)
                    term_k = nn(slope, q_half)
                    sum_v = term_v if sum_v is None else sum_v + term_v
                    sum_k = term_k if sum_k is None else sum_k + term_k
                    half = slice(index * head_dim, (index + 1) * head_dim)
                    dq_ref[half, rows] += nn(k_turned[half, :], slope)
                acc_v[...] += sum_v
                acc_k[...] += sum_k

            @pl.when(needed & whole)
            def _():
                part(None)

            @pl.when(needed & jnp.logical_not(whole))
            def _():
                ids = kcol_ref[cols, :]
                part(jnp.concatenate([ids, ids], axis=1) == qrow_ref[pl.ds(qi, 1), :])

            return inner

        lax.fori_loop(0, tiles_q, q_loop, 0)
        dk_ref[cols, :] = acc_k[...].astype(BF16)
        dv_ref[cols, :] = acc_v[...].astype(BF16)
        return carry

    lax.fori_loop(0, tiles_k, k_loop, 0)


def back_attend(q, g, k, v, own_ids, key_ids, head_dim, seed=None):
    tokens, width = q.shape
    far = k.shape[0]
    table, _, _ = mask_tables(own_ids, key_ids)
    kcol = jnp.broadcast_to(key_ids[:, None], (far, PAIR))
    qrow = own_ids.reshape(-1, TILE)
    q_spec = pl.BlockSpec((tokens, PAIR), lambda p, t: (0, p))
    k_spec = pl.BlockSpec((far, PAIR), lambda p, t: (0, p))
    dq_spec = pl.BlockSpec((PAIR, tokens), lambda p, t: (p, 0))
    specs = [
        q_spec,
        q_spec,
        k_spec,
        k_spec,
        pl.BlockSpec(kcol.shape, lambda p, t: (0, 0)),
        pl.BlockSpec(qrow.shape, lambda p, t: (0, 0)),
    ]
    operands = [q, g, k, v, kcol, qrow]
    if seed is not None:
        operands.append(seed)
        specs.append(dq_spec)
    return pl.pallas_call(
        partial(back_attend_kernel, head_dim, seed is not None),
        grid_spec=pltpu.PrefetchScalarGridSpec(
            num_scalar_prefetch=1,
            grid=(width // PAIR,),
            in_specs=specs,
            out_specs=[k_spec, k_spec, dq_spec],
            scratch_shapes=[pltpu.VMEM((TILE, PAIR), F32), pltpu.VMEM((TILE, PAIR), F32)],
        ),
        out_shape=[
            jax.ShapeDtypeStruct((far, width), BF16),
            jax.ShapeDtypeStruct((far, width), BF16),
            jax.ShapeDtypeStruct((width, tokens), F32),
        ],
        compiler_params=params(),
        cost_estimate=pl.CostEstimate(
            flops=16 * tokens * far * width, bytes_accessed=far * width * 8, transcendentals=0
        ),
        name="back_attend",
    )(table, *operands)


def back_project_kernel(units, turned, head_dim, need, x_ref, w_ref, *refs):
    dx_ref, dw_ref = refs[-2:]
    step = pl.program_id(0)

    @pl.when(step == 0)
    def _():
        dw_ref[...] = jnp.zeros_like(dw_ref)

    @pl.when(need[step] > 0)
    def _():
        grads = []
        for index in range(units):
            unit_ref, scale_ref, grad_ref = refs[3 * index : 3 * index + 3]
            grad = grad_ref[...].astype(F32)
            if index < turned:
                grad = grad.T
            unit = unit_ref[...].astype(F32)
            inner = head_sum(grad * unit, head_dim)
            grads.append(
                ((TAU / math.pi) * scale_ref[...] * (grad - unit * inner)).astype(BF16)
            )
        value_refs = refs[3 * units : -2]
        value = value_refs[0][...].astype(F32)
        for extra in value_refs[1:]:
            value = value + extra[...].astype(F32)
        grads.append(value.astype(BF16))
        joined = jnp.concatenate(grads, axis=1)
        dx_ref[...] = nt(joined, w_ref[...]).astype(BF16)
        dw_ref[...] += tn(x_ref[...], joined)

    @pl.when(need[step] == 0)
    def _():
        dx_ref[...] = jnp.zeros_like(dx_ref)


def back_project(x, weight, parts, turned, values, need, head_dim):
    rows, depth = x.shape
    width = values[0].shape[1]
    row_spec = pl.BlockSpec((CHUNK, width), lambda i, n: (i, 0))
    wide_spec = pl.BlockSpec((CHUNK, depth), lambda i, n: (i, 0))
    weight_spec = pl.BlockSpec(weight.shape, lambda i, n: (0, 0))
    specs, operands = [wide_spec, weight_spec], [x, weight]
    for index, (unit, scale, grad) in enumerate(parts):
        operands += [unit, scale, grad]
        specs += [row_spec, row_spec]
        specs.append(
            pl.BlockSpec((width, CHUNK), lambda i, n: (0, i)) if index < turned else row_spec
        )
    operands += values
    specs += [row_spec] * len(values)
    return pl.pallas_call(
        partial(back_project_kernel, len(parts), turned, head_dim),
        grid_spec=pltpu.PrefetchScalarGridSpec(
            num_scalar_prefetch=1,
            grid=(rows // CHUNK,),
            in_specs=specs,
            out_specs=[wide_spec, weight_spec],
        ),
        out_shape=[
            jax.ShapeDtypeStruct((rows, depth), BF16),
            jax.ShapeDtypeStruct(weight.shape, F32),
        ],
        compiler_params=params(),
        cost_estimate=pl.CostEstimate(
            flops=4 * rows * depth * weight.shape[1],
            bytes_accessed=rows * 12 * depth,
            transcendentals=0,
        ),
        name="back_project",
    )(need, *operands)


def band_windows(ids_ext, tokens):
    start = STRIP // 2
    return jnp.stack(
        [ids_ext[start + row : start + row + 2 * STRIP] for row in range(0, tokens, STRIP)]
    )


def lane_taps(conv_taps, mirrored):
    front = STRIP // 2 - RIM
    heads = conv_taps.shape[0]
    taps = conv_taps[:, ::-1] if mirrored else conv_taps
    return jnp.pad(taps, ((0, -heads % 8), (front, 2 * STRIP - front - CONV)))


def fill_bands(taps_ref, bands, heads):
    for head in range(heads):
        row = jnp.broadcast_to(taps_ref[head : head + 1, :], (STRIP, 2 * STRIP))
        bands[head] = pltpu.roll(row, 0, 1, stride=1, stride_axis=0)


def band_product(band, same, window):
    band = jnp.where(same, band, 0.0)
    high = band.astype(BF16)
    low = (band - high.astype(F32)).astype(BF16)
    return nn(high, window) + nn(low, window)


def mix_kernel(head_dim, g_ref, v_ref, qcol_ref, krow_ref, taps_ref, out_ref, bands):
    heads = g_ref.shape[1] // head_dim
    step = pl.program_id(0)

    @pl.when(step == 0)
    def _():
        fill_bands(taps_ref, bands, heads)

    masks = head_masks(head_dim)
    window = v_ref[pl.ds(pl.multiple_of(step * STRIP + STRIP // 2, STRIP // 2), 2 * STRIP), :]
    ids = qcol_ref[...]
    same = jnp.concatenate([ids, ids], axis=1) == krow_ref[pl.ds(step, 1), :]
    pieces = []
    for pair in range(heads // 2):
        values = window[:, pair * PAIR : (pair + 1) * PAIR]
        total = None
        for index, mask in enumerate(masks):
            term = band_product(bands[2 * pair + index], same, values * mask)
            total = term if total is None else total + term
        pieces.append(total)
    gathered = g_ref[...]
    scale = lax.rsqrt(head_sum(gathered * gathered, head_dim) * (1.0 / head_dim) + EPS_UNIT)
    out_ref[...] = (gathered * scale + jnp.concatenate(pieces, axis=1)).astype(BF16)


def mix(gathered, values_ext, own_ids, ids_ext, conv_taps, head_dim):
    tokens, width = gathered.shape
    heads = width // head_dim
    qcol = jnp.broadcast_to(own_ids[:, None], (tokens, PAIR))
    krow = band_windows(ids_ext, tokens)
    taps = lane_taps(conv_taps, False)
    row_spec = pl.BlockSpec((STRIP, width), lambda i: (i, 0))
    return pl.pallas_call(
        partial(mix_kernel, head_dim),
        grid=(tokens // STRIP,),
        in_specs=[
            row_spec,
            pl.BlockSpec(values_ext.shape, lambda i: (0, 0)),
            pl.BlockSpec((STRIP, PAIR), lambda i: (i, 0)),
            pl.BlockSpec(krow.shape, lambda i: (0, 0)),
            pl.BlockSpec(taps.shape, lambda i: (0, 0)),
        ],
        out_specs=row_spec,
        out_shape=jax.ShapeDtypeStruct((tokens, width), BF16),
        scratch_shapes=[pltpu.VMEM((heads, STRIP, 2 * STRIP), F32)],
        compiler_params=params(),
        cost_estimate=pl.CostEstimate(
            flops=4 * tokens * 2 * STRIP * width, bytes_accessed=tokens * width * 8, transcendentals=0
        ),
        name="mix",
    )(gathered, values_ext, qcol, krow, taps)


def back_norm_kernel(head_dim, g_ref, m_ref, out_ref):
    gathered, grad = g_ref[...], m_ref[...].astype(F32)
    scale = lax.rsqrt(head_sum(gathered * gathered, head_dim) * (1.0 / head_dim) + EPS_UNIT)
    mean = head_sum(grad * gathered, head_dim) * (1.0 / head_dim)
    out_ref[...] = (scale * (grad - (scale * scale) * gathered * mean)).astype(BF16)


def back_norm(gathered, grad_mixed, head_dim):
    tokens, width = gathered.shape
    row_spec = pl.BlockSpec((TILE, width), lambda i: (i, 0))
    return pl.pallas_call(
        partial(back_norm_kernel, head_dim),
        grid=(tokens // TILE,),
        in_specs=[row_spec, row_spec],
        out_specs=row_spec,
        out_shape=jax.ShapeDtypeStruct((tokens, width), BF16),
        compiler_params=params(),
        cost_estimate=pl.CostEstimate(
            flops=tokens * width * 512, bytes_accessed=tokens * width * 8, transcendentals=0
        ),
        name="back_norm",
    )(gathered, grad_mixed)


def back_conv_kernel(
    head_dim, v_ref, m_ref, col_ref, row_ref, taps_ref, dv_ref, tap_ref, bands, sums
):
    heads = dv_ref.shape[1] // head_dim
    step = pl.program_id(0)

    @pl.when(step == 0)
    def _():
        fill_bands(taps_ref, bands, heads)
        sums[...] = jnp.zeros_like(sums)

    masks = head_masks(head_dim)
    around = pl.ds(pl.multiple_of(step * STRIP + STRIP // 2, STRIP // 2), 2 * STRIP)
    centre = pl.ds(pl.multiple_of(step * STRIP + STRIP, STRIP), STRIP)
    ids = col_ref[...]
    same = jnp.concatenate([ids, ids], axis=1) == row_ref[pl.ds(step, 1), :]
    pieces = []
    for pair in range(heads // 2):
        cols = slice(pair * PAIR, (pair + 1) * PAIR)
        grads = m_ref[around, cols]
        values = v_ref[around, cols]
        here = m_ref[centre, cols]
        total = None
        for index, mask in enumerate(masks):
            head = 2 * pair + index
            term = band_product(bands[head], same, grads * mask)
            total = term if total is None else total + term
            sums[head] += jnp.where(same, nt(here * mask, values), 0.0)
        pieces.append(total)
    dv_ref[...] = jnp.concatenate(pieces, axis=1)

    @pl.when(step == pl.num_programs(0) - 1)
    def _():
        tap_ref[...] = jnp.zeros_like(tap_ref)
        places = [lax.broadcasted_iota(jnp.int32, (STRIP, STRIP), d) for d in (0, 1)]
        flip = (places[0] + places[1] == STRIP - 1).astype(F32).astype(BF16)
        for head in range(heads):
            whole = sums[head]
            high = whole.astype(BF16)
            low = (whole - high.astype(F32)).astype(BF16)
            turned = pltpu.roll(
                nn(flip, high) + nn(flip, low), STRIP + 1, 1, stride=1, stride_axis=0
            )
            tap_ref[head : head + 1, :] = jnp.sum(turned, axis=0, keepdims=True)


def back_conv(values_ext, grad_ext, own_ids, ids_ext, conv_taps, head_dim):
    tokens, width = own_ids.shape[0], values_ext.shape[1]
    heads = width // head_dim
    col = jnp.broadcast_to(own_ids[:, None], (tokens, PAIR))
    row = band_windows(ids_ext, tokens)
    taps = lane_taps(conv_taps, True)
    front = STRIP // 2 - RIM
    grad_values, tap_sums = pl.pallas_call(
        partial(back_conv_kernel, head_dim),
        grid=(tokens // STRIP,),
        in_specs=[
            pl.BlockSpec(values_ext.shape, lambda i: (0, 0)),
            pl.BlockSpec(grad_ext.shape, lambda i: (0, 0)),
            pl.BlockSpec((STRIP, PAIR), lambda i: (i, 0)),
            pl.BlockSpec(row.shape, lambda i: (0, 0)),
            pl.BlockSpec(taps.shape, lambda i: (0, 0)),
        ],
        out_specs=[
            pl.BlockSpec((STRIP, width), lambda i: (i, 0)),
            pl.BlockSpec(taps.shape, lambda i: (0, 0)),
        ],
        out_shape=[
            jax.ShapeDtypeStruct((tokens, width), F32),
            jax.ShapeDtypeStruct(taps.shape, F32),
        ],
        scratch_shapes=[
            pltpu.VMEM((heads, STRIP, 2 * STRIP), F32),
            pltpu.VMEM((heads, STRIP, 2 * STRIP), F32),
        ],
        compiler_params=params(),
        cost_estimate=pl.CostEstimate(
            flops=6 * tokens * 2 * STRIP * width, bytes_accessed=tokens * width * 8, transcendentals=0
        ),
        name="back_conv",
    )(values_ext, grad_ext, col, row, taps)
    return grad_values, tap_sums[:heads, front : front + CONV]


def occupancy_kernel(head_dim, hashes, k_ref, w_ref, out_ref):
    combos = 4
    lanes = hashes * combos
    wide = hashes * combos * combos

    @pl.when(pl.program_id(1) == 0)
    def _():
        out_ref[...] = jnp.zeros_like(out_ref)

    source = lax.broadcasted_iota(jnp.int32, (lanes, wide), 0)
    target = lax.broadcasted_iota(jnp.int32, (lanes, wide), 1)
    same_hash = (source // combos) == (target // (combos * combos))
    picks = []
    for divisor in (1, combos):
        chosen = same_hash & ((source % combos) == ((target // divisor) % combos))
        picks.append(chosen.astype(F32).astype(BF16))
    keys = k_ref[...]
    for index in range(2):
        signed = nn(keys, w_ref[index])
        halves = []
        for half in range(2):
            product = None
            for pick in range(2):
                start = (half * 2 + pick) * 2 * lanes
                one = 1.0 + jnp.exp(-signed[:, start : start + lanes])
                two = 1.0 + jnp.exp(-signed[:, start + lanes : start + 2 * lanes])
                spread = nn((1.0 / (one * two)).astype(BF16), picks[pick])
                product = spread if product is None else product * spread
            halves.append(product.astype(BF16))
        low, high = halves
        for start in range(0, wide, PAIR):
            block = slice(start, start + PAIR)
            out_ref[index, block, :] += tn(high[:, block], low[:, block])


def occupancy(key_unit, hyperplanes, scale):
    tokens, width = key_unit.shape
    hashes, bits, head_dim = hyperplanes.shape
    pairs = width // PAIR
    wide = hashes * 16
    planes = SHARP * hyperplanes.astype(F32)
    columns = []
    for group in range(bits // 2):
        for bit in range(2):
            signs = 2.0 * ((jnp.arange(4) // (2**bit)) % 2).astype(F32) - 1.0
            plane = planes[:, 2 * group + bit, :]
            columns.append((plane.T[:, :, None] * signs).reshape(head_dim, hashes * 4))
    weight = jnp.concatenate(columns, axis=1).astype(BF16)
    blank = jnp.zeros_like(weight)
    weights = jnp.stack(
        [jnp.concatenate([weight, blank], axis=0), jnp.concatenate([blank, weight], axis=0)]
    )
    counts = pl.pallas_call(
        partial(occupancy_kernel, head_dim, hashes),
        grid=(pairs, tokens // TILE),
        in_specs=[
            pl.BlockSpec((TILE, PAIR), lambda p, t: (t, p)),
            pl.BlockSpec(weights.shape, lambda p, t: (0, 0, 0)),
        ],
        out_specs=pl.BlockSpec((2, wide, PAIR), lambda p, t: (p, 0, 0)),
        out_shape=jax.ShapeDtypeStruct((2 * pairs, wide, PAIR), F32),
        compiler_params=params(),
        cost_estimate=pl.CostEstimate(
            flops=tokens * width * 16000, bytes_accessed=tokens * width * 4, transcendentals=0
        ),
        name="occupancy",
    )(key_unit, weights)
    blocks = counts.reshape(2 * pairs, wide // PAIR, PAIR // 16, 16, PAIR // 16, 16)
    picked = jnp.stack([blocks[:, :, i, :, i, :] for i in range(PAIR // 16)], axis=2)
    return picked.reshape(2 * pairs, hashes, 256) * scale


def doc_ids(lengths, positions, all_tokens):
    doc_ends = jnp.cumsum(lengths)
    doc_index = jnp.sum((doc_ends[None, :] <= positions[:, None]).astype(jnp.int32), axis=1)
    doc_index = jnp.where(positions < 0, -1, doc_index)
    return jnp.where(positions >= all_tokens, FAR_ID, doc_index)


def shifted(block, axis, distance):
    count = lax.axis_size(axis)
    route = [(i, i + distance) for i in range(count) if 0 <= i + distance < count]
    return lax.ppermute(block, axis, route)


def swapped(block, axis):
    return lax.ppermute(block, axis, [(0, 1), (1, 0)])


def tp_sum(partial_low):
    return partial_low.astype(F32) + swapped(partial_low, "tp").astype(F32)


def with_rims(block):
    rows, width = block.shape
    below = shifted(block[rows - RIM :], "seq", 1)
    above = shifted(block[:RIM], "seq", -1)
    blank = jnp.zeros((STRIP - RIM, width), block.dtype)
    return jnp.concatenate([blank, below, block, above, blank], axis=0)


def layer_norm(vectors, gain_row, shift_row):
    center = vectors - jnp.mean(vectors, axis=-1, keepdims=True)
    spread = jnp.mean(center * center, axis=-1, keepdims=True)
    return center * lax.rsqrt(spread + EPS_LAYER) * gain_row + shift_row


def body(
    inputs,
    cotangent,
    query_weight,
    key_weight,
    value_weight,
    out_weight,
    up_weight,
    down_weight,
    conv_taps,
    attn_gain,
    attn_shift,
    ffn_gain,
    ffn_shift,
    hyperplanes,
    lengths,
):
    tokens, depth = inputs.shape
    head_dim = hyperplanes.shape[2]
    width = query_weight.shape[1]
    half = tokens // 2
    my_index = lax.axis_index("seq")
    my_side = lax.axis_index("tp")
    all_tokens = tokens * lax.axis_size("seq")
    far_reach = (MOST + tokens - 2) // tokens
    near = [d for d in range(1, far_reach + 1) if d <= far_reach // 2]
    far = [d for d in range(1, far_reach + 1) if d > far_reach // 2]
    groups = [[s * d for d in part for s in (1, -1)] for part in (near, far)]

    own_ids = doc_ids(lengths, my_index * tokens + jnp.arange(tokens, dtype=jnp.int32), all_tokens)
    ids_ext = doc_ids(
        lengths,
        my_index * tokens - STRIP + jnp.arange(tokens + 2 * STRIP, dtype=jnp.int32),
        all_tokens,
    )

    mine_rows = lax.dynamic_slice_in_dim(inputs, my_side * half, half, 0)
    group_x, group_ids = [], []
    for distances in groups:
        mine = jnp.concatenate([shifted(mine_rows, "seq", d) for d in distances], axis=0)
        group_x.append(jnp.concatenate([mine, swapped(mine, "tp")], axis=0))
        spots = [
            (my_index - d) * tokens + side * half + jnp.arange(half, dtype=jnp.int32)
            for side in (my_side, 1 - my_side)
            for d in distances
        ]
        group_ids.append(doc_ids(lengths, jnp.concatenate(spots), all_tokens))

    weight_qkv = jnp.concatenate([query_weight, key_weight, value_weight], axis=1)
    weight_kv = weight_qkv[:, width:]
    query_unit, query_scale, key_unit, key_scale, values = project(inputs, weight_qkv, 2, head_dim)
    values_ext = with_rims(values)
    occ_local = occupancy(key_unit, hyperplanes, 2.0**BITS / all_tokens)
    gathered = attend(query_unit, key_unit, values, own_ids, own_ids, head_dim)
    group_kv = []
    for x_far, ids_far in zip(group_x, group_ids):
        key_far, scale_far, value_far = project(x_far, weight_kv, 1, head_dim)
        group_kv.append((key_far, scale_far, value_far))
        gathered = attend(
            query_unit, key_far, value_far, own_ids, ids_far, head_dim, seed=gathered
        )
    mixed = mix(gathered, values_ext, own_ids, ids_ext, conv_taps, head_dim)

    attn_out = tp_sum(nn(mixed, out_weight).astype(BF16))
    first_norm, first_back = jax.vjp(
        layer_norm, inputs.astype(F32) + attn_out, attn_gain, attn_shift
    )
    first_low = first_norm.astype(BF16)
    hidden = nn(first_low, up_weight)
    active = jax.nn.gelu(hidden, approximate=False).astype(BF16)
    ffn_out = tp_sum(nn(active, down_weight).astype(BF16))
    result, second_back = jax.vjp(layer_norm, first_norm + ffn_out, ffn_gain, ffn_shift)
    output = result.astype(BF16)
    grad_second, grad_ffn_gain, grad_ffn_shift = second_back(cotangent.astype(F32))
    grad_ffn = grad_second.astype(BF16)
    grad_active = nt(grad_ffn, down_weight)
    unused_gelu, gelu_back = jax.vjp(partial(jax.nn.gelu, approximate=False), hidden)
    grad_hidden = gelu_back(grad_active)[0].astype(BF16)
    grad_first = grad_second + tp_sum(nt(grad_hidden, up_weight).astype(BF16))
    grad_residual, grad_attn_gain, grad_attn_shift = first_back(grad_first)
    grad_attn = grad_residual.astype(BF16)
    grad_mixed = nt(grad_attn, out_weight).astype(BF16)

    grad_down = tn(active, grad_ffn)
    grad_up = tn(first_low, grad_hidden)
    grad_out = tn(mixed, grad_attn)
    dense = jnp.concatenate(
        [grad_down.reshape(-1, depth), grad_up.reshape(-1, depth), grad_out.reshape(-1, depth)]
    ).astype(BF16)
    dense = lax.psum(dense, "seq")

    grad_rows = back_norm(gathered, grad_mixed, head_dim)
    grad_ext = with_rims(grad_mixed)

    grad_query_turned = None
    kv_weight_grad = None
    homes = None
    for distances, x_far, ids_far, kv_far in reversed(
        list(zip(groups, group_x, group_ids, group_kv))
    ):
        key_far, scale_far, value_far = kv_far
        dk, dv, grad_query_turned = back_attend(
            query_unit,
            grad_rows,
            key_far,
            value_far,
            own_ids,
            ids_far,
            head_dim,
            seed=grad_query_turned,
        )
        need = (
            (ids_far[CHUNK - 1 :: CHUNK] >= own_ids[0]) & (ids_far[::CHUNK] <= own_ids[-1])
        ).astype(jnp.int32)
        dx, dw = back_project(
            x_far, weight_kv, [(key_far, scale_far, dk)], 0, [dv], need, head_dim
        )
        kv_weight_grad = dw if kv_weight_grad is None else kv_weight_grad + dw
        count = len(distances) * half
        both = tp_half_sum(dx[:count], dx[count:])
        for index, distance in enumerate(distances):
            home = shifted(both[index * half : (index + 1) * half], "seq", -distance)
            home = home.astype(F32)
            homes = home if homes is None else homes + home

    dk, dv, grad_query_turned = back_attend(
        query_unit,
        grad_rows,
        key_unit,
        values,
        own_ids,
        own_ids,
        head_dim,
        seed=grad_query_turned,
    )
    grad_conv_values, grad_taps = back_conv(
        values_ext, grad_ext, own_ids, ids_ext, conv_taps, head_dim
    )
    need = jnp.ones((tokens // CHUNK,), jnp.int32)
    dx, dw = back_project(
        inputs,
        weight_qkv,
        [(query_unit, query_scale, grad_query_turned), (key_unit, key_scale, dk)],
        1,
        [dv, grad_conv_values],
        need,
        head_dim,
    )
    mine = lax.dynamic_slice_in_dim(dx, my_side * half, half, 0)
    other = lax.dynamic_slice_in_dim(dx, (1 - my_side) * half, half, 0)
    mine_total = (
        lax.dynamic_slice_in_dim(grad_residual, my_side * half, half, 0)
        + homes
        + tp_half_sum(mine, other).astype(F32)
    )
    other_total = swapped(mine_total, "tp")
    lower = jnp.where(my_side == 0, mine_total, other_total)
    upper = jnp.where(my_side == 0, other_total, mine_total)
    grad_inputs = jnp.concatenate([lower, upper], axis=0)

    qkv = jnp.concatenate([dw[:, :width], dw[:, width:] + kv_weight_grad], axis=1).astype(BF16)
    qkv = lax.psum(qkv, "seq").astype(F32)
    small = lax.psum(
        (grad_taps, grad_attn_gain, grad_attn_shift, grad_ffn_gain, grad_ffn_shift), "seq"
    )
    occ = lax.psum(occ_local, "seq")
    dense = dense.astype(F32)
    ff = down_weight.shape[0]
    return (
        output,
        grad_inputs,
        qkv[:, :width],
        qkv[:, width : 2 * width],
        qkv[:, 2 * width :],
        dense[2 * ff :],
        dense[ff : 2 * ff].reshape(up_weight.shape),
        dense[:ff],
        small[0],
        small[1],
        small[2],
        small[3],
        small[4],
        occ,
    )


def tp_half_sum(mine, other):
    return (mine.astype(F32) + swapped(other, "tp").astype(F32)).astype(BF16)


def solution(mesh):
    return jax.shard_map(
        body,
        mesh=mesh,
        in_specs=(
            P("seq", None),
            P("seq", None),
            P(None, "tp"),
            P(None, "tp"),
            P(None, "tp"),
            P("tp", None),
            P(None, "tp"),
            P("tp", None),
            P("tp", None),
            P(),
            P(),
            P(),
            P(),
            P(),
            P(),
        ),
        out_specs=(
            P("seq", None),
            P("seq", None),
            P(None, "tp"),
            P(None, "tp"),
            P(None, "tp"),
            P("tp", None),
            P(None, "tp"),
            P("tp", None),
            P("tp", None),
            P(),
            P(),
            P(),
            P(),
            P("tp", None, None),
        ),
        check_vma=False,
    )
```

time: 3780 us -> 1160 us (0.31)
  waiting for transfers between devices: 1390 us -> 197 us
  starting transfers between devices: 992 us -> 405 us
  matrix products: 528 us -> 49.8 us
  other arithmetic: 315 us -> 52.8 us
  local copies, waits for them, and re-layouts: 364 us -> 109 us
  Pallas kernels: 0 us -> 240 us
  loops' own time: 76.5 us -> 0 us
    ppermute x56 -> x29, waiting for transfers between devices: 894 us -> 50.1 us  [the longest x20 46.7 us: shifted(): return lax.ppermute(block, axis, route)]
    ppermute x56 -> x29, starting transfers between devices: 992 us -> 405 us  [the longest x20 403 us: shifted(): return lax.ppermute(block, axis, route)]
    dot_general x32 -> x9, matrix products: 528 us -> 49.8 us  [the longest x3 23.6 us: nn(): lax.dot_general(left, right, (((1,), (0,)), ((), ())), preferred_element_...]
    psum x5 -> x2, waiting for transfers between devices: 501 us -> 146 us  [the longest x1 93.2 us: body(): occ = lax.psum(occ_local, 'seq')]
    pallas_call x0 -> x16, Pallas kernels: none -> 240 us  [the longest x3 72.2 us: back_attend(): pl.pallas_call(partial(back_attend_kernel, head_dim, seed is not None), g...]
    convert_element_type x66 -> x0, local copies, waits for them, and re-layouts: 197 us -> none  [the longest x32 97.5 us: body(): conv_taps[None, :, offset, None] * rim_values[offset:offset + tokens]]
    convert_element_type x34 -> x4, other arithmetic: 117 us -> 10.3 us  [the longest x2 6.64 us: tp_half_sum(): return (mine.astype(F32) + swapped(other, 'tp').astype(F32)).astype(BF16)]
    add x52 -> x11, other arithmetic: 91.3 us -> 5.56 us  [the longest x1 5.49 us: body(): lax.dynamic_slice_in_dim(grad_residual, my_side * half, half, 0) + homes]
  transfers between devices with their start and end apart: 61 -> 31, of which waited for: 36 -> 9; matrix products, arithmetic and copies ran while one was open for 25% -> 12% of each run, Pallas kernels for 0% -> 17%
where the time goes in v1:
time: 1160 us
  starting transfers between devices  405 us (35%)
  Pallas kernels  240 us (21%)
  waiting for transfers between devices  197 us (17%)
  local copies, waits for them, and re-layouts  109 us (9%)
  blocking collectives  89.1 us (8%)
  other arithmetic  52.8 us (5%)
  matrix products  49.8 us (4%)
  between operations  15.6 us (1%)
    ppermute x20, starting transfers between devices, shifted(): return lax.ppermute(block, axis, route)  403 us
    psum x1, waiting for transfers between devices, body(): occ = lax.psum(occ_local, 'seq')  93.2 us
    psum x1, blocking collectives, body(): lax.psum((grad_taps, grad_attn_gain, grad_attn_shift, grad_ffn_gain, grad...  89.1 us
    pallas_call x3, Pallas kernels, back_attend(): pl.pallas_call(partial(back_attend_kernel, head_dim, seed is not None), g...  72.2 us
    psum x1, waiting for transfers between devices, body(): qkv = lax.psum(qkv, 'seq').astype(F32)  53.1 us
    pallas_call x3, Pallas kernels, attend(): pl.pallas_call(partial(attend_kernel, head_dim, seed is not None), grid_s...  51.9 us
    ppermute x20, waiting for transfers between devices, shifted(): return lax.ppermute(block, axis, route)  46.7 us
    pallas_call x3, Pallas kernels, back_project(): pl.pallas_call(partial(back_project_kernel, len(parts), turned, head_dim)...  41 us
  transfers between devices with their start and end apart: 31, of which 9 were waited for; matrix products, arithmetic and copies ran while one was open for 12% of the time, Pallas kernels for 17%

profile of v1, /device:TPU:0, one launch (start us, length us, event | category | flops | bytes accessed | tf_op | source)
XLA Modules:
  0.0 1156.8 jit_solution(10036064520448844941)
XLA Ops:
  9.5 5.7 collective-permute-start.5
  16.5 5.5 collective-permute-start.7
  23.3 5.5 collective-permute-start
  34.9 6.4 project.3
  42.1 7.3 collective-permute-done.5
  50.7 39.1 %collective-permute-start.2 = (bf16[512,768]{1,0:T(8,128)(2,1)}, bf16[512,768]{1,0:T(8,128)(2,1)}, u32[]{:S(2)}, u32[]{:S(2)}) collective-permute-start(bf16[512,768]{1,0:T(8,128)(2,1)} %constant_dynamic-slice_fusion.1), channel_id=1, source_target_pairs={{0,8},{2,10},{4,12},{6,14},{8,16},{10,18},{12,20},{14,22},{16,24},... | collective-permute-start | bytes 2359304 | tf_op jit(solution)/shard_map/ppermute | solution.py:683
  98.3 10.1 collective-permute-start.10
  115.6 29.0 %attend.3.rest_0_ = f32[1024,384]{1,0:T(8,128)} custom-call(s32[16]{0:T(128)} %pad_add_fusion.3.table, bf16[1024,384]{1,0:T(8,128)(2,1)} %get-tuple-element.42.q_ref.refs_0_, bf16[1024,384]{1,0:T(8,128)(2,1)} %get-tuple-element.47.k_ref.refs_3_, bf16[1024,384]{1,0:T(8,128)(2,1)} %get-tuple-element.48.v_ref, ...), custom_call_target="tpu_custom_call" | custom-call | flops 3221225472 | bytes 1572864 | tf_op jit(solution)/shard_map/attend/pallas_call | solution.py:197
  164.9 3.8 constant_dynamic-update-slice_fusion.12.x_ref
  168.8 13.2 %project.5 = (bf16[4096,384]{1,0:T(8,128)(2,1)}, f32[4096,384]{1,0:T(8,128)}, bf16[4096,384]{1,0:T(8,128)(2,1)}) custom-call(bf16[4096,768]{1,0:T(8,128)(2,1)} %constant_dynamic-update-slice_fusion.12.x_ref, bf16[768,768]{1,0:T(8,128)(2,1)} %copy-done.25), custom_call_target="tpu_custom_call" | custom-call | flops 4831838208 | bytes 18874368 | tf_op jit(solution)/shard_map/project/pallas_call | solution.py:96
  182.0 3.8 constant_dynamic-update-slice_fusion.4.x_ref
  185.8 13.2 %project.4 = (bf16[4096,384]{1,0:T(8,128)(2,1)}, f32[4096,384]{1,0:T(8,128)}, bf16[4096,384]{1,0:T(8,128)(2,1)}) custom-call(bf16[4096,768]{1,0:T(8,128)(2,1)} %constant_dynamic-update-slice_fusion.4.x_ref, bf16[768,768]{1,0:T(8,128)(2,1)} %copy-done.25), custom_call_target="tpu_custom_call" | custom-call | flops 4831838208 | bytes 18874368 | tf_op jit(solution)/shard_map/project/pallas_call | solution.py:96
  199.0 14.3 %attend.4.rest_0_ = f32[1024,384]{1,0:T(8,128)} custom-call(s32[40]{0:T(128)} %get-tuple-element.148.table, bf16[1024,384]{1,0:T(8,128)(2,1)} %get-tuple-element.42.q_ref.refs_0_, bf16[4096,384]{1,0:T(8,128)(2,1)} %get-tuple-element.45.k_ref.refs_0_, bf16[4096,384]{1,0:T(8,128)(2,1)} %get-tuple-element.46.v_ref, ...), custom_call_target="tpu_custom_call" | custom-call | flops 12884901888 | bytes 6291456 | tf_op jit(solution)/shard_map/attend/pallas_call | solution.py:197
  213.4 8.6 attend.5.g_ref
  222.0 7.9 mix.1
  237.0 17.4 %multiply_convert_fusion = (bf16[1024,1536]{1,0:T(8,128)(2,1)S(1)}, f32[1024,1536]{1,0:T(8,128)}, f32[1024,1536]{1,0:T(8,128)}) fusion(bf16[768,1536]{1,0:T(8,128)(2,1)S(1)} %copy-done, f32[1024,768]{1,0:T(8,128)S(1)} %get-tuple-element.95, f32[768]{0:T(1024)S(1)} %copy-done.34, f32[768]{0:T(1024)S(1)} %copy-done.28, f32[1024]{0:T(1024)S(1)} %fusion.15, ...), kind=kOutput, calls=%fused_computation.5 | convolution fusion | flops 2522087424 | bytes 21248000 | tf_op jit(solution)/shard_map/dot_general | solution.py:46
  254.4 4.1 convolution_convert_fusion.4
  262.3 4.2 fusion.46
  274.9 5.7 add_convert_fusion.2
  280.6 5.7 convolution_convert_fusion.3
  289.3 7.3 convolution_convert_fusion
  300.1 5.8 convolution_convert_fusion.1
  314.4 4.3 back_norm.1.g_ref
  318.7 14.3 %collective-permute-start.25 = (bf16[16,384]{1,0:T(8,128)(2,1)S(1)}, bf16[16,384]{1,0:T(8,128)(2,1)S(1)}, u32[]{:S(2)}, u32[]{:S(2)}) collective-permute-start(bf16[16,384]{1,0:T(8,128)(2,1)S(1)} %get-tuple-element.121), channel_id=1, source_target_pairs={{0,2},{2,4},{4,6},{6,8},{8,10},{10,12},{12,14},{14,16},{16,18},{18... | collective-permute-start | bytes 36872 | tf_op jit(solution)/shard_map/ppermute | solution.py:683
  337.4 11.1 back_attend.3
  348.5 13.2 %back_project.3 = (bf16[4096,768]{1,0:T(8,128)(2,1)}, f32[768,768]{1,0:T(8,128)}) custom-call(s32[8]{0:T(128)} %and_convert_fusion.1.need, bf16[4096,768]{1,0:T(8,128)(2,1)} %constant_dynamic-update-slice_fusion.4.x_ref, bf16[768,768]{1,0:T(8,128)(2,1)} %copy-done.25, bf16[4096,384]{1,0:T(8,128)(2,1)} %get-tuple-element.43.k_ref.refs_0_, ...), custom_call_target="tpu_custom_call" | custom-call | flops 9663676416 | bytes 37748736 | tf_op jit(solution)/shard_map/back_project/pallas_call | solution.py:391
  368.3 20.0 %back_attend.4 = (bf16[4096,384]{1,0:T(8,128)(2,1)}, bf16[4096,384]{1,0:T(8,128)(2,1)}, f32[384,1024]{1,0:T(8,128)}) custom-call(s32[40]{0:T(128)} %get-tuple-element.148.table, bf16[1024,384]{1,0:T(8,128)(2,1)} %get-tuple-element.42.q_ref.refs_0_, bf16[1024,384]{1,0:T(8,128)(2,1)} %back_norm.1.g_ref, bf16[4096,384]{1,0:T(8,128)(2,1)} %get-tuple-element.45.k_ref.refs_0_, ...), custom_call_target="tpu_custom_call" | custom-call | flops 25769803776 | bytes 12582912 | tf_op jit(solution)/shard_map/back_attend/pallas_call | solution.py:319
  388.4 14.5 %back_project.4 = (bf16[4096,768]{1,0:T(8,128)(2,1)}, f32[768,768]{1,0:T(8,128)}) custom-call(s32[8]{0:T(128)} %and_convert_fusion.need, bf16[4096,768]{1,0:T(8,128)(2,1)} %constant_dynamic-update-slice_fusion.12.x_ref, bf16[768,768]{1,0:T(8,128)(2,1)} %copy-done.25, bf16[4096,384]{1,0:T(8,128)(2,1)} %get-tuple-element.45.k_ref.refs_0_, ...), custom_call_target="tpu_custom_call" | custom-call | flops 9663676416 | bytes 37748736 | tf_op jit(solution)/shard_map/back_project/pallas_call | solution.py:391
  410.4 41.1 %back_attend.5 = (bf16[1024,384]{1,0:T(8,128)(2,1)}, bf16[1024,384]{1,0:T(8,128)(2,1)}, f32[384,1024]{1,0:T(8,128)}) custom-call(s32[16]{0:T(128)} %pad_add_fusion.3.table, bf16[1024,384]{1,0:T(8,128)(2,1)} %get-tuple-element.42.q_ref.refs_0_, bf16[1024,384]{1,0:T(8,128)(2,1)} %back_norm.1.g_ref, bf16[1024,384]{1,0:T(8,128)(2,1)} %get-tuple-element.47.k_ref.refs_3_, ...), custom_call_target="tpu_custom_call" | custom-call | flops 6442450944 | bytes 3145728 | tf_op jit(solution)/shard_map/back_attend/pallas_call | solution.py:319
  452.6 8.5 back_conv.1
  461.7 13.3 %back_project.5 = (bf16[1024,768]{1,0:T(8,128)(2,1)}, f32[768,1152]{1,0:T(8,128)}) custom-call(s32[2]{0:T(128)} %broadcast_45_need.2.need, bf16[1024,768]{1,0:T(8,128)(2,1)} %x_ref.3, bf16[768,1152]{1,0:T(8,128)(2,1)} %copy-done.26, bf16[1024,384]{1,0:T(8,128)(2,1)} %get-tuple-element.42.q_ref.refs_0_, f32[1024,384]{1,0:T(8,128)} %get-tuple-element.58.refs_1_, ...), custom_call_target="tpu_custom_call" | custom-call | flops 3623878656 | bytes 9437184 | tf_op jit(solution)/shard_map/back_project/pallas_call | solution.py:391
  481.3 3.8 add_convert_fusion.1
  486.6 266.7 %collective-permute-start.17 = (bf16[512,768]{1,0:T(8,128)(2,1)S(1)}, bf16[512,768]{1,0:T(8,128)(2,1)S(1)}, u32[]{:S(2)}, u32[]{:S(2)}) collective-permute-start(bf16[512,768]{1,0:T(8,128)(2,1)S(1)} %get-tuple-element.112), channel_id=1, source_target_pairs={{0,6},{2,8},{4,10},{6,12},{8,14},{10,16},{12,18},{14,20},{16,22},{... | collective-permute-start | bytes 2359304 | tf_op jit(solution)/shard_map/ppermute | solution.py:683
  754.6 5.6 collective-permute-start.19
  766.1 13.1 %collective-permute-done.16 = bf16[512,768]{1,0:T(8,128)(2,1)S(1)} collective-permute-done((bf16[512,768]{1,0:T(8,128)(2,1)S(1)}, bf16[512,768]{1,0:T(8,128)(2,1)S(1)}, u32[]{:S(2)}, u32[]{:S(2)}) %collective-permute-start.16) | collective-permute-done | bytes 786464 | tf_op jit(solution)/shard_map/ppermute | solution.py:683
  779.2 11.2 collective-permute-start.22
  790.4 4.0 collective-permute-done.17
  795.6 22.0 %collective-permute-done.18 = bf16[512,768]{1,0:T(8,128)(2,1)S(1)} collective-permute-done((bf16[512,768]{1,0:T(8,128)(2,1)S(1)}, bf16[512,768]{1,0:T(8,128)(2,1)S(1)}, u32[]{:S(2)}, u32[]{:S(2)}) %collective-permute-start.18) | collective-permute-done | bytes 786464 | tf_op jit(solution)/shard_map/ppermute | solution.py:683
  817.7 25.7 %collective-permute-start.24 = (bf16[512,768]{1,0:T(8,128)(2,1)}, bf16[512,768]{1,0:T(8,128)(2,1)}, u32[]{:S(2)}, u32[]{:S(2)}) collective-permute-start(bf16[512,768]{1,0:T(8,128)(2,1)} %get-tuple-element.114), channel_id=1, source_target_pairs={{0,4},{2,6},{4,8},{6,10},{8,12},{10,14},{12,16},{14,18},{16,20},{1... | collective-permute-start | bytes 2359304 | tf_op jit(solution)/shard_map/ppermute | solution.py:683
  844.3 20.8 %occupancy.1 = f32[6,512,128]{2,1,0:T(8,128)} custom-call(bf16[1024,384]{1,0:T(8,128)(2,1)} %get-tuple-element.47.k_ref.refs_3_, bf16[2,128,1024]{2,1,0:T(8,128)(2,1)} %pad_maximum_fusion.5.w_ref), custom_call_target="tpu_custom_call" | custom-call | flops 6291456000 | bytes 1572864 | tf_op jit(solution)/shard_map/occupancy/pallas_call | solution.py:653
  865.1 8.4 reshape.438
  873.5 5.5 convert_add_fusion
  879.0 6.7 fusion.49
  890.1 89.1 %all-reduce.4 = (f32[6,33]{1,0:T(8,128)}, f32[768]{0:T(1024)}, f32[768]{0:T(1024)}, f32[768]{0:T(1024)}, f32[768]{0:T(1024)}) all-reduce(f32[6,33]{1,0:T(8,128)S(1)} %slice.258, f32[768]{0:T(1024)S(1)} %get-tuple-element.70, f32[768]{0:T(1024)S(1)} %get-tuple-element.74, ...), channel_id=1, replica_groups=mesh['seq'=16,'tp'=2] {'seq'}, use_global_device_ids=true, to_apply=%region_15.16 | all-reduce | flops 3270 | bytes 26160 | tf_op jit(solution)/shard_map/psum | solution.py:870
  983.2 53.1 %all-reduce.11.cloned.1.call-done = (bf16[768,1152]{1,0:T(8,128)(2,1)}, bf16[3456,768]{1,0:T(8,128)(2,1)}) async-done(((bf16[768,1152]{1,0:T(8,128)(2,1)}, bf16[3456,768]{1,0:T(8,128)(2,1)}), (bf16[768,1152]{1,0:T(8,128)(2,1)}, bf16[3456,768]{1,0:T(8,128)(2,1)})) %all-reduce.11.cloned.1.call-update) | async-done | bytes 7077904 | tf_op jit(solution)/shard_map/psum | solution.py:869
  1036.3 6.8 fusion.50
  1045.3 6.1 reshape.437
  1054.9 93.2 %all-reduce.9.cloned.1.call-done = f32[6,32,256]{2,1,0:T(8,128)} async-done(((f32[6,32,256]{2,1,0:T(8,128)}), f32[6,32,256]{2,1,0:T(8,128)}) %all-reduce.9.cloned.1.call-update) | async-done | bytes 196624 | tf_op jit(solution)/shard_map/psum | solution.py:873
  (327 shorter events, 135.4 us)
Async XLA Ops:
  7.2 229.6 %copy-start = (bf16[768,1536]{1,0:T(8,128)(2,1)S(1)}, bf16[768,1536]{1,0:T(8,128)(2,1)}, u32[]{:S(2)}) copy-start(bf16[768,1536]{1,0:T(8,128)(2,1)} %param.21) | copy-start | bytes 7077892
  7.2 1029.1 %all-reduce.11.cloned.1.call-start = ((), (), s32[]{:S(2)}) async-start(), calls=%async_computation.1 | async-start | bytes 14155776 | tf_op jit(solution)/shard_map/psum | solution.py:869
  9.5 39.9 %collective-permute-start.5 = (bf16[512,768]{1,0:T(8,128)(2,1)}, bf16[512,768]{1,0:T(8,128)(2,1)}, u32[]{:S(2)}, u32[]{:S(2)}) collective-permute-start(bf16[512,768]{1,0:T(8,128)(2,1)} %constant_dynamic-slice_fusion.1), channel_id=1, source_target_pairs={{0,2},{2,4},{4,6},{6,8},{8,10},{10,12},{12,14},{14,16},{16,18},{18... | collective-permute-start | bytes 2359304 | tf_op jit(solution)/shard_map/ppermute | solution.py:683
  15.2 35.5 %collective-permute-start.6 = (bf16[512,768]{1,0:T(8,128)(2,1)}, bf16[512,768]{1,0:T(8,128)(2,1)}, u32[]{:S(2)}, u32[]{:S(2)}) collective-permute-start(bf16[512,768]{1,0:T(8,128)(2,1)} %constant_dynamic-slice_fusion.1), channel_id=1, source_target_pairs={{2,0},{4,2},{6,4},{8,6},{10,8},{12,10},{14,12},{16,14},{18,16},{20... | collective-permute-start | bytes 2359304 | tf_op jit(solution)/shard_map/ppermute | solution.py:683
  16.5 73.3 %collective-permute-start.7 = (bf16[512,768]{1,0:T(8,128)(2,1)}, bf16[512,768]{1,0:T(8,128)(2,1)}, u32[]{:S(2)}, u32[]{:S(2)}) collective-permute-start(bf16[512,768]{1,0:T(8,128)(2,1)} %constant_dynamic-slice_fusion.1), channel_id=1, source_target_pairs={{0,4},{2,6},{4,8},{6,10},{8,12},{10,14},{12,16},{14,18},{16,20},{1... | collective-permute-start | bytes 2359304 | tf_op jit(solution)/shard_map/ppermute | solution.py:683
  22.0 71.8 %collective-permute-start.8 = (bf16[512,768]{1,0:T(8,128)(2,1)}, bf16[512,768]{1,0:T(8,128)(2,1)}, u32[]{:S(2)}, u32[]{:S(2)}) collective-permute-start(bf16[512,768]{1,0:T(8,128)(2,1)} %constant_dynamic-slice_fusion.1), channel_id=1, source_target_pairs={{4,0},{6,2},{8,4},{10,6},{12,8},{14,10},{16,12},{18,14},{20,16},{2... | collective-permute-start | bytes 2359304 | tf_op jit(solution)/shard_map/ppermute | solution.py:683
  23.3 75.1 %collective-permute-start = (bf16[512,768]{1,0:T(8,128)(2,1)}, bf16[512,768]{1,0:T(8,128)(2,1)}, u32[]{:S(2)}, u32[]{:S(2)}) collective-permute-start(bf16[512,768]{1,0:T(8,128)(2,1)} %constant_dynamic-slice_fusion.1), channel_id=1, source_target_pairs={{0,6},{2,8},{4,10},{6,12},{8,14},{10,16},{12,18},{14,20},{16,22},{... | collective-permute-start | bytes 2359304 | tf_op jit(solution)/shard_map/ppermute | solution.py:683
  29.9 61.2 %copy-start.36 = (s32[4]{0:T(128)}, s32[4]{0:T(128)S(1)}, u32[]{:S(2)}) copy-start(s32[4]{0:T(128)S(1)} %slice.214) | copy-start | bytes 52
  30.0 61.1 %copy-start.38 = (s32[4]{0:T(128)}, s32[4]{0:T(128)S(1)}, u32[]{:S(2)}) copy-start(s32[4]{0:T(128)S(1)} %slice.215) | copy-start | bytes 52
  49.4 59.1 %collective-permute-start.1 = (bf16[512,768]{1,0:T(8,128)(2,1)}, bf16[512,768]{1,0:T(8,128)(2,1)}, u32[]{:S(2)}, u32[]{:S(2)}) collective-permute-start(bf16[512,768]{1,0:T(8,128)(2,1)} %constant_dynamic-slice_fusion.1), channel_id=1, source_target_pairs={{6,0},{8,2},{10,4},{12,6},{14,8},{16,10},{18,12},{20,14},{22,16},{... | collective-permute-start | bytes 2359304 | tf_op jit(solution)/shard_map/ppermute | solution.py:683
  50.7 59.3 %collective-permute-start.2 = (bf16[512,768]{1,0:T(8,128)(2,1)}, bf16[512,768]{1,0:T(8,128)(2,1)}, u32[]{:S(2)}, u32[]{:S(2)}) collective-permute-start(bf16[512,768]{1,0:T(8,128)(2,1)} %constant_dynamic-slice_fusion.1), channel_id=1, source_target_pairs={{0,8},{2,10},{4,12},{6,14},{8,16},{10,18},{12,20},{14,22},{16,24},... | collective-permute-start | bytes 2359304 | tf_op jit(solution)/shard_map/ppermute | solution.py:683
  89.8 20.3 %collective-permute-start.3 = (bf16[512,768]{1,0:T(8,128)(2,1)}, bf16[512,768]{1,0:T(8,128)(2,1)}, u32[]{:S(2)}, u32[]{:S(2)}) collective-permute-start(bf16[512,768]{1,0:T(8,128)(2,1)} %constant_dynamic-slice_fusion.1), channel_id=1, source_target_pairs={{8,0},{10,2},{12,4},{14,6},{16,8},{18,10},{20,12},{22,14},{24,16},... | collective-permute-start | bytes 2359304 | tf_op jit(solution)/shard_map/ppermute | solution.py:683
  97.0 68.0 %collective-permute-start.9 = (bf16[2048,768]{1,0:T(8,128)(2,1)}, bf16[2048,768]{1,0:T(8,128)(2,1)}, u32[]{:S(2)}, u32[]{:S(2)}) collective-permute-start(bf16[2048,768]{1,0:T(8,128)(2,1)} %pad_maximum_fusion.2), channel_id=1, source_target_pairs={{0,1},{1,0},{2,3},{3,2},{4,5},{5,4},{6,7},{7,6},{8,9},{9,8},{10,11... | collective-permute-start | bytes 9437192 | tf_op jit(solution)/shard_map/ppermute | solution.py:687
  98.3 48.2 %collective-permute-start.10 = (bf16[16,384]{1,0:T(8,128)(2,1)S(1)}, bf16[16,384]{1,0:T(8,128)(2,1)S(1)}, u32[]{:S(2)}, u32[]{:S(2)}) collective-permute-start(bf16[16,384]{1,0:T(8,128)(2,1)S(1)} %get-tuple-element.123), channel_id=1, source_target_pairs={{0,2},{2,4},{4,6},{6,8},{8,10},{10,12},{12,14},{14,16},{16,18},{18... | collective-permute-start | bytes 36872 | tf_op jit(solution)/shard_map/ppermute | solution.py:683
  108.5 39.4 %collective-permute-start.11 = (bf16[16,384]{1,0:T(8,128)(2,1)S(1)}, bf16[16,384]{1,0:T(8,128)(2,1)S(1)}, u32[]{:S(2)}, u32[]{:S(2)}) collective-permute-start(bf16[16,384]{1,0:T(8,128)(2,1)S(1)} %get-tuple-element.122), channel_id=1, source_target_pairs={{2,0},{4,2},{6,4},{8,6},{10,8},{12,10},{14,12},{16,14},{18,16},{20... | collective-permute-start | bytes 36872 | tf_op jit(solution)/shard_map/ppermute | solution.py:683
  113.3 68.7 %collective-permute-start.4 = (bf16[2048,768]{1,0:T(8,128)(2,1)}, bf16[2048,768]{1,0:T(8,128)(2,1)}, u32[]{:S(2)}, u32[]{:S(2)}) collective-permute-start(bf16[2048,768]{1,0:T(8,128)(2,1)} %pad_maximum_fusion.1), channel_id=1, source_target_pairs={{0,1},{1,0},{2,3},{3,2},{4,5},{5,4},{6,7},{7,6},{8,9},{9,8},{10,11... | collective-permute-start | bytes 9437192 | tf_op jit(solution)/shard_map/ppermute | solution.py:687
  115.6 29.0 %copy-start.37 = (s32[4]{0:T(128)S(1)}, s32[4]{0:T(128)}, u32[]{:S(2)}) copy-start(s32[4]{0:T(128)} %copy-done.36) | copy-start | bytes 52
  115.6 29.0 %copy-start.39 = (s32[4]{0:T(128)S(1)}, s32[4]{0:T(128)}, u32[]{:S(2)}) copy-start(s32[4]{0:T(128)} %copy-done.38) | copy-start | bytes 52
  115.6 29.0 %copy-start.40 = (s32[16]{0:T(128)S(1)}, s32[16]{0:T(128)}, u32[]{:S(2)}) copy-start(s32[16]{0:T(128)} %slice.217) | copy-start | bytes 196
  115.6 29.0 %copy-start.41 = (s32[16]{0:T(128)S(1)}, s32[16]{0:T(128)}, u32[]{:S(2)}) copy-start(s32[16]{0:T(128)} %slice.218) | copy-start | bytes 196
  115.6 29.0 %copy-start.42 = (s32[16]{0:T(128)S(1)}, s32[16]{0:T(128)}, u32[]{:S(2)}) copy-start(s32[16]{0:T(128)} %slice.219) | copy-start | bytes 196
  115.6 29.6 %copy-start.32 = (f32[6,33]{1,0:T(8,128)S(1)}, f32[6,33]{1,0:T(8,128)}, u32[]{:S(2)}) copy-start(f32[6,33]{1,0:T(8,128)} %param.23) | copy-start | bytes 2380
  232.0 3.6 collective-permute-start.12
  258.5 3.8 collective-permute-start.13
  286.3 19.6 %collective-permute-start.14 = (bf16[1024,768]{1,0:T(8,128)(2,1)}, bf16[1024,768]{1,0:T(8,128)(2,1)}, u32[]{:S(2)}, u32[]{:S(2)}) collective-permute-start(bf16[1024,768]{1,0:T(8,128)(2,1)} %convolution_convert_fusion.3), channel_id=1, source_target_pairs={{0,1},{1,0},{2,3},{3,2},{4,5},{5,4},{6,7},{7,6},{8,9},{9,8},{10,11... | collective-permute-start | bytes 4718600 | tf_op jit(solution)/shard_map/ppermute | solution.py:687
  318.7 132.8 %collective-permute-start.25 = (bf16[16,384]{1,0:T(8,128)(2,1)S(1)}, bf16[16,384]{1,0:T(8,128)(2,1)S(1)}, u32[]{:S(2)}, u32[]{:S(2)}) collective-permute-start(bf16[16,384]{1,0:T(8,128)(2,1)S(1)} %get-tuple-element.121), channel_id=1, source_target_pairs={{0,2},{2,4},{4,6},{6,8},{8,10},{10,12},{12,14},{14,16},{16,18},{18... | collective-permute-start | bytes 36872 | tf_op jit(solution)/shard_map/ppermute | solution.py:683
  333.0 118.7 %collective-permute-start.26 = (bf16[16,384]{1,0:T(8,128)(2,1)S(1)}, bf16[16,384]{1,0:T(8,128)(2,1)S(1)}, u32[]{:S(2)}, u32[]{:S(2)}) collective-permute-start(bf16[16,384]{1,0:T(8,128)(2,1)S(1)} %get-tuple-element.120), channel_id=1, source_target_pairs={{2,0},{4,2},{6,4},{8,6},{10,8},{12,10},{14,12},{16,14},{18,16},{20... | collective-permute-start | bytes 36872 | tf_op jit(solution)/shard_map/ppermute | solution.py:683
  365.4 115.8 %collective-permute-start.15 = (bf16[2048,768]{1,0:T(8,128)(2,1)}, bf16[2048,768]{1,0:T(8,128)(2,1)}, u32[]{:S(2)}, u32[]{:S(2)}) collective-permute-start(bf16[2048,768]{1,0:T(8,128)(2,1)} %slice.235), channel_id=1, source_target_pairs={{0,1},{1,0},{2,3},{3,2},{4,5},{5,4},{6,7},{7,6},{8,9},{9,8},{10,11... | collective-permute-start | bytes 9437192 | tf_op jit(solution)/shard_map/ppermute | solution.py:687
  406.6 348.0 %collective-permute-start.20 = (bf16[2048,768]{1,0:T(8,128)(2,1)}, bf16[2048,768]{1,0:T(8,128)(2,1)}, u32[]{:S(2)}, u32[]{:S(2)}) collective-permute-start(bf16[2048,768]{1,0:T(8,128)(2,1)} %slice.243), channel_id=1, source_target_pairs={{0,1},{1,0},{2,3},{3,2},{4,5},{5,4},{6,7},{7,6},{8,9},{9,8},{10,11... | collective-permute-start | bytes 9437192 | tf_op jit(solution)/shard_map/ppermute | solution.py:687
  410.4 41.1 %copy-start.8 = (bf16[1024,384]{1,0:T(8,128)(2,1)S(1)}, bf16[1024,384]{1,0:T(8,128)(2,1)}, u32[]{:S(2)}) copy-start(bf16[1024,384]{1,0:T(8,128)(2,1)} %copy-done.7) | copy-start | bytes 2359300
  479.7 668.3 %all-reduce.9.cloned.1.call-start = ((), (), s32[]{:S(2)}) async-start(), calls=%async_computation | async-start | bytes 393216 | tf_op jit(solution)/shard_map/psum | solution.py:873
  481.1 279.1 %slice-start = ((s8[6291456]{0:T(1024)(128)(4,1)}), s8[4194304]{0:T(1024)(128)(4,1)S(1)}, s32[]{:S(2)}) async-start(s8[6291456]{0:T(1024)(128)(4,1)} %bitcast.83), calls=%async_computation.2 | async-start | bytes 8388608
  481.2 279.1 %slice-start.1 = ((s8[6291456]{0:T(1024)(128)(4,1)}), s8[2097152]{0:T(1024)(128)(4,1)S(1)}, s32[]{:S(2)}) async-start(s8[6291456]{0:T(1024)(128)(4,1)} %bitcast.83), calls=%async_computation.3 | async-start | bytes 4194304
  481.2 283.6 %collective-permute-start.27 = (bf16[512,768]{1,0:T(8,128)(2,1)S(1)}, bf16[512,768]{1,0:T(8,128)(2,1)S(1)}, u32[]{:S(2)}, u32[]{:S(2)}) collective-permute-start(bf16[512,768]{1,0:T(8,128)(2,1)S(1)} %constant_dynamic-slice_fusion), channel_id=1, source_target_pairs={{0,1},{1,0},{2,3},{3,2},{4,5},{5,4},{6,7},{7,6},{8,9},{9,8},{10,11... | collective-permute-start | bytes 2359304 | tf_op jit(solution)/shard_map/ppermute | solution.py:687
  485.3 294.0 %collective-permute-start.16 = (bf16[512,768]{1,0:T(8,128)(2,1)S(1)}, bf16[512,768]{1,0:T(8,128)(2,1)S(1)}, u32[]{:S(2)}, u32[]{:S(2)}) collective-permute-start(bf16[512,768]{1,0:T(8,128)(2,1)S(1)} %get-tuple-element.109), channel_id=1, source_target_pairs={{6,0},{8,2},{10,4},{12,6},{14,8},{16,10},{18,12},{20,14},{22,16},{... | collective-permute-start | bytes 2359304 | tf_op jit(solution)/shard_map/ppermute | solution.py:683
  486.6 307.8 %collective-permute-start.17 = (bf16[512,768]{1,0:T(8,128)(2,1)S(1)}, bf16[512,768]{1,0:T(8,128)(2,1)S(1)}, u32[]{:S(2)}, u32[]{:S(2)}) collective-permute-start(bf16[512,768]{1,0:T(8,128)(2,1)S(1)} %get-tuple-element.112), channel_id=1, source_target_pairs={{0,6},{2,8},{4,10},{6,12},{8,14},{10,16},{12,18},{14,20},{16,22},{... | collective-permute-start | bytes 2359304 | tf_op jit(solution)/shard_map/ppermute | solution.py:683
  753.3 64.4 %collective-permute-start.18 = (bf16[512,768]{1,0:T(8,128)(2,1)S(1)}, bf16[512,768]{1,0:T(8,128)(2,1)S(1)}, u32[]{:S(2)}, u32[]{:S(2)}) collective-permute-start(bf16[512,768]{1,0:T(8,128)(2,1)S(1)} %get-tuple-element.111), channel_id=1, source_target_pairs={{8,0},{10,2},{12,4},{14,6},{16,8},{18,10},{20,12},{22,14},{24,16},... | collective-permute-start | bytes 2359304 | tf_op jit(solution)/shard_map/ppermute | solution.py:683
  754.6 118.9 %collective-permute-start.19 = (bf16[512,768]{1,0:T(8,128)(2,1)S(1)}, bf16[512,768]{1,0:T(8,128)(2,1)}, u32[]{:S(2)}, u32[]{:S(2)}) collective-permute-start(bf16[512,768]{1,0:T(8,128)(2,1)S(1)} %get-tuple-element.110), channel_id=1, source_target_pairs={{0,8},{2,10},{4,12},{6,14},{8,16},{10,18},{12,20},{14,22},{16,24},... | collective-permute-start | bytes 2359304 | tf_op jit(solution)/shard_map/ppermute | solution.py:683
  764.8 52.9 %copy-start.17 = (bf16[512,768]{1,0:T(8,128)(2,1)}, bf16[512,768]{1,0:T(8,128)(2,1)S(1)}, u32[]{:S(2)}) copy-start(bf16[512,768]{1,0:T(8,128)(2,1)S(1)} %collective-permute-done.27) | copy-start | bytes 2359300
  764.8 108.6 %collective-permute-start.21 = (bf16[512,768]{1,0:T(8,128)(2,1)}, bf16[512,768]{1,0:T(8,128)(2,1)}, u32[]{:S(2)}, u32[]{:S(2)}) collective-permute-start(bf16[512,768]{1,0:T(8,128)(2,1)} %get-tuple-element.113), channel_id=1, source_target_pairs={{2,0},{4,2},{6,4},{8,6},{10,8},{12,10},{14,12},{16,14},{18,16},{20... | collective-permute-start | bytes 2359304 | tf_op jit(solution)/shard_map/ppermute | solution.py:683
  779.2 64.1 %copy-start.19 = (bf16[512,768]{1,0:T(8,128)(2,1)}, bf16[512,768]{1,0:T(8,128)(2,1)S(1)}, u32[]{:S(2)}) copy-start(bf16[512,768]{1,0:T(8,128)(2,1)S(1)} %collective-permute-done.16) | copy-start | bytes 2359300
  779.2 94.2 %collective-permute-start.22 = (bf16[512,768]{1,0:T(8,128)(2,1)}, bf16[512,768]{1,0:T(8,128)(2,1)}, u32[]{:S(2)}, u32[]{:S(2)}) collective-permute-start(bf16[512,768]{1,0:T(8,128)(2,1)} %get-tuple-element.116), channel_id=1, source_target_pairs={{0,2},{2,4},{4,6},{6,8},{8,10},{10,12},{12,14},{14,16},{16,18},{18... | collective-permute-start | bytes 2359304 | tf_op jit(solution)/shard_map/ppermute | solution.py:683
  794.3 49.1 %copy-start.20 = (bf16[512,768]{1,0:T(8,128)(2,1)}, bf16[512,768]{1,0:T(8,128)(2,1)S(1)}, u32[]{:S(2)}) copy-start(bf16[512,768]{1,0:T(8,128)(2,1)S(1)} %collective-permute-done.17) | copy-start | bytes 2359300
  794.3 79.1 %collective-permute-start.23 = (bf16[512,768]{1,0:T(8,128)(2,1)}, bf16[512,768]{1,0:T(8,128)(2,1)}, u32[]{:S(2)}, u32[]{:S(2)}) collective-permute-start(bf16[512,768]{1,0:T(8,128)(2,1)} %get-tuple-element.115), channel_id=1, source_target_pairs={{4,0},{6,2},{8,4},{10,6},{12,8},{14,10},{16,12},{18,14},{20,16},{2... | collective-permute-start | bytes 2359304 | tf_op jit(solution)/shard_map/ppermute | solution.py:683
  817.7 25.8 %copy-start.21 = (bf16[512,768]{1,0:T(8,128)(2,1)}, bf16[512,768]{1,0:T(8,128)(2,1)S(1)}, u32[]{:S(2)}) copy-start(bf16[512,768]{1,0:T(8,128)(2,1)S(1)} %collective-permute-done.18) | copy-start | bytes 2359300
  817.7 55.8 %collective-permute-start.24 = (bf16[512,768]{1,0:T(8,128)(2,1)}, bf16[512,768]{1,0:T(8,128)(2,1)}, u32[]{:S(2)}, u32[]{:S(2)}) collective-permute-start(bf16[512,768]{1,0:T(8,128)(2,1)} %get-tuple-element.114), channel_id=1, source_target_pairs={{0,4},{2,6},{4,8},{6,10},{8,12},{10,14},{12,16},{14,18},{16,20},{1... | collective-permute-start | bytes 2359304 | tf_op jit(solution)/shard_map/ppermute | solution.py:683
  879.0 100.3 %collective-permute-start.28 = (f32[512,768]{1,0:T(8,128)}, f32[512,768]{1,0:T(8,128)}, u32[]{:S(2)}, u32[]{:S(2)}) collective-permute-start(f32[512,768]{1,0:T(8,128)} %convert_add_fusion), channel_id=1, source_target_pairs={{0,1},{1,0},{2,3},{3,2},{4,5},{5,4},{6,7},{7,6},{8,9},{9,8},{10,11... | collective-permute-start | bytes 4718600 | tf_op jit(solution)/shard_map/ppermute | solution.py:687
  1051.4 98.3 %copy-start.1 = (bf16[768,1536]{1,0:T(8,128)(2,1)S(1)}, bf16[768,1536]{1,0:T(8,128)(2,1)}, u32[]{:S(2)}) copy-start(bf16[768,1536]{1,0:T(8,128)(2,1)} %param.21) | copy-start | bytes 7077892
  (34 other events, 189.6 us)
Sparse Core Ops, SparseCore 0:
  479.8 556.4 all-reduce.10
  1042.2 105.8 all-reduce.8

commit v2 on v1

v2 whole, which is shorter than its diff:
```python
from functools import partial
import math

import jax
import jax.numpy as jnp
from jax import lax
from jax.experimental import pallas as pl
from jax.experimental.pallas import tpu as pltpu
from jax.sharding import PartitionSpec as P

TAU = 8
BITS = 8
CONV = 33
MOST = 4096
RIM = (CONV - 1) // 2

EPS_UNIT = 1e-06
EPS_LAYER = 1e-05
SHARP = 4.0
CLIP_EDGE = 0.999

CHUNK = 512
Q_TILE = 512
Q_TILE_BACK = 256
PAIR = 128
STRIP = 128
FAR_ID = 1 << 20

LIGHT = pl.CostEstimate(flops=1 << 20, bytes_accessed=1 << 16, transcendentals=0)

F32 = jnp.float32
BF16 = jnp.bfloat16

ARC = (
    0.49999961256980896,
    -0.06828052550554276,
    0.027964841574430466,
    -0.014291195198893547,
    0.006136968266218901,
    -0.001371906721033156,
)


def params(**kwargs):
    return pltpu.CompilerParams(vmem_limit_bytes=56 << 20, **kwargs)


def nn(left, right):
    return lax.dot_general(left, right, (((1,), (0,)), ((), ())), preferred_element_type=F32)


def nt(left, right):
    return lax.dot_general(left, right, (((1,), (1,)), ((), ())), preferred_element_type=F32)


def tn(left, right):
    return lax.dot_general(left, right, (((0,), (0,)), ((), ())), preferred_element_type=F32)


def head_masks(head_dim):
    lanes = lax.broadcasted_iota(jnp.int32, (1, PAIR), 1)
    first = (lanes < head_dim).astype(F32)
    return first.astype(BF16), (1.0 - first).astype(BF16)


def head_sum(rows, head_dim):
    here = lax.broadcasted_iota(jnp.int32, (PAIR, PAIR), 0) // head_dim
    there = lax.broadcasted_iota(jnp.int32, (PAIR, PAIR), 1) // head_dim
    ones = (here == there).astype(F32).astype(BF16)
    sums = []
    for start in range(0, rows.shape[1], PAIR):
        part = rows[:, start : start + PAIR]
        high = part.astype(BF16)
        low = (part - high.astype(F32)).astype(BF16)
        sums.append(nn(high, ones) + nn(low, ones))
    return jnp.concatenate(sums, axis=1)


def pick_half(mine_refs, other_ref, kept):
    step = pl.program_id(0)
    for index, ref in enumerate(mine_refs):

        @pl.when(step == index)
        def _():
            kept[...] = ref[...]

    @pl.when(step >= len(mine_refs))
    def _():
        kept[...] = other_ref[...]


def other_spec(count, shape):
    return pl.BlockSpec(shape, lambda i, t: (jnp.maximum(i - count, 0), 0))


def half_specs(count, shape):
    return [pl.BlockSpec(shape, lambda i, t: (0, 0))] * count + [other_spec(count, shape)]


def project_kernel(units, count, head_dim, table, *refs):
    if count:
        mine_refs, other_ref, w_ref = refs[:count], refs[count], refs[count + 1]
        out_refs, kept = refs[count + 2 : -1], refs[-1]
        pick_half(mine_refs, other_ref, kept)
    else:
        kept, w_ref = refs[:2]
        out_refs = refs[2:]
    width = out_refs[-1].shape[1]
    needed = table[pl.num_programs(0) + pl.program_id(0)] > 0

    @pl.when(needed)
    def _():
        whole = nn(kept[...], w_ref[...])
        for index in range(units):
            part = whole[:, index * width : (index + 1) * width]
            scale = lax.rsqrt(head_sum(part * part, head_dim) * (1.0 / head_dim) + EPS_UNIT)
            scale = scale * (1.0 / math.sqrt(head_dim))
            out_refs[2 * index][...] = (part * scale).astype(BF16)
            out_refs[2 * index + 1][...] = scale
        out_refs[-1][...] = whole[:, units * width :].astype(BF16)


def project(table, halves, weight, units, head_dim):
    depth = halves[0].shape[1]
    rows = sum(h.shape[0] for h in halves)
    count = len(halves) - 1
    width = weight.shape[1] // (units + 1)
    row_spec = pl.BlockSpec((CHUNK, width), lambda i, t: (t[i], 0))
    spare = CHUNK if count else 0
    if count:
        x_specs = half_specs(count, (CHUNK, depth))
    else:
        x_specs = [pl.BlockSpec((CHUNK, depth), lambda i, t: (i, 0))]
    unit_shapes = [
        jax.ShapeDtypeStruct((rows + spare, width), BF16),
        jax.ShapeDtypeStruct((rows + spare, width), F32),
    ]
    return pl.pallas_call(
        partial(project_kernel, units, count, head_dim),
        grid_spec=pltpu.PrefetchScalarGridSpec(
            num_scalar_prefetch=1,
            grid=(rows // CHUNK,),
            in_specs=x_specs + [pl.BlockSpec(weight.shape, lambda i, t: (0, 0))],
            out_specs=[row_spec] * (2 * units + 1),
            scratch_shapes=[pltpu.VMEM((CHUNK, depth), BF16)] if count else [],
        ),
        out_shape=unit_shapes * units + [jax.ShapeDtypeStruct((rows + spare, width), BF16)],
        compiler_params=params(),
        cost_estimate=pl.CostEstimate(
            flops=4 * rows * depth * weight.shape[1], bytes_accessed=rows * depth, transcendentals=0
        ),
        name="project",
    )(table, *halves, weight)


def collide_parts(scores):
    size = jnp.minimum(jnp.abs(scores), CLIP_EDGE)
    rest = 1.0 - size
    root = lax.rsqrt(rest)
    poly = ARC[5]
    for factor in ARC[4::-1]:
        poly = poly * size + factor
    angle = (rest * root) * poly
    return size, root, jnp.where(scores < 0.0, angle, 1.0 - angle)


def tile_facts(table, tiles_q, tiles_k, qi, kt, base):
    q_low, q_high = table[qi], table[tiles_q + qi]
    k_low, k_high = table[base + kt], table[base + tiles_k + kt]
    needed = (k_high >= q_low) & (k_low <= q_high)
    whole = (q_low == q_high) & (k_low == k_high)
    return needed, whole


def id_column(row, lanes):
    column = jnp.broadcast_to(row, (PAIR, row.shape[1])).T
    return jnp.concatenate([column] * (lanes // PAIR), axis=1)


def attend_kernel(head_dim, groups, seeded, table, q_ref, qrow_ref, *rest):
    out_ref = rest[-1]
    tiles_q = q_ref.shape[0] // Q_TILE
    masks = head_masks(head_dim)
    if seeded:
        out_ref[...] = rest[-2][...]
    else:
        out_ref[...] = jnp.zeros_like(out_ref)

    base = 2 * tiles_q
    for group in range(groups):
        k_ref, v_ref, krow_ref = rest[3 * group : 3 * group + 3]
        tiles_k = k_ref.shape[0] // CHUNK
        attend_group(
            head_dim, masks, base, tiles_q, tiles_k, table, q_ref, qrow_ref, k_ref, v_ref, krow_ref, out_ref
        )
        base += 2 * tiles_k


def attend_group(
    head_dim, masks, base, tiles_q, tiles_k, table, q_ref, qrow_ref, k_ref, v_ref, krow_ref, out_ref
):
    def q_loop(qi, carry):
        rows = pl.ds(pl.multiple_of(qi * Q_TILE, Q_TILE), Q_TILE)

        def k_loop(kt, inner):
            needed, whole = tile_facts(table, tiles_q, tiles_k, qi, kt, base)

            def part(same):
                cols = pl.ds(pl.multiple_of(kt * CHUNK, CHUNK), CHUNK)
                q, k, v = q_ref[rows, :], k_ref[cols, :], v_ref[cols, :]
                total = None
                for mask in masks:
                    chance = collide_parts(nt(q * mask, k))[2]
                    chance = chance * chance
                    chance = chance * chance
                    chance = chance * chance
                    if same is not None:
                        chance = jnp.where(same, chance, 0.0)
                    term = nn(chance.astype(BF16), v * mask)
                    total = term if total is None else total + term
                out_ref[rows, :] += total

            @pl.when(needed & whole)
            def _():
                part(None)

            @pl.when(needed & jnp.logical_not(whole))
            def _():
                part(id_column(qrow_ref[pl.ds(qi, 1), :], CHUNK) == krow_ref[pl.ds(kt, 1), :])

            return inner

        return lax.fori_loop(0, tiles_k, k_loop, carry)

    lax.fori_loop(0, tiles_q, q_loop, 0)


def attend(table, q, own_ids, sources, head_dim, seed=None):
    tokens, width = q.shape
    q_spec = pl.BlockSpec((tokens, PAIR), lambda p, t: (0, p))
    qrow = own_ids.reshape(-1, Q_TILE)
    operands = [q, qrow]
    specs = [q_spec, pl.BlockSpec(qrow.shape, lambda p, t: (0, 0))]
    rows = 0
    for k, v, ids in sources:
        krow = ids.reshape(-1, CHUNK)
        k_spec = pl.BlockSpec((ids.shape[0], PAIR), lambda p, t: (0, p))
        operands += [k, v, krow]
        specs += [k_spec, k_spec, pl.BlockSpec(krow.shape, lambda p, t: (0, 0))]
        rows += ids.shape[0]
    if seed is not None:
        operands.append(seed)
        specs.append(q_spec)
    return pl.pallas_call(
        partial(attend_kernel, head_dim, len(sources), seed is not None),
        grid_spec=pltpu.PrefetchScalarGridSpec(
            num_scalar_prefetch=1, grid=(width // PAIR,), in_specs=specs, out_specs=q_spec
        ),
        out_shape=jax.ShapeDtypeStruct((tokens, width), F32),
        compiler_params=params(),
        cost_estimate=pl.CostEstimate(
            flops=32 * tokens * rows * width, bytes_accessed=rows * width * 4, transcendentals=0
        ),
        name="attend",
    )(table, *operands)


def back_attend_kernel(
    head_dim, seeded, table, q_ref, g_ref, k_ref, v_ref, qrow_ref, krow_ref, *rest
):
    dk_ref, dv_ref, dq_ref, acc_k, acc_v = rest[-5:]
    tiles_q, tiles_k = q_ref.shape[0] // Q_TILE_BACK, k_ref.shape[0] // CHUNK
    masks = head_masks(head_dim)
    if seeded:
        dq_ref[...] = rest[0][...]
    else:
        dq_ref[...] = jnp.zeros_like(dq_ref)

    def k_loop(kt, carry):
        cols = pl.ds(pl.multiple_of(kt * CHUNK, CHUNK), CHUNK)
        low, high = table[0], table[2 * tiles_q - 1]
        touched = (table[2 * tiles_q + tiles_k + kt] >= low) & (table[2 * tiles_q + kt] <= high)

        def q_loop(qi, inner):
            needed, whole = tile_facts(table, tiles_q, tiles_k, qi, kt, 2 * tiles_q)

            def part(same):
                rows = pl.ds(pl.multiple_of(qi * Q_TILE_BACK, Q_TILE_BACK), Q_TILE_BACK)
                q, g, k, v = q_ref[rows, :], g_ref[rows, :], k_ref[cols, :], v_ref[cols, :]
                k_turned = k.T
                sum_k, sum_v = None, None
                for index, mask in enumerate(masks):
                    q_half, g_half = q * mask, g * mask
                    scores = nt(k, q_half)
                    size, root, chance = collide_parts(scores)
                    second = chance * chance
                    fourth = second * second
                    weights = fourth * fourth
                    slope = (fourth * second) * (chance * (root * lax.rsqrt(1.0 + size)))
                    inside = jnp.abs(scores) <= CLIP_EDGE
                    if same is not None:
                        inside = inside & same
                        weights = jnp.where(same, weights, 0.0)
                    slope = jnp.where(inside, nt(v, g_half) * slope, 0.0).astype(BF16)
                    term_v = nn(weights.astype(BF16), g_half)
                    term_k = nn(slope, q_half)
                    sum_v = term_v if sum_v is None else sum_v + term_v
                    sum_k = term_k if sum_k is None else sum_k + term_k
                    half = slice(index * head_dim, (index + 1) * head_dim)
                    dq_ref[half, rows] += nn(k_turned[half, :], slope)
                acc_v[...] += sum_v
                acc_k[...] += sum_k

            @pl.when(needed & whole)
            def _():
                part(None)

            @pl.when(needed & jnp.logical_not(whole))
            def _():
                ids = id_column(krow_ref[pl.ds(kt, 1), :], Q_TILE_BACK)
                part(ids == qrow_ref[pl.ds(qi, 1), :])

            return inner

        @pl.when(touched)
        def _():
            acc_k[...] = jnp.zeros_like(acc_k)
            acc_v[...] = jnp.zeros_like(acc_v)
            lax.fori_loop(0, tiles_q, q_loop, 0)
            dk_ref[cols, :] = acc_k[...].astype(BF16)
            dv_ref[cols, :] = acc_v[...].astype(BF16)

        @pl.when(jnp.logical_not(touched))
        def _():
            dk_ref[cols, :] = jnp.zeros((CHUNK, PAIR), BF16)
            dv_ref[cols, :] = jnp.zeros((CHUNK, PAIR), BF16)

        return carry

    lax.fori_loop(0, tiles_k, k_loop, 0)


def back_attend(table, q, g, k, v, own_ids, key_ids, head_dim, seed=None, cost=LIGHT):
    tokens, width = q.shape
    far = key_ids.shape[0]
    qrow, krow = own_ids.reshape(-1, Q_TILE_BACK), key_ids.reshape(-1, CHUNK)
    q_spec = pl.BlockSpec((tokens, PAIR), lambda p, t: (0, p))
    k_spec = pl.BlockSpec((far, PAIR), lambda p, t: (0, p))
    dq_spec = pl.BlockSpec((PAIR, tokens), lambda p, t: (p, 0))
    specs = [
        q_spec,
        q_spec,
        k_spec,
        k_spec,
        pl.BlockSpec(qrow.shape, lambda p, t: (0, 0)),
        pl.BlockSpec(krow.shape, lambda p, t: (0, 0)),
    ]
    operands = [q, g, k, v, qrow, krow]
    if seed is not None:
        operands.append(seed)
        specs.append(dq_spec)
    return pl.pallas_call(
        partial(back_attend_kernel, head_dim, seed is not None),
        grid_spec=pltpu.PrefetchScalarGridSpec(
            num_scalar_prefetch=1,
            grid=(width // PAIR,),
            in_specs=specs,
            out_specs=[k_spec, k_spec, dq_spec],
            scratch_shapes=[pltpu.VMEM((CHUNK, PAIR), F32), pltpu.VMEM((CHUNK, PAIR), F32)],
        ),
        out_shape=[
            jax.ShapeDtypeStruct((far, width), BF16),
            jax.ShapeDtypeStruct((far, width), BF16),
            jax.ShapeDtypeStruct((width, tokens), F32),
        ],
        compiler_params=params(),
        cost_estimate=cost,
        name="back_attend",
    )(table, *operands)


def back_project_kernel(units, turned, terms, rims, count, head_dim, table, *refs):
    mine_refs, other_ref, w_ref = refs[:count], refs[count], refs[count + 1]
    dx_mine, dx_other, dw_ref, kept, sum_ref = refs[-5:]
    refs = refs[count + 2 : -5]
    step = pl.program_id(0)
    place, needed = table[step], table[pl.num_programs(0) + step] > 0

    @pl.when(step == 0)
    def _():
        dw_ref[...] = jnp.zeros_like(dw_ref)

    def store(value):
        @pl.when(step < count)
        def _():
            dx_mine[...] = value

        @pl.when(step >= count)
        def _():
            dx_other[...] = value

    @pl.when(needed)
    def _():
        pick_half(mine_refs, other_ref, kept)
        grads = []
        for index in range(units):
            unit_ref, scale_ref, grad_ref = refs[3 * index : 3 * index + 3]
            grad = grad_ref[...].astype(F32)
            if index < turned:
                grad = grad.T
            unit = unit_ref[...].astype(F32)
            inner = head_sum(grad * unit, head_dim)
            grads.append(
                ((TAU / math.pi) * scale_ref[...] * (grad - unit * inner)).astype(BF16)
            )
        value_refs = refs[3 * units : 3 * units + terms]
        value = value_refs[0][...].astype(F32)
        for extra in value_refs[1:]:
            value = value + extra[...].astype(F32)
        if rims is not None:
            rim_ref = refs[-1]
            sum_ref[...] = value

            @pl.when(place == rims)
            def _():
                sum_ref[CHUNK - STRIP :, :] += rim_ref[:STRIP, :]

            @pl.when(place == rims + 1)
            def _():
                sum_ref[:STRIP, :] += rim_ref[STRIP:, :]

            value = sum_ref[...]
        grads.append(value.astype(BF16))
        joined = jnp.concatenate(grads, axis=1)
        store(nt(joined, w_ref[...]).astype(BF16))
        dw_ref[...] += tn(kept[...], joined)

    @pl.when(jnp.logical_not(needed))
    def _():
        store(jnp.zeros(dx_mine.shape, BF16))


def back_project(table, halves, weight, parts, turned, values, head_dim, rims=None, rim=None):
    depth = halves[0].shape[1]
    count = len(halves) - 1
    width = values[0].shape[1]
    row_spec = pl.BlockSpec((CHUNK, width), lambda i, t: (t[4 * count + i], 0))
    weight_spec = pl.BlockSpec(weight.shape, lambda i, t: (0, 0))
    wide_specs = [
        pl.BlockSpec((CHUNK, depth), lambda i, t: (jnp.minimum(i, count - 1), 0)),
        other_spec(count, (CHUNK, depth)),
    ]
    specs = half_specs(count, (CHUNK, depth)) + [weight_spec]
    operands = [*halves, weight]
    for index, (unit, scale, grad) in enumerate(parts):
        operands += [unit, scale, grad]
        specs += [row_spec, row_spec]
        specs.append(
            pl.BlockSpec((width, CHUNK), lambda i, t: (0, t[4 * count + i]))
            if index < turned
            else row_spec
        )
    operands += values
    specs += [row_spec] * len(values)
    if rim is not None:
        operands.append(rim)
        specs.append(pl.BlockSpec(rim.shape, lambda i, t: (0, 0)))
    return pl.pallas_call(
        partial(back_project_kernel, len(parts), turned, len(values), rims, count, head_dim),
        grid_spec=pltpu.PrefetchScalarGridSpec(
            num_scalar_prefetch=1,
            grid=(2 * count,),
            in_specs=specs,
            out_specs=wide_specs + [weight_spec],
            scratch_shapes=[pltpu.VMEM((CHUNK, depth), BF16), pltpu.VMEM((CHUNK, width), F32)],
        ),
        out_shape=[
            jax.ShapeDtypeStruct((count * CHUNK, depth), BF16),
            jax.ShapeDtypeStruct((count * CHUNK, depth), BF16),
            jax.ShapeDtypeStruct(weight.shape, F32),
        ],
        compiler_params=params(),
        cost_estimate=LIGHT,
        name="back_project",
    )(table, *operands)


def band_windows(ids_ext, strips):
    start = STRIP // 2
    return jnp.stack([ids_ext[start + row : start + row + 2 * STRIP] for row in range(0, strips * STRIP, STRIP)])


def lane_taps(conv_taps, mirrored):
    front = STRIP // 2 - RIM
    heads = conv_taps.shape[0]
    taps = conv_taps[:, ::-1] if mirrored else conv_taps
    return jnp.pad(taps, ((0, -heads % 8), (front, 2 * STRIP - front - CONV)))


def fill_bands(taps_ref, bands, heads):
    for head in range(heads):
        row = jnp.broadcast_to(taps_ref[head : head + 1, :], (STRIP, 2 * STRIP))
        bands[head] = pltpu.roll(row, 0, 1, stride=1, stride_axis=0)


def band_product(band, same, window):
    band = jnp.where(same, band, 0.0)
    high = band.astype(BF16)
    low = (band - high.astype(F32)).astype(BF16)
    return nn(high, window) + nn(low, window)


def fill_extended(kept, edge, centre_ref, rim_ref):
    rows = centre_ref.shape[0]
    kept[...] = jnp.zeros_like(kept)
    kept[edge : edge + rows, :] = centre_ref[...]
    if rim_ref is not None:
        kept[edge - RIM : edge, :] = rim_ref[:RIM, :]
        kept[edge + rows : edge + rows + RIM, :] = rim_ref[RIM:, :]


def mix_kernel(head_dim, g_ref, col_ref, v_ref, rim_ref, row_ref, taps_ref, out_ref, bands, kept):
    heads = g_ref.shape[1] // head_dim
    step = pl.program_id(0)

    @pl.when(step == 0)
    def _():
        fill_bands(taps_ref, bands, heads)
        fill_extended(kept, STRIP, v_ref, rim_ref)

    masks = head_masks(head_dim)
    window = kept[pl.ds(pl.multiple_of(step * STRIP + STRIP // 2, STRIP // 2), 2 * STRIP), :]
    ids = col_ref[...]
    same = jnp.concatenate([ids, ids], axis=1) == row_ref[pl.ds(step, 1), :]
    pieces = []
    for pair in range(heads // 2):
        values = window[:, pair * PAIR : (pair + 1) * PAIR]
        total = None
        for index, mask in enumerate(masks):
            term = band_product(bands[2 * pair + index], same, values * mask)
            total = term if total is None else total + term
        pieces.append(total)
    gathered = g_ref[...]
    scale = lax.rsqrt(head_sum(gathered * gathered, head_dim) * (1.0 / head_dim) + EPS_UNIT)
    out_ref[...] = (gathered * scale + jnp.concatenate(pieces, axis=1)).astype(BF16)


def mix(gathered, values, rim, ids_ext, col, conv_taps, head_dim):
    tokens, width = gathered.shape
    heads = width // head_dim
    strips = tokens // STRIP
    row = band_windows(ids_ext[STRIP:], strips)
    taps = lane_taps(conv_taps, False)
    row_spec = pl.BlockSpec((STRIP, width), lambda i: (i, 0))
    whole = [values, rim, row, taps]
    return pl.pallas_call(
        partial(mix_kernel, head_dim),
        grid=(strips,),
        in_specs=[row_spec, pl.BlockSpec((STRIP, PAIR), lambda i: (i + 2, 0))]
        + [pl.BlockSpec(a.shape, lambda i: (0, 0)) for a in whole],
        out_specs=row_spec,
        out_shape=jax.ShapeDtypeStruct((tokens, width), BF16),
        scratch_shapes=[
            pltpu.VMEM((heads, STRIP, 2 * STRIP), F32),
            pltpu.VMEM((tokens + 2 * STRIP, width), BF16),
        ],
        compiler_params=params(),
        cost_estimate=LIGHT,
        name="mix",
    )(gathered, col, *whole)


def back_norm_kernel(head_dim, g_ref, m_ref, out_ref):
    gathered, grad = g_ref[...], m_ref[...].astype(F32)
    scale = lax.rsqrt(head_sum(gathered * gathered, head_dim) * (1.0 / head_dim) + EPS_UNIT)
    mean = head_sum(grad * gathered, head_dim) * (1.0 / head_dim)
    out_ref[...] = (scale * (grad - (scale * scale) * gathered * mean)).astype(BF16)


def back_norm(gathered, grad_mixed, head_dim):
    tokens, width = gathered.shape
    row_spec = pl.BlockSpec((CHUNK, width), lambda i: (i, 0))
    return pl.pallas_call(
        partial(back_norm_kernel, head_dim),
        grid=(tokens // CHUNK,),
        in_specs=[row_spec, row_spec],
        out_specs=row_spec,
        out_shape=jax.ShapeDtypeStruct((tokens, width), BF16),
        compiler_params=params(),
        cost_estimate=LIGHT,
        name="back_norm",
    )(gathered, grad_mixed)


def back_conv_kernel(
    head_dim, col_ref, v_ref, rim_ref, m_ref, row_ref, taps_ref, dv_ref, tap_ref, bands, sums, kept_v, kept_m
):
    heads = dv_ref.shape[1] // head_dim
    step, steps = pl.program_id(0), pl.num_programs(0)

    @pl.when(step == 0)
    def _():
        fill_bands(taps_ref, bands, heads)
        fill_extended(kept_v, 2 * STRIP, v_ref, rim_ref)
        fill_extended(kept_m, 2 * STRIP, m_ref, None)
        sums[...] = jnp.zeros_like(sums)

    masks = head_masks(head_dim)
    around = pl.ds(pl.multiple_of(step * STRIP + STRIP // 2, STRIP // 2), 2 * STRIP)
    centre = pl.ds(pl.multiple_of(step * STRIP + STRIP, STRIP), STRIP)
    ids = col_ref[...]
    same = jnp.concatenate([ids, ids], axis=1) == row_ref[pl.ds(step, 1), :]
    pieces = []
    for pair in range(heads // 2):
        cols = slice(pair * PAIR, (pair + 1) * PAIR)
        grads, values, here = kept_m[around, cols], kept_v[around, cols], kept_m[centre, cols]
        total = None
        for index, mask in enumerate(masks):
            head = 2 * pair + index
            term = band_product(bands[head], same, grads * mask)
            total = term if total is None else total + term
            sums[head] += jnp.where(same, nt(here * mask, values), 0.0)
        pieces.append(total)
    dv_ref[...] = jnp.concatenate(pieces, axis=1)

    @pl.when(step == steps - 1)
    def _():
        tap_ref[...] = jnp.zeros_like(tap_ref)
        places = [lax.broadcasted_iota(jnp.int32, (STRIP, STRIP), d) for d in (0, 1)]
        flip = (places[0] + places[1] == STRIP - 1).astype(F32).astype(BF16)
        for head in range(heads):
            total = sums[head]
            high = total.astype(BF16)
            low = (total - high.astype(F32)).astype(BF16)
            turned = pltpu.roll(
                nn(flip, high) + nn(flip, low), STRIP + 1, 1, stride=1, stride_axis=0
            )
            tap_ref[head : head + 1, :] = jnp.sum(turned, axis=0, keepdims=True)


def back_conv(values, rim, grad_mixed, ids_ext, col, conv_taps, head_dim):
    tokens, width = values.shape
    heads = width // head_dim
    strips = tokens // STRIP + 2
    row = band_windows(ids_ext, strips)
    taps = lane_taps(conv_taps, True)
    front = STRIP // 2 - RIM
    whole = [values, rim, grad_mixed, row, taps]
    grad_values, tap_sums = pl.pallas_call(
        partial(back_conv_kernel, head_dim),
        grid=(strips,),
        in_specs=[pl.BlockSpec((STRIP, PAIR), lambda i: (i + 1, 0))]
        + [pl.BlockSpec(a.shape, lambda i: (0, 0)) for a in whole],
        out_specs=[
            pl.BlockSpec((STRIP, width), lambda i: (i, 0)),
            pl.BlockSpec(taps.shape, lambda i: (0, 0)),
        ],
        out_shape=[
            jax.ShapeDtypeStruct((strips * STRIP, width), F32),
            jax.ShapeDtypeStruct(taps.shape, F32),
        ],
        scratch_shapes=[
            pltpu.VMEM((heads, STRIP, 2 * STRIP), F32),
            pltpu.VMEM((heads, STRIP, 2 * STRIP), F32),
            pltpu.VMEM((tokens + 4 * STRIP, width), BF16),
            pltpu.VMEM((tokens + 4 * STRIP, width), BF16),
        ],
        compiler_params=params(),
        cost_estimate=LIGHT,
        name="back_conv",
    )(col, *whole)
    return grad_values, tap_sums[:heads, front : front + CONV]


def occupancy_kernel(hashes, k_ref, w_ref, out_ref, counts):
    combos = 4
    lanes = hashes * combos
    side = combos * combos
    wide = hashes * side

    @pl.when(pl.program_id(1) == 0)
    def _():
        counts[...] = jnp.zeros_like(counts)

    source = lax.broadcasted_iota(jnp.int32, (lanes, wide), 0)
    target = lax.broadcasted_iota(jnp.int32, (lanes, wide), 1)
    same_hash = (source // combos) == (target // side)
    picks = []
    for divisor in (1, combos):
        chosen = same_hash & ((source % combos) == ((target // divisor) % combos))
        picks.append(chosen.astype(F32).astype(BF16))
    keys = k_ref[...]
    for index in range(2):
        signed = nn(keys, w_ref[index])
        halves = []
        for half in range(2):
            product = None
            for pick in range(2):
                start = (half * 2 + pick) * 2 * lanes
                one = 1.0 + jnp.exp(-signed[:, start : start + lanes])
                two = 1.0 + jnp.exp(-signed[:, start + lanes : start + 2 * lanes])
                spread = nn((1.0 / (one * two)).astype(BF16), picks[pick])
                product = spread if product is None else product * spread
            halves.append(product.astype(BF16))
        low, high = halves
        for start in range(0, wide, PAIR):
            block = slice(start, start + PAIR)
            counts[index, block, :] += tn(high[:, block], low[:, block])

    @pl.when(pl.program_id(1) == pl.num_programs(1) - 1)
    def _():
        row = lax.broadcasted_iota(jnp.int32, (wide, PAIR), 0)
        lane = lax.broadcasted_iota(jnp.int32, (wide, PAIR), 1)
        diagonal = ((row % PAIR) // side) == (lane // side)
        fold = [lax.broadcasted_iota(jnp.int32, (PAIR, side * side), d) for d in (0, 1)]
        fold = ((fold[0] % side) == (fold[1] % side)).astype(F32).astype(BF16)
        spot = [lax.broadcasted_iota(jnp.int32, (wide, side * side), d) for d in (0, 1)]
        kept = (spot[0] % side) == (spot[1] // side)
        home = [lax.broadcasted_iota(jnp.int32, (hashes, wide), d) for d in (0, 1)]
        home = (home[0] == home[1] // side).astype(F32).astype(BF16)
        for index in range(2):
            left = jnp.where(diagonal, counts[index], 0.0)
            total = None
            for _ in range(3):
                piece = left.astype(BF16)
                left = left - piece.astype(F32)
                spread = jnp.where(kept, nn(piece, fold), 0.0).astype(BF16)
                term = nn(home, spread)
                total = term if total is None else total + term
            out_ref[index] = total


def occupancy(key_unit, hyperplanes, scale):
    tokens, width = key_unit.shape
    hashes, bits, head_dim = hyperplanes.shape
    pairs = width // PAIR
    wide = hashes * 16
    planes = SHARP * hyperplanes.astype(F32)
    columns = []
    for group in range(bits // 2):
        for bit in range(2):
            signs = 2.0 * ((jnp.arange(4) // (2**bit)) % 2).astype(F32) - 1.0
            plane = planes[:, 2 * group + bit, :]
            columns.append((plane.T[:, :, None] * signs).reshape(head_dim, hashes * 4))
    weight = jnp.concatenate(columns, axis=1).astype(BF16)
    blank = jnp.zeros_like(weight)
    weights = jnp.stack(
        [jnp.concatenate([weight, blank], axis=0), jnp.concatenate([blank, weight], axis=0)]
    )
    counts = pl.pallas_call(
        partial(occupancy_kernel, hashes),
        grid=(pairs, tokens // CHUNK),
        in_specs=[
            pl.BlockSpec((CHUNK, PAIR), lambda p, t: (t, p)),
            pl.BlockSpec(weights.shape, lambda p, t: (0, 0, 0)),
        ],
        out_specs=pl.BlockSpec((2, hashes, 256), lambda p, t: (p, 0, 0)),
        out_shape=jax.ShapeDtypeStruct((2 * pairs, hashes, 256), F32),
        scratch_shapes=[pltpu.VMEM((2, wide, PAIR), F32)],
        compiler_params=params(),
        cost_estimate=pl.CostEstimate(
            flops=tokens * width * 32000, bytes_accessed=tokens * width * 4, transcendentals=0
        ),
        name="occupancy",
    )(key_unit, weights)
    return counts * scale


PLANE = 4


def sum_plan(n, rows):
    unit = 16 * n
    units = -(-rows // unit)
    first = -(-2 * units // 3)
    streams = [(0, first * unit, True)]
    if units > first:
        streams.append((first * unit, (units - first) * unit, False))
    return units * unit, streams


def sum_kernel(n, streams, split, *refs):
    count = len(streams)
    table_ref, misc_ref = refs[:2]
    outs, misc_out = refs[2 : 2 + split], refs[2 + split]
    scratch = refs[3 + split :]
    send, recv = scratch[-2:]
    me = lax.axis_index("seq")
    groups = n // PLANE
    near_me, far_me = lax.rem(me, PLANE), me // PLANE

    def device(plane_first, one, two):
        return {"seq": two * PLANE + one if plane_first else one * PLANE + two}

    barrier = pltpu.get_barrier_semaphore()
    for step in range(1, PLANE):
        pl.semaphore_signal(
            barrier, 1, device_id=device(True, lax.rem(near_me + step, PLANE), far_me)
        )
    for step in range(1, groups):
        pl.semaphore_signal(
            barrier, 1, device_id=device(True, near_me, lax.rem(far_me + step, groups))
        )
    pl.semaphore_wait(barrier, PLANE - 1 + groups - 1)

    facts = []
    for index, (base, rows, plane_first) in enumerate(streams):
        sizes = (PLANE, groups) if plane_first else (groups, PLANE)
        mine = (near_me, far_me) if plane_first else (far_me, near_me)
        buffers = scratch[5 * index : 5 * index + 5]
        source = misc_ref if index == count - 1 else table_ref
        block, chunk = rows // sizes[0], rows // n
        facts.append((index, source, base, plane_first, sizes, mine, block, chunk, buffers))

    def at(start, number):
        return pl.ds(pl.multiple_of(start, 8), number)

    def start_all(phase):
        started = []
        for index, source, base, plane_first, sizes, mine, block, chunk, buffers in facts:
            got_one, part, got_two, merged, full = buffers
            side = 0 if phase in (0, 3) else 1
            for step in range(1, sizes[side]):
                to = lax.rem(mine[side] + step, sizes[side])
                if phase == 0:
                    src, dst = source.at[at(base + to * block, block), :], got_one.at[step - 1]
                elif phase == 1:
                    src, dst = part.at[at(to * chunk, chunk), :], got_two.at[step - 1]
                elif phase == 2:
                    src = dst = merged.at[at(mine[1] * chunk, chunk), :]
                else:
                    src, dst = merged, full.at[at(mine[0] * block, block), :]
                pair = (to, mine[1]) if side == 0 else (mine[0], to)
                copy = pltpu.make_async_remote_copy(
                    src_ref=src,
                    dst_ref=dst,
                    send_sem=send.at[index, phase, step - 1],
                    recv_sem=recv.at[index, phase, step - 1],
                    device_id=device(plane_first, *pair),
                    device_id_type=pl.DeviceIdType.MESH,
                )
                copy.start()
                started.append(copy)
        return started

    def wait_all(started):
        for copy in started:
            copy.wait()

    wait_all(start_all(0))
    for index, source, base, plane_first, sizes, mine, block, chunk, buffers in facts:
        got_one, part, got_two, merged, full = buffers

        def add(piece, carry):
            rows = at(piece * chunk, chunk)
            total = source[at(base + mine[0] * block + piece * chunk, chunk), :].astype(F32)
            for step in range(sizes[0] - 1):
                total = total + got_one[step, rows, :].astype(F32)
            part[rows, :] = total.astype(part.dtype)
            return carry

        lax.fori_loop(0, sizes[1], add, 0)
    wait_all(start_all(1))
    for index, source, base, plane_first, sizes, mine, block, chunk, buffers in facts:
        got_one, part, got_two, merged, full = buffers
        rows = at(mine[1] * chunk, chunk)
        total = part[rows, :].astype(F32)
        for step in range(sizes[1] - 1):
            total = total + got_two[step].astype(F32)
        merged[rows, :] = total.astype(merged.dtype)
    wait_all(start_all(2))
    started = start_all(3)
    for index, source, base, plane_first, sizes, mine, block, chunk, buffers in facts:
        merged, full = buffers[3:]
        full[at(mine[0] * block, block), :] = merged[...]
    wait_all(started)
    for index, source, base, plane_first, sizes, mine, block, chunk, buffers in facts:
        full = buffers[4]

        def put(piece, carry):
            rows = at(piece * chunk, chunk)
            if index == count - 1:
                misc_out[rows, :] = full[rows, :]
            else:
                there = at(base + piece * chunk, chunk)
                for part_index, out in enumerate(outs):
                    width = out.shape[1]
                    lanes = slice(part_index * width, (part_index + 1) * width)
                    out[there, :] = full[rows, lanes].astype(F32)
            return carry

        lax.fori_loop(0, n, put, 0)


def sum_over_seq(table, misc, split):
    n = lax.axis_size("seq")
    rows, width = table.shape
    padded, streams = sum_plan(n, rows)
    if padded > rows:
        table = jnp.pad(table, ((0, padded - rows), (0, 0)))
    lanes = -(-misc.size // (8 * n * PAIR)) * PAIR
    misc_table = jnp.pad(misc, (0, 8 * n * lanes - misc.size)).reshape(8 * n, lanes)
    streams = streams + [(0, 8 * n, True)]
    scratch = []
    for index, (_, stream_rows, plane_first) in enumerate(streams):
        last = index == len(streams) - 1
        kind, lane_count = (F32, lanes) if last else (BF16, width)
        one, two = (PLANE, n // PLANE) if plane_first else (n // PLANE, PLANE)
        block, chunk = stream_rows // one, stream_rows // n
        scratch += [
            pltpu.VMEM((one - 1, block, lane_count), kind),
            pltpu.VMEM((block, lane_count), kind),
            pltpu.VMEM((two - 1, chunk, lane_count), kind),
            pltpu.VMEM((block, lane_count), kind),
            pltpu.VMEM((stream_rows, lane_count), kind),
        ]
    partners = max(PLANE, n // PLANE) - 1
    sems = pltpu.SemaphoreType.DMA((len(streams), 4, partners))
    in_vmem = pl.BlockSpec(memory_space=pltpu.VMEM)
    shapes = [jax.ShapeDtypeStruct((padded, width // split), F32)] * split
    *sums, misc_sum = pl.pallas_call(
        partial(sum_kernel, n, streams, split),
        in_specs=[in_vmem, in_vmem],
        out_specs=[in_vmem] * (split + 1),
        out_shape=shapes + [jax.ShapeDtypeStruct(misc_table.shape, F32)],
        scratch_shapes=scratch + [sems, sems],
        compiler_params=params(collective_id=0, has_side_effects=True),
        cost_estimate=pl.CostEstimate(flops=1 << 36, bytes_accessed=1 << 24, transcendentals=0),
        name="sum_over_seq",
    )(table, misc_table)
    return [total[:rows] for total in sums], misc_sum.reshape(-1)[: misc.size]


def doc_ids(lengths, positions, all_tokens):
    doc_ends = jnp.cumsum(lengths)
    doc_index = jnp.sum((doc_ends[None, :] <= positions[:, None]).astype(jnp.int32), axis=1)
    doc_index = jnp.where(positions < 0, -1, doc_index)
    return jnp.where(positions >= all_tokens, FAR_ID, doc_index)


def shifted(block, axis, distance):
    count = lax.axis_size(axis)
    route = [(i, i + distance) for i in range(count) if 0 <= i + distance < count]
    return lax.ppermute(block, axis, route)


def swapped(block, axis):
    return lax.ppermute(block, axis, [(0, 1), (1, 0)])


def tp_sum(partial_low):
    return partial_low.astype(F32) + swapped(partial_low, "tp").astype(F32)


def after(value, *others):
    return lax.optimization_barrier((value, *others))[0]


def layer_norm(vectors, gain_row, shift_row):
    center = vectors - jnp.mean(vectors, axis=-1, keepdims=True)
    spread = jnp.mean(center * center, axis=-1, keepdims=True)
    return center * lax.rsqrt(spread + EPS_LAYER) * gain_row + shift_row


def body(
    inputs,
    cotangent,
    query_weight,
    key_weight,
    value_weight,
    out_weight,
    up_weight,
    down_weight,
    conv_taps,
    attn_gain,
    attn_shift,
    ffn_gain,
    ffn_shift,
    hyperplanes,
    lengths,
):
    tokens, depth = inputs.shape
    head_dim = hyperplanes.shape[2]
    width = query_weight.shape[1]
    half = tokens // 2
    my_index = lax.axis_index("seq")
    my_side = lax.axis_index("tp")
    all_tokens = tokens * lax.axis_size("seq")
    far_reach = (MOST + tokens - 2) // tokens
    close = far_reach // 2
    near = list(range(close, 0, -1)) + list(range(-1, -close - 1, -1))
    far = list(range(far_reach, close, -1)) + list(range(-close - 1, -far_reach - 1, -1))
    groups = [near, far]
    first_token = my_index * tokens

    mine_rows = lax.dynamic_slice_in_dim(inputs, my_side * half, half, 0)
    near_mine = [shifted(mine_rows, "seq", d) for d in near]

    def ids_at(positions):
        return doc_ids(lengths, positions, all_tokens)

    def span(start, count, step=1):
        return start + step * jnp.arange(count, dtype=jnp.int32)

    ids_ext = ids_at(span(first_token - 2 * STRIP, tokens + 4 * STRIP))
    ids_col = jnp.broadcast_to(ids_ext[:, None], (ids_ext.shape[0], PAIR))
    own_ids = ids_at(span(first_token, tokens))
    q_count = tokens // Q_TILE_BACK
    k_starts = [
        jnp.concatenate([span(first_token - d * tokens, tokens // CHUNK, CHUNK) for d in part])
        for part in groups + [[0]]
    ]
    k_counts = [starts.shape[0] for starts in k_starts]
    q_starts = span(first_token, q_count, Q_TILE_BACK)
    ends = ids_at(
        jnp.concatenate(
            [q_starts, q_starts + Q_TILE_BACK - 1]
            + [starts + extra for starts in k_starts for extra in (0, CHUNK - 1)]
        )
    )
    q_low, q_high = ends[:q_count], ends[q_count : 2 * q_count]
    ratio = Q_TILE // Q_TILE_BACK
    q_ends = [q_low[::ratio], q_high[ratio - 1 :: ratio]]
    tables, back_tables, chunk_tables, fill_tables, needs, group_ids = [], [], [], [], [], []
    spot = 2 * q_count
    for starts, count in zip(k_starts, k_counts):
        pieces = ends[spot : spot + 2 * count]
        spot += 2 * count
        tables.append(pieces)
        back_tables.append(jnp.concatenate([q_low, q_high, pieces]))
        need = ((pieces[count:] >= q_low[0]) & (pieces[:count] <= q_high[-1])).astype(jnp.int32)
        need = need.reshape(-1, 2)
        places = span(0, count).reshape(-1, 2)
        ordered = []
        for pair in (places, need):
            mine = jnp.where(my_side == 0, pair[:, 0], pair[:, 1])
            other = jnp.where(my_side == 0, pair[:, 1], pair[:, 0])
            ordered += [mine, other]
        place = jnp.concatenate(ordered[:2])
        wanted = jnp.concatenate(ordered[2:])
        chunk_tables.append(jnp.concatenate([place, wanted, place * wanted]))
        fill_tables.append(jnp.concatenate([jnp.where(wanted > 0, place, count), wanted]))
        needs.append(need)
        group_ids.append(
            ids_at((starts[:, None] + jnp.arange(CHUNK, dtype=jnp.int32)).reshape(-1))
        )
    near_at, far_at, own_at = range(3)

    weight_qkv = jnp.concatenate([query_weight, key_weight, value_weight], axis=1)
    weight_kv = weight_qkv[:, width:]
    plain_table = jnp.array(list(range(tokens // CHUNK)) + [1] * (tokens // CHUNK), jnp.int32)
    query_unit, query_scale, key_unit, key_scale, values = project(
        plain_table, [inputs], weight_qkv, 2, head_dim
    )
    gathered = attend(
        jnp.concatenate([*q_ends, tables[own_at]]),
        query_unit,
        own_ids,
        [(key_unit, values, own_ids)],
        head_dim,
    )

    def other_half(mine):
        return jnp.concatenate([swapped(term, "tp") for term in mine], axis=0)

    *near_mine, late_rows = after((*near_mine, mine_rows), gathered)
    far_mine = [shifted(late_rows, "seq", d) for d in far]
    near_other = other_half(near_mine)
    occ_local = occupancy(after(key_unit, *near_mine), hyperplanes, 2.0**BITS / all_tokens)
    near_x = [*near_mine, after(near_other, occ_local)]
    near_kv = project(fill_tables[near_at], near_x, weight_kv, 1, head_dim)
    *far_mine, query_late = after((*far_mine, query_unit), *near_kv)
    far_other = other_half(far_mine)
    gathered = attend(
        jnp.concatenate([*q_ends, tables[near_at]]),
        query_late,
        own_ids,
        [(near_kv[0], near_kv[2], group_ids[near_at])],
        head_dim,
        seed=gathered,
    )
    far_x = [*far_mine, after(far_other, gathered)]
    far_kv = project(fill_tables[far_at], far_x, weight_kv, 1, head_dim)
    gathered = attend(
        jnp.concatenate([*q_ends, tables[far_at]]),
        query_unit,
        own_ids,
        [(far_kv[0], far_kv[2], group_ids[far_at])],
        head_dim,
        seed=gathered,
    )
    group_x, group_kv = [near_x, far_x], [near_kv, far_kv]
    edge = close * tokens
    sides = needs[near_at].reshape(-1)[edge // CHUNK - 1 : edge // CHUNK + 1]
    values_rim = jnp.where(
        jnp.repeat(sides, RIM)[:, None] > 0, group_kv[near_at][2][edge - RIM : edge + RIM], 0
    )
    mixed = mix(gathered, values, values_rim, ids_ext, ids_col, conv_taps, head_dim)

    attn_out = tp_sum(nn(mixed, out_weight).astype(BF16))
    first_norm, first_back = jax.vjp(
        layer_norm, inputs.astype(F32) + attn_out, attn_gain, attn_shift
    )
    first_low = first_norm.astype(BF16)
    hidden = nn(first_low, up_weight)
    active = jax.nn.gelu(hidden, approximate=False).astype(BF16)
    ffn_out = tp_sum(nn(active, down_weight).astype(BF16))
    result, second_back = jax.vjp(layer_norm, first_norm + ffn_out, ffn_gain, ffn_shift)
    output = result.astype(BF16)
    grad_second, grad_ffn_gain, grad_ffn_shift = second_back(cotangent.astype(F32))
    grad_ffn = grad_second.astype(BF16)
    grad_active = nt(grad_ffn, down_weight)
    unused_gelu, gelu_back = jax.vjp(partial(jax.nn.gelu, approximate=False), hidden)
    grad_hidden = gelu_back(grad_active)[0].astype(BF16)
    grad_first = grad_second + tp_sum(nt(grad_hidden, up_weight).astype(BF16))
    grad_residual, grad_attn_gain, grad_attn_shift = first_back(grad_first)
    grad_attn = grad_residual.astype(BF16)
    grad_mixed = nt(grad_attn, out_weight).astype(BF16)

    grad_down = tn(active, grad_ffn).astype(BF16)
    grad_up = tn(first_low, grad_hidden).astype(BF16)
    grad_out = tn(mixed, grad_attn).astype(BF16)
    down_out = jnp.concatenate([grad_down, grad_out], axis=0)
    grad_up_low, down_out_low = grad_up, down_out
    grad_up, down_out = lax.psum((grad_up_low, down_out_low), "seq")

    grad_rows = back_norm(gathered, after(grad_mixed, grad_up_low, down_out_low), head_dim)

    def back_scores(index, grad_rows, seed):
        key_far, _, value_far = group_kv[index]
        return back_attend(
            back_tables[index],
            query_unit,
            grad_rows,
            key_far,
            value_far,
            own_ids,
            group_ids[index],
            head_dim,
            seed=seed,
        )

    def back_inputs(index, dk, dv, **rims):
        key_far, scale_far, _ = group_kv[index]
        parts = [(key_far, scale_far, dk)]
        return back_project(
            chunk_tables[index], group_x[index], weight_kv, parts, 0, [dv], head_dim, **rims
        )

    def send_home(distances, dx_mine, came):
        both = [
            (
                dx_mine[i * half : (i + 1) * half].astype(F32)
                + came[i * half : (i + 1) * half].astype(F32)
            ).astype(BF16)
            for i in range(len(distances))
        ]
        return both, [shifted(term, "seq", -d) for term, d in zip(both, distances)]

    dk, dv, turned = back_scores(far_at, grad_rows, None)
    far_dx, dx_other, far_dw = back_inputs(far_at, dk, dv)
    far_came = swapped(dx_other, "tp")
    grad_conv_values, grad_taps = back_conv(
        values, values_rim, after(grad_mixed, far_dx), ids_ext, ids_col, conv_taps, head_dim
    )
    rim = jnp.concatenate([grad_conv_values[:STRIP], grad_conv_values[-STRIP:]], axis=0)
    dk, dv, turned = back_scores(near_at, after(grad_rows, grad_conv_values), turned)
    near_dx, dx_other, near_dw = back_inputs(
        near_at, dk, dv, rims=close * (tokens // CHUNK) - 1, rim=rim
    )
    near_came = swapped(dx_other, "tp")
    far_came, grad_up, down_out = after((far_came, grad_up, down_out), near_dx)
    terms, far_homes = send_home(far, far_dx, far_came)
    dk, dv, turned = back_attend(
        back_tables[own_at],
        query_unit,
        after(grad_rows, *terms),
        key_unit,
        values,
        own_ids,
        own_ids,
        head_dim,
        seed=turned,
        cost=pl.CostEstimate(flops=1 << 35, bytes_accessed=1 << 20, transcendentals=0),
    )
    terms, near_homes = send_home(near, near_dx, after(near_came, dk))
    dk, far_homes = after((dk, far_homes), *terms)
    own_mine = mine_rows
    own_other = lax.dynamic_slice_in_dim(inputs, (1 - my_side) * half, half, 0)
    dx_mine, dx_other, dw = back_project(
        chunk_tables[own_at],
        [own_mine, own_other],
        weight_qkv,
        [(query_unit, query_scale, turned), (key_unit, key_scale, dk)],
        1,
        [dv, grad_conv_values[STRIP:-STRIP]],
        head_dim,
    )

    qkv = jnp.concatenate([dw[:, :width], dw[:, width:] + near_dw + far_dw], axis=1).astype(BF16)
    misc = [
        occ_local,
        grad_taps,
        grad_attn_gain,
        grad_attn_shift,
        grad_ffn_gain,
        grad_ffn_shift,
    ]
    packed = jnp.concatenate([term.reshape(-1) for term in misc])
    qkv, packed = sum_over_seq(qkv, packed, 3)

    came = swapped(dx_other, "tp")
    near_homes = after(tuple(near_homes), packed)
    total = (
        lax.dynamic_slice_in_dim(grad_residual, my_side * half, half, 0)
        + dx_mine.astype(F32)
        + came.astype(F32)
    )
    for home in (*far_homes, *near_homes):
        total = total + home.astype(F32)
    other_total = swapped(total, "tp")
    lower = jnp.where(my_side == 0, total, other_total)
    upper = jnp.where(my_side == 0, other_total, total)
    grad_inputs = jnp.concatenate([lower, upper], axis=0)

    unpacked, at = [], 0
    for term in misc:
        unpacked.append(packed[at : at + term.size].reshape(term.shape))
        at += term.size
    down_out = down_out.astype(F32)
    ff = down_weight.shape[0]
    return (
        output,
        grad_inputs,
        *qkv,
        down_out[ff:],
        grad_up.astype(F32),
        down_out[:ff],
        *unpacked[1:],
        unpacked[0],
    )


def solution(mesh):
    return jax.shard_map(
        body,
        mesh=mesh,
        in_specs=(
            P("seq", None),
            P("seq", None),
            P(None, "tp"),
            P(None, "tp"),
            P(None, "tp"),
            P("tp", None),
            P(None, "tp"),
            P("tp", None),
            P("tp", None),
            P(),
            P(),
            P(),
            P(),
            P(),
            P(),
        ),
        out_specs=(
            P("seq", None),
            P("seq", None),
            P(None, "tp"),
            P(None, "tp"),
            P(None, "tp"),
            P("tp", None),
            P(None, "tp"),
            P("tp", None),
            P("tp", None),
            P(),
            P(),
            P(),
            P(),
            P("tp", None, None),
        ),
        check_vma=False,
    )
```

time: 1160 us -> 781 us (0.67)
  starting transfers between devices: 405 us -> 78 us
  Pallas kernels: 240 us -> 370 us
  blocking collectives: 89.1 us -> 0 us
  local copies, waits for them, and re-layouts: 109 us -> 51.6 us
  waiting for transfers between devices: 197 us -> 154 us
    ppermute x20 -> x16, starting transfers between devices: 403 us -> 73.6 us  [shifted(): return lax.ppermute(block, axis, route)]
    psum x1 -> x0, blocking collectives: 89.1 us -> none  [body(): lax.psum((grad_taps, grad_attn_gain, grad_attn_shift, grad_ffn_gain, grad...]
    pallas_call x13 -> x14, Pallas kernels: 167 us -> 250 us  [the longest x3 75.1 us: attend(): pl.pallas_call(partial(attend_kernel, head_dim, len(sources), seed is not...]
    pallas_call x3, Pallas kernels: 72.2 us -> 121 us  [back_attend(): pl.pallas_call(partial(back_attend_kernel, head_dim, seed is not None), g...]
    psum x2 -> x1, waiting for transfers between devices: 146 us -> 123 us  [body(): grad_up, down_out = lax.psum((grad_up_low, down_out_low), 'seq')]
    ppermute x20 -> x16, waiting for transfers between devices: 46.7 us -> 24.7 us  [shifted(): return lax.ppermute(block, axis, route)]
    unnamed x128 -> x167, local copies, waits for them, and re-layouts: 31.4 us -> 12 us
    reshape x3, local copies, waits for them, and re-layouts: 18 us -> 1.5 us  [the longest x1 0.74 us: sum_over_seq(): jnp.pad(misc, (0, 8 * n * lanes - misc.size)).reshape(8 * n, lanes)]
  transfers between devices with their start and end apart: 31 -> 32, of which waited for: 9 -> 6; matrix products, arithmetic and copies ran while one was open for 12% -> 10% of each run, Pallas kernels for 17% -> 45%
where the time goes in v2:
time: 781 us; the launch traced here: 770 us
  Pallas kernels  370 us (47%)
  waiting for transfers between devices  154 us (20%)
  starting transfers between devices  78 us (10%)
  other arithmetic  55.3 us (7%)
  local copies, waits for them, and re-layouts  51.6 us (7%)
  matrix products  41 us (5%)
  between operations  19.5 us (2%)
    psum x1, waiting for transfers between devices, body(): grad_up, down_out = lax.psum((grad_up_low, down_out_low), 'seq')  123 us
    pallas_call x3, Pallas kernels, back_attend(): pl.pallas_call(partial(back_attend_kernel, head_dim, seed is not None), g...  121 us
    pallas_call x3, Pallas kernels, attend(): pl.pallas_call(partial(attend_kernel, head_dim, len(sources), seed is not...  75.1 us
    ppermute x16, starting transfers between devices, shifted(): return lax.ppermute(block, axis, route)  73.6 us
    pallas_call x1, Pallas kernels, sum_over_seq(): pl.pallas_call(partial(sum_kernel, n, streams, split), in_specs=[in_vmem,...  61.6 us
    pallas_call x3, Pallas kernels, back_project(): pl.pallas_call(partial(back_project_kernel, len(parts), turned, len(value...  45.8 us
    pallas_call x3, Pallas kernels, project(): pl.pallas_call(partial(project_kernel, units, count, head_dim), grid_spec...  25.8 us
    ppermute x16, waiting for transfers between devices, shifted(): return lax.ppermute(block, axis, route)  24.7 us
  transfers between devices with their start and end apart: 32, of which 6 were waited for; matrix products, arithmetic and copies ran while one was open for 10% of the time, Pallas kernels for 45%

profile of v2, /device:TPU:0, one launch (start us, length us, event | category | flops | bytes accessed | tf_op | source)
XLA Modules:
  0.0 769.7 jit_solution(13602099759405363246)
XLA Ops:
  7.3 2.8 constant_dynamic-slice_fusion
  10.1 5.8 collective-permute-start
  15.9 4.3 collective-permute-start.1
  42.9 7.5 project.3
  54.6 26.9 %attend.3.rest_3_ = f32[1024,384]{1,0:T(8,128)} custom-call(s32[8]{0:T(128)} %pad_add_fusion.7.table, bf16[1024,384]{1,0:T(8,128)(2,1)} %get-tuple-element.96.q_ref.refs_3_, s32[2,512]{1,0:T(2,128)} %compare_select_fusion.1.qrow_ref.rest_2_.krow_ref, bf16[1024,384]{1,0:T(8,128)(2,1)} %get-tuple-element.87.rest_0_.k_ref.refs_6_, ...), custom_call_target="tpu_custom_call" | custom-call | flops 12884901888 | bytes 1572864 | tf_op jit(solution)/shard_map/attend/pallas_call | solution.py:254
  82.6 6.9 collective-permute-start.4
  89.5 19.6 %occupancy.1 = f32[6,32,256]{2,1,0:T(8,128)} custom-call(bf16[1024,384]{1,0:T(8,128)(2,1)} %get-tuple-element.87.rest_0_.k_ref.refs_6_, bf16[2,128,1024]{2,1,0:T(8,128)(2,1)} %pad_maximum_fusion.5.w_ref), custom_call_target="tpu_custom_call" | custom-call | flops 12582912000 | bytes 1572864 | tf_op jit(solution)/shard_map/occupancy/pallas_call | solution.py:750
  110.8 2.9 collective-permute-start.5
  118.3 11.0 %project.4 = (bf16[4608,384]{1,0:T(8,128)(2,1)}, f32[4608,384]{1,0:T(8,128)}, bf16[4608,384]{1,0:T(8,128)(2,1)}) custom-call(s32[16]{0:T(128)} %pad_add_fusion.9.table, bf16[512,768]{1,0:T(8,128)(2,1)} %collective-permute-done.refs_0_, bf16[512,768]{1,0:T(8,128)(2,1)} %collective-permute-done.1.refs_1_, bf16[512,768]{1,0:T(8,128)(2,1)} %collective-permute-done.2.refs_2_, ...), custom_call_target="tpu_custom_call" | custom-call | flops 9663676416 | bytes 3145728 | tf_op jit(solution)/shard_map/project/pallas_call | solution.py:138
  129.2 18.3 %collective-permute-done.5.refs_1_ = bf16[512,768]{1,0:T(8,128)(2,1)S(1)} collective-permute-done((bf16[512,768]{1,0:T(8,128)(2,1)}, bf16[512,768]{1,0:T(8,128)(2,1)S(1)}, u32[]{:S(2)}, u32[]{:S(2)}) %collective-permute-start.5) | collective-permute-done | bytes 786464 | tf_op jit(solution)/shard_map/ppermute | solution.py:944
  147.6 5.7 collective-permute-done.7.refs_3_
  154.3 41.4 %attend.4.rest_3_ = f32[1024,384]{1,0:T(8,128)} custom-call(s32[20]{0:T(128)} %get-tuple-element.224.table, bf16[1024,384]{1,0:T(8,128)(2,1)} %get-tuple-element.96.q_ref.refs_3_, s32[2,512]{1,0:T(2,128)} %compare_select_fusion.1.qrow_ref.rest_2_.krow_ref, bf16[4608,384]{1,0:T(8,128)(2,1)} %get-tuple-element.89.rest_0_.k_ref.refs_6_, ...), custom_call_target="tpu_custom_call" | custom-call | flops 51539607552 | bytes 6291456 | tf_op jit(solution)/shard_map/attend/pallas_call | solution.py:254
  199.0 7.4 project.5
  206.4 6.9 attend.5.g_ref
  214.4 8.2 %mix.1 = bf16[1024,384]{1,0:T(8,128)(2,1)} custom-call(f32[1024,384]{1,0:T(8,128)} %attend.5.g_ref, s32[1536,128]{1,0:T(8,128)} %broadcast_in_dim.118.col_ref, bf16[1024,384]{1,0:T(8,128)(2,1)} %get-tuple-element.81.rest_1_.v_ref, bf16[32,384]{1,0:T(8,128)(2,1)} %slice_select_fusion.rim_ref, s32[8,256]{1,0:T(8,128)} %stack.64.row_ref, f32[8,256]{1,0:T(8,128)} %pad.13.taps_ref), custom_call_target="tpu_custom_call" | custom-call | flops 1048576 | bytes 65536 | tf_op jit(solution)/shard_map/mix/pallas_call | solution.py:556
  222.6 2.1 convolution_convert_fusion.2
  224.8 3.4 collective-permute-done.16
  229.6 17.0 %multiply_convert_fusion = (bf16[1024,1536]{1,0:T(8,128)(2,1)S(1)}, f32[1024,1536]{1,0:T(8,128)S(1)}, f32[1024,1536]{1,0:T(8,128)}) fusion(bf16[768,1536]{1,0:T(8,128)(2,1)S(1)} %copy-done, f32[1024,768]{1,0:T(8,128)S(1)} %get-tuple-element.172, f32[768]{0:T(1024)S(1)} %copy-done.61, f32[768]{0:T(1024)S(1)} %copy-done.30, f32[1024]{0:T(1024)S(1)} %fusion.21, ...), kind=kOutput, calls=%fused_computation.3 | convolution fusion | flops 2522087424 | bytes 21248000 | tf_op jit(solution)/shard_map/dot_general | solution.py:49
  246.7 2.6 convolution_convert_fusion.4
  249.5 3.3 collective-permute-done.17
  256.7 2.8 fusion.48
  259.5 6.3 add_convert_fusion
  265.8 2.6 convolution_convert_fusion.3
  268.7 3.3 convolution_convert_fusion
  272.0 4.2 convolution_convert_fusion.1
  276.2 2.1 multiply_reduce_fusion
  288.4 3.4 back_norm.1.g_ref
  291.7 8.7 %back_attend.3 = (bf16[4096,384]{1,0:T(8,128)(2,1)}, bf16[4096,384]{1,0:T(8,128)(2,1)}, f32[384,1024]{1,0:T(8,128)}) custom-call(s32[24]{0:T(128)} %pad_add_fusion.12.table, bf16[1024,384]{1,0:T(8,128)(2,1)} %get-tuple-element.96.q_ref.refs_3_, bf16[1024,384]{1,0:T(8,128)(2,1)} %back_norm.1.g_ref, bf16[4608,384]{1,0:T(8,128)(2,1)} %get-tuple-element.98.rest_0_.k_ref.refs_6_, ...), custom_call_target="tpu_custom_call" | custom-call | flops 1048576 | bytes 65536 | tf_op jit(solution)/shard_map/back_attend/pallas_call | solution.py:362
  300.6 11.0 %back_project.3 = (bf16[2048,768]{1,0:T(8,128)(2,1)}, bf16[2048,768]{1,0:T(8,128)(2,1)}, f32[768,768]{1,0:T(8,128)}) custom-call(s32[24]{0:T(128)} %concatenate.123.table, bf16[512,768]{1,0:T(8,128)(2,1)} %copy-done.17, bf16[512,768]{1,0:T(8,128)(2,1)} %copy-done.18, bf16[512,768]{1,0:T(8,128)(2,1)} %copy-done.19, ...), custom_call_target="tpu_custom_call" | custom-call | flops 1048576 | bytes 65536 | tf_op jit(solution)/shard_map/back_project/pallas_call | solution.py:468
  315.4 9.9 %back_conv.1 = (f32[1280,384]{1,0:T(8,128)}, f32[8,256]{1,0:T(8,128)}) custom-call(s32[1536,128]{1,0:T(8,128)} %broadcast_in_dim.118.col_ref, bf16[1024,384]{1,0:T(8,128)(2,1)} %get-tuple-element.81.rest_1_.v_ref, bf16[32,384]{1,0:T(8,128)(2,1)} %slice_select_fusion.rim_ref, bf16[1024,384]{1,0:T(8,128)(2,1)} %convolution_convert_fusion.5.m_ref, ...), custom_call_target="tpu_custom_call" | custom-call | flops 1048576 | bytes 65536 | tf_op jit(solution)/shard_map/back_conv/pallas_call | solution.py:649
  325.3 67.8 %back_attend.4 = (bf16[4096,384]{1,0:T(8,128)(2,1)}, bf16[4096,384]{1,0:T(8,128)(2,1)}, f32[384,1024]{1,0:T(8,128)}) custom-call(s32[24]{0:T(128)} %bitcast.94, bf16[1024,384]{1,0:T(8,128)(2,1)} %get-tuple-element.96.q_ref.refs_3_, bf16[1024,384]{1,0:T(8,128)(2,1)} %back_norm.1.g_ref, bf16[4608,384]{1,0:T(8,128)(2,1)} %get-tuple-element.89.rest_0_.k_ref.refs_6_, ...), custom_call_target="tpu_custom_call" | custom-call | flops 1048576 | bytes 65536 | tf_op jit(solution)/shard_map/back_attend/pallas_call | solution.py:362
  394.9 19.2 %back_project.4 = (bf16[2048,768]{1,0:T(8,128)(2,1)}, bf16[2048,768]{1,0:T(8,128)(2,1)}, f32[768,768]{1,0:T(8,128)}) custom-call(s32[24]{0:T(128)} %concatenate.125.table, bf16[512,768]{1,0:T(8,128)(2,1)} %collective-permute-done.refs_0_, bf16[512,768]{1,0:T(8,128)(2,1)} %collective-permute-done.1.refs_1_, bf16[512,768]{1,0:T(8,128)(2,1)} %collective-permute-done.2.refs_2_, ...), custom_call_target="tpu_custom_call" | custom-call | flops 1048576 | bytes 65536 | tf_op jit(solution)/shard_map/back_project/pallas_call | solution.py:468
  414.9 122.8 %all-reduce.8.cloned.1.call-done = (bf16[768,1536]{1,0:T(8,128)(2,1)}, bf16[1920,768]{1,0:T(8,128)(2,1)}) async-done(((bf16[768,1536]{1,0:T(8,128)(2,1)}, bf16[1920,768]{1,0:T(8,128)(2,1)}), (bf16[768,1536]{1,0:T(8,128)(2,1)}, bf16[1920,768]{1,0:T(8,128)(2,1)})) %all-reduce.8.cloned.1.call-update) | async-done | bytes 5308432 | tf_op jit(solution)/shard_map/psum | solution.py:1125
  537.6 4.7 add_convert_fusion.8
  544.9 6.4 collective-permute-start.22
  551.2 4.5 collective-permute-start.23
  555.8 44.1 %back_attend.5 = (bf16[1024,384]{1,0:T(8,128)(2,1)}, bf16[1024,384]{1,0:T(8,128)(2,1)}, f32[384,1024]{1,0:T(8,128)}) custom-call(s32[12]{0:T(128)} %pad_add_fusion.11.table, bf16[1024,384]{1,0:T(8,128)(2,1)} %get-tuple-element.96.q_ref.refs_3_, bf16[1024,384]{1,0:T(8,128)(2,1)} %back_norm.1.g_ref, bf16[1024,384]{1,0:T(8,128)(2,1)} %get-tuple-element.87.rest_0_.k_ref.refs_6_, ...), custom_call_target="tpu_custom_call" | custom-call | flops 34359738368 | bytes 1048576 | tf_op jit(solution)/shard_map/back_attend/pallas_call | solution.py:362
  599.9 4.0 add_convert_fusion.4
  606.5 5.5 collective-permute-start.28
  612.0 27.0 %collective-permute-start.29 = (bf16[512,768]{1,0:T(8,128)(2,1)}, bf16[512,768]{1,0:T(8,128)(2,1)}, u32[]{:S(2)}, u32[]{:S(2)}) collective-permute-start(bf16[512,768]{1,0:T(8,128)(2,1)} %get-tuple-element.179), channel_id=1, source_target_pairs={{0,4},{2,6},{4,8},{6,10},{8,12},{10,14},{12,16},{14,18},{16,20},{1... | collective-permute-start | bytes 2359304 | tf_op jit(solution)/shard_map/ppermute | solution.py:944
  646.1 2.7 slice.382.refs_10_
  648.8 15.6 %back_project.5 = (bf16[512,768]{1,0:T(8,128)(2,1)}, bf16[512,768]{1,0:T(8,128)(2,1)}, f32[768,1152]{1,0:T(8,128)}) custom-call(s32[6]{0:T(128)} %concatenate.120.table, bf16[512,768]{1,0:T(8,128)(2,1)} %get-tuple-element.82.refs_0_, bf16[512,768]{1,0:T(8,128)(2,1)} %get-tuple-element.192.refs_1_, bf16[768,1152]{1,0:T(8,128)(2,1)} %get-tuple-element.195.refs_1_.refs_2_, ...), custom_call_target="tpu_custom_call" | custom-call | flops 1048576 | bytes 65536 | tf_op jit(solution)/shard_map/back_project/pallas_call | solution.py:468
  664.7 4.8 concatenate.129
  671.2 4.2 slice.415
  675.4 2.3 slice.414
  677.7 3.0 convert_element_type.305
  684.6 5.3 convert_add_fusion
  690.4 61.6 %sum_over_seq.1 = (f32[768,384]{1,0:T(8,128)}, f32[768,384]{1,0:T(8,128)}, f32[768,384]{1,0:T(8,128)}, f32[128,512]{1,0:T(8,128)}) custom-call(bf16[768,1152]{1,0:T(8,128)(2,1)} %pad_maximum_fusion.4.refs_0_, f32[128,512]{1,0:T(8,128)} %reshape.379.refs_1_), custom_call_target="tpu_custom_call" | custom-call | flops 68719476736 | bytes 16777216 | tf_op jit(solution)/shard_map/sum_over_seq/pallas_call | solution.py:921
  (363 shorter events, 86.4 us)
Async XLA Ops:
  7.2 222.3 %copy-start = (bf16[768,1536]{1,0:T(8,128)(2,1)S(1)}, bf16[768,1536]{1,0:T(8,128)(2,1)}, u32[]{:S(2)}) copy-start(bf16[768,1536]{1,0:T(8,128)(2,1)} %param.22) | copy-start | bytes 7077892
  7.2 15.8 %copy-start.75 = (s32[32]{0:T(128)S(1)}, s32[32]{0:T(128)}, u32[]{:S(2)}) copy-start(s32[32]{0:T(128)} %param.30) | copy-start | bytes 388
  7.2 20.1 %copy-start.23 = (bf16[768,384]{1,0:T(8,128)(2,1)S(1)}, bf16[768,384]{1,0:T(8,128)(2,1)}, u32[]{:S(2)}) copy-start(bf16[768,384]{1,0:T(8,128)(2,1)} %param.18) | copy-start | bytes 1769476
  7.2 21.0 %copy-start.29 = (bf16[32,8,64]{2,1,0:T(8,128)(2,1)S(1)}, bf16[32,8,64]{2,1,0:T(8,128)(2,1)}, u32[]{:S(2)}) copy-start(bf16[32,8,64]{2,1,0:T(8,128)(2,1)} %param.29) | copy-start | bytes 98308
  7.2 530.4 %all-reduce.8.cloned.1.call-start = ((), (), s32[]{:S(2)}) async-start(), calls=%async_computation | async-start | bytes 10616832 | tf_op jit(solution)/shard_map/psum | solution.py:1125
  10.1 71.3 %collective-permute-start = (bf16[512,768]{1,0:T(8,128)(2,1)}, bf16[512,768]{1,0:T(8,128)(2,1)}, u32[]{:S(2)}, u32[]{:S(2)}) collective-permute-start(bf16[512,768]{1,0:T(8,128)(2,1)} %get-tuple-element.82.refs_0_), channel_id=1, source_target_pairs={{0,4},{2,6},{4,8},{6,10},{8,12},{10,14},{12,16},{14,18},{16,20},{1... | collective-permute-start | bytes 2359304 | tf_op jit(solution)/shard_map/ppermute | solution.py:944
  15.9 65.6 %collective-permute-start.1 = (bf16[512,768]{1,0:T(8,128)(2,1)}, bf16[512,768]{1,0:T(8,128)(2,1)}, u32[]{:S(2)}, u32[]{:S(2)}) collective-permute-start(bf16[512,768]{1,0:T(8,128)(2,1)} %get-tuple-element.82.refs_0_), channel_id=1, source_target_pairs={{0,2},{2,4},{4,6},{6,8},{8,10},{10,12},{12,14},{14,16},{16,18},{18... | collective-permute-start | bytes 2359304 | tf_op jit(solution)/shard_map/ppermute | solution.py:944
  20.2 61.3 %collective-permute-start.2 = (bf16[512,768]{1,0:T(8,128)(2,1)}, bf16[512,768]{1,0:T(8,128)(2,1)}, u32[]{:S(2)}, u32[]{:S(2)}) collective-permute-start(bf16[512,768]{1,0:T(8,128)(2,1)} %get-tuple-element.82.refs_0_), channel_id=1, source_target_pairs={{2,0},{4,2},{6,4},{8,6},{10,8},{12,10},{14,12},{16,14},{18,16},{20... | collective-permute-start | bytes 2359304 | tf_op jit(solution)/shard_map/ppermute | solution.py:944
  21.5 60.0 %collective-permute-start.3 = (bf16[512,768]{1,0:T(8,128)(2,1)}, bf16[512,768]{1,0:T(8,128)(2,1)}, u32[]{:S(2)}, u32[]{:S(2)}) collective-permute-start(bf16[512,768]{1,0:T(8,128)(2,1)} %get-tuple-element.82.refs_0_), channel_id=1, source_target_pairs={{4,0},{6,2},{8,4},{10,6},{12,8},{14,10},{16,12},{18,14},{20,16},{2... | collective-permute-start | bytes 2359304 | tf_op jit(solution)/shard_map/ppermute | solution.py:944
  38.8 14.5 %copy-start.42 = (s32[256]{0:T(256)}, s32[256]{0:T(256)S(1)}, u32[]{:S(2)}) copy-start(s32[256]{0:T(256)S(1)} %get-tuple-element.215) | copy-start | bytes 3076
  38.8 14.5 %copy-start.44 = (s32[256]{0:T(256)}, s32[256]{0:T(256)S(1)}, u32[]{:S(2)}) copy-start(s32[256]{0:T(256)S(1)} %get-tuple-element.216) | copy-start | bytes 3076
  38.8 14.5 %copy-start.46 = (s32[256]{0:T(256)}, s32[256]{0:T(256)S(1)}, u32[]{:S(2)}) copy-start(s32[256]{0:T(256)S(1)} %get-tuple-element.217) | copy-start | bytes 3076
  81.5 29.3 %collective-permute-start.10 = (bf16[512,768]{1,0:T(8,128)(2,1)}, bf16[512,768]{1,0:T(8,128)(2,1)S(1)}, u32[]{:S(2)}, u32[]{:S(2)}) collective-permute-start(bf16[512,768]{1,0:T(8,128)(2,1)} %collective-permute-done.2.refs_2_), channel_id=1, source_target_pairs={{0,1},{1,0},{2,3},{3,2},{4,5},{5,4},{6,7},{7,6},{8,9},{9,8},{10,11... | collective-permute-start | bytes 2359304 | tf_op jit(solution)/shard_map/ppermute | solution.py:948
  81.5 32.1 %collective-permute-start.11 = (bf16[512,768]{1,0:T(8,128)(2,1)}, bf16[512,768]{1,0:T(8,128)(2,1)S(1)}, u32[]{:S(2)}, u32[]{:S(2)}) collective-permute-start(bf16[512,768]{1,0:T(8,128)(2,1)} %collective-permute-done.3.refs_3_), channel_id=1, source_target_pairs={{0,1},{1,0},{2,3},{3,2},{4,5},{5,4},{6,7},{7,6},{8,9},{9,8},{10,11... | collective-permute-start | bytes 2359304 | tf_op jit(solution)/shard_map/ppermute | solution.py:948
  82.0 32.9 %collective-permute-start.8 = (bf16[512,768]{1,0:T(8,128)(2,1)}, bf16[512,768]{1,0:T(8,128)(2,1)S(1)}, u32[]{:S(2)}, u32[]{:S(2)}) collective-permute-start(bf16[512,768]{1,0:T(8,128)(2,1)} %collective-permute-done.refs_0_), channel_id=1, source_target_pairs={{0,1},{1,0},{2,3},{3,2},{4,5},{5,4},{6,7},{7,6},{8,9},{9,8},{10,11... | collective-permute-start | bytes 2359304 | tf_op jit(solution)/shard_map/ppermute | solution.py:948
  82.1 34.2 %collective-permute-start.9 = (bf16[512,768]{1,0:T(8,128)(2,1)}, bf16[512,768]{1,0:T(8,128)(2,1)S(1)}, u32[]{:S(2)}, u32[]{:S(2)}) collective-permute-start(bf16[512,768]{1,0:T(8,128)(2,1)} %collective-permute-done.1.refs_1_), channel_id=1, source_target_pairs={{0,1},{1,0},{2,3},{3,2},{4,5},{5,4},{6,7},{7,6},{8,9},{9,8},{10,11... | collective-permute-start | bytes 2359304 | tf_op jit(solution)/shard_map/ppermute | solution.py:948
  82.6 46.7 %collective-permute-start.4 = (bf16[512,768]{1,0:T(8,128)(2,1)}, bf16[512,768]{1,0:T(8,128)(2,1)S(1)}, u32[]{:S(2)}, u32[]{:S(2)}) collective-permute-start(bf16[512,768]{1,0:T(8,128)(2,1)} %get-tuple-element.82.refs_0_), channel_id=1, source_target_pairs={{0,8},{2,10},{4,12},{6,14},{8,16},{10,18},{12,20},{14,22},{16,24},... | collective-permute-start | bytes 2359304 | tf_op jit(solution)/shard_map/ppermute | solution.py:944
  110.8 36.8 %collective-permute-start.5 = (bf16[512,768]{1,0:T(8,128)(2,1)}, bf16[512,768]{1,0:T(8,128)(2,1)S(1)}, u32[]{:S(2)}, u32[]{:S(2)}) collective-permute-start(bf16[512,768]{1,0:T(8,128)(2,1)} %get-tuple-element.82.refs_0_), channel_id=1, source_target_pairs={{0,6},{2,8},{4,10},{6,12},{8,14},{10,16},{12,18},{14,20},{16,22},{... | collective-permute-start | bytes 2359304 | tf_op jit(solution)/shard_map/ppermute | solution.py:944
  113.7 33.9 %collective-permute-start.6 = (bf16[512,768]{1,0:T(8,128)(2,1)}, bf16[512,768]{1,0:T(8,128)(2,1)S(1)}, u32[]{:S(2)}, u32[]{:S(2)}) collective-permute-start(bf16[512,768]{1,0:T(8,128)(2,1)} %get-tuple-element.82.refs_0_), channel_id=1, source_target_pairs={{6,0},{8,2},{10,4},{12,6},{14,8},{16,10},{18,12},{20,14},{22,16},{... | collective-permute-start | bytes 2359304 | tf_op jit(solution)/shard_map/ppermute | solution.py:944
  115.0 38.2 %collective-permute-start.7 = (bf16[512,768]{1,0:T(8,128)(2,1)}, bf16[512,768]{1,0:T(8,128)(2,1)}, u32[]{:S(2)}, u32[]{:S(2)}) collective-permute-start(bf16[512,768]{1,0:T(8,128)(2,1)} %get-tuple-element.82.refs_0_), channel_id=1, source_target_pairs={{8,0},{10,2},{12,4},{14,6},{16,8},{18,10},{20,12},{22,14},{24,16},... | collective-permute-start | bytes 2359304 | tf_op jit(solution)/shard_map/ppermute | solution.py:944
  129.2 66.4 %copy-start.17 = (bf16[512,768]{1,0:T(8,128)(2,1)}, bf16[512,768]{1,0:T(8,128)(2,1)S(1)}, u32[]{:S(2)}) copy-start(bf16[512,768]{1,0:T(8,128)(2,1)S(1)} %collective-permute-done.4.refs_0_) | copy-start | bytes 2359300
  147.6 48.1 %copy-start.18 = (bf16[512,768]{1,0:T(8,128)(2,1)}, bf16[512,768]{1,0:T(8,128)(2,1)S(1)}, u32[]{:S(2)}) copy-start(bf16[512,768]{1,0:T(8,128)(2,1)S(1)} %collective-permute-done.5.refs_1_) | copy-start | bytes 2359300
  147.6 48.1 %copy-start.19 = (bf16[512,768]{1,0:T(8,128)(2,1)}, bf16[512,768]{1,0:T(8,128)(2,1)S(1)}, u32[]{:S(2)}) copy-start(bf16[512,768]{1,0:T(8,128)(2,1)S(1)} %collective-permute-done.6.refs_2_) | copy-start | bytes 2359300
  153.3 43.9 %collective-permute-start.12 = (bf16[512,768]{1,0:T(8,128)(2,1)S(1)}, bf16[512,768]{1,0:T(8,128)(2,1)S(1)}, u32[]{:S(2)}, u32[]{:S(2)}) collective-permute-start(bf16[512,768]{1,0:T(8,128)(2,1)S(1)} %collective-permute-done.4.refs_0_), channel_id=1, source_target_pairs={{0,1},{1,0},{2,3},{3,2},{4,5},{5,4},{6,7},{7,6},{8,9},{9,8},{10,11... | collective-permute-start | bytes 2359304 | tf_op jit(solution)/shard_map/ppermute | solution.py:948
  153.3 43.9 %collective-permute-start.13 = (bf16[512,768]{1,0:T(8,128)(2,1)S(1)}, bf16[512,768]{1,0:T(8,128)(2,1)S(1)}, u32[]{:S(2)}, u32[]{:S(2)}) collective-permute-start(bf16[512,768]{1,0:T(8,128)(2,1)S(1)} %collective-permute-done.5.refs_1_), channel_id=1, source_target_pairs={{0,1},{1,0},{2,3},{3,2},{4,5},{5,4},{6,7},{7,6},{8,9},{9,8},{10,11... | collective-permute-start | bytes 2359304 | tf_op jit(solution)/shard_map/ppermute | solution.py:948
  153.8 43.4 %collective-permute-start.14 = (bf16[512,768]{1,0:T(8,128)(2,1)S(1)}, bf16[512,768]{1,0:T(8,128)(2,1)S(1)}, u32[]{:S(2)}, u32[]{:S(2)}) collective-permute-start(bf16[512,768]{1,0:T(8,128)(2,1)S(1)} %collective-permute-done.6.refs_2_), channel_id=1, source_target_pairs={{0,1},{1,0},{2,3},{3,2},{4,5},{5,4},{6,7},{7,6},{8,9},{9,8},{10,11... | collective-permute-start | bytes 2359304 | tf_op jit(solution)/shard_map/ppermute | solution.py:948
  153.8 43.4 %collective-permute-start.15 = (bf16[512,768]{1,0:T(8,128)(2,1)}, bf16[512,768]{1,0:T(8,128)(2,1)S(1)}, u32[]{:S(2)}, u32[]{:S(2)}) collective-permute-start(bf16[512,768]{1,0:T(8,128)(2,1)} %collective-permute-done.7.refs_3_), channel_id=1, source_target_pairs={{0,1},{1,0},{2,3},{3,2},{4,5},{5,4},{6,7},{7,6},{8,9},{9,8},{10,11... | collective-permute-start | bytes 2359304 | tf_op jit(solution)/shard_map/ppermute | solution.py:948
  154.3 41.4 %copy-start.74 = (pred[32]{0:T(512)(128)(4,1)S(1)}, pred[32]{0:T(512)(128)(4,1)}, u32[]{:S(2)}) copy-start(pred[32]{0:T(512)(128)(4,1)} %gt.25) | copy-start | bytes 100
  224.7 3.5 collective-permute-start.16
  229.6 17.1 %copy-start.76 = (bf16[1536,768]{1,0:T(8,128)(2,1)S(1)}, bf16[1536,768]{1,0:T(8,128)(2,1)}, u32[]{:S(2)}) copy-start(bf16[1536,768]{1,0:T(8,128)(2,1)} %param.23) | copy-start | bytes 7077892
  249.3 3.5 collective-permute-start.17
  268.4 7.8 %collective-permute-start.18 = (bf16[1024,768]{1,0:T(8,128)(2,1)S(1)}, bf16[1024,768]{1,0:T(8,128)(2,1)S(1)}, u32[]{:S(2)}, u32[]{:S(2)}) collective-permute-start(bf16[1024,768]{1,0:T(8,128)(2,1)S(1)} %convolution_convert_fusion.3), channel_id=1, source_target_pairs={{0,1},{1,0},{2,3},{3,2},{4,5},{5,4},{6,7},{7,6},{8,9},{9,8},{10,11... | collective-permute-start | bytes 4718600 | tf_op jit(solution)/shard_map/ppermute | solution.py:948
  311.7 103.2 %collective-permute-start.19 = (bf16[2048,768]{1,0:T(8,128)(2,1)}, bf16[2048,768]{1,0:T(8,128)(2,1)}, u32[]{:S(2)}, u32[]{:S(2)}) collective-permute-start(bf16[2048,768]{1,0:T(8,128)(2,1)} %get-tuple-element.106), channel_id=1, source_target_pairs={{0,1},{1,0},{2,3},{3,2},{4,5},{5,4},{6,7},{7,6},{8,9},{9,8},{10,11... | collective-permute-start | bytes 9437192 | tf_op jit(solution)/shard_map/ppermute | solution.py:948
  414.1 185.8 %collective-permute-start.24 = (bf16[2048,768]{1,0:T(8,128)(2,1)}, bf16[2048,768]{1,0:T(8,128)(2,1)}, u32[]{:S(2)}, u32[]{:S(2)}) collective-permute-start(bf16[2048,768]{1,0:T(8,128)(2,1)} %get-tuple-element.120), channel_id=1, source_target_pairs={{0,1},{1,0},{2,3},{3,2},{4,5},{5,4},{6,7},{7,6},{8,9},{9,8},{10,11... | collective-permute-start | bytes 9437192 | tf_op jit(solution)/shard_map/ppermute | solution.py:948
  542.3 62.9 %collective-permute-start.20 = (bf16[512,768]{1,0:T(8,128)(2,1)}, bf16[512,768]{1,0:T(8,128)(2,1)}, u32[]{:S(2)}, u32[]{:S(2)}) collective-permute-start(bf16[512,768]{1,0:T(8,128)(2,1)} %get-tuple-element.186), channel_id=1, source_target_pairs={{8,0},{10,2},{12,4},{14,6},{16,8},{18,10},{20,12},{22,14},{24,16},... | collective-permute-start | bytes 2359304 | tf_op jit(solution)/shard_map/ppermute | solution.py:944
  543.6 62.9 %collective-permute-start.21 = (bf16[512,768]{1,0:T(8,128)(2,1)S(1)}, bf16[512,768]{1,0:T(8,128)(2,1)}, u32[]{:S(2)}, u32[]{:S(2)}) collective-permute-start(bf16[512,768]{1,0:T(8,128)(2,1)S(1)} %get-tuple-element.185), channel_id=1, source_target_pairs={{6,0},{8,2},{10,4},{12,6},{14,8},{16,10},{18,12},{20,14},{22,16},{... | collective-permute-start | bytes 2359304 | tf_op jit(solution)/shard_map/ppermute | solution.py:944
  544.9 67.1 %collective-permute-start.22 = (bf16[512,768]{1,0:T(8,128)(2,1)S(1)}, bf16[512,768]{1,0:T(8,128)(2,1)}, u32[]{:S(2)}, u32[]{:S(2)}) collective-permute-start(bf16[512,768]{1,0:T(8,128)(2,1)S(1)} %get-tuple-element.184), channel_id=1, source_target_pairs={{0,6},{2,8},{4,10},{6,12},{8,14},{10,16},{12,18},{14,20},{16,22},{... | collective-permute-start | bytes 2359304 | tf_op jit(solution)/shard_map/ppermute | solution.py:944
  551.2 97.5 %collective-permute-start.23 = (bf16[512,768]{1,0:T(8,128)(2,1)}, bf16[512,768]{1,0:T(8,128)(2,1)}, u32[]{:S(2)}, u32[]{:S(2)}) collective-permute-start(bf16[512,768]{1,0:T(8,128)(2,1)} %get-tuple-element.183), channel_id=1, source_target_pairs={{0,8},{2,10},{4,12},{6,14},{8,16},{10,18},{12,20},{14,22},{16,24},... | collective-permute-start | bytes 2359304 | tf_op jit(solution)/shard_map/ppermute | solution.py:944
  555.8 44.1 %copy-start.5 = (bf16[2048,768]{1,0:T(8,128)(2,1)S(1)}, bf16[2048,768]{1,0:T(8,128)(2,1)}, u32[]{:S(2)}) copy-start(bf16[2048,768]{1,0:T(8,128)(2,1)} %get-tuple-element.113) | copy-start | bytes 9437188
  599.9 39.1 %copy-start.26 = (s32[44]{0:T(128)S(1)}, s32[44]{0:T(128)}, u32[]{:S(2)}) copy-start(s32[44]{0:T(128)} %copy-done.24) | copy-start | bytes 532
  603.9 76.9 %collective-permute-start.26 = (bf16[512,768]{1,0:T(8,128)(2,1)}, bf16[512,768]{1,0:T(8,128)(2,1)}, u32[]{:S(2)}, u32[]{:S(2)}) collective-permute-start(bf16[512,768]{1,0:T(8,128)(2,1)} %get-tuple-element.182), channel_id=1, source_target_pairs={{4,0},{6,2},{8,4},{10,6},{12,8},{14,10},{16,12},{18,14},{20,16},{2... | collective-permute-start | bytes 2359304 | tf_op jit(solution)/shard_map/ppermute | solution.py:944
  605.2 75.7 %collective-permute-start.27 = (bf16[512,768]{1,0:T(8,128)(2,1)}, bf16[512,768]{1,0:T(8,128)(2,1)}, u32[]{:S(2)}, u32[]{:S(2)}) collective-permute-start(bf16[512,768]{1,0:T(8,128)(2,1)} %get-tuple-element.181), channel_id=1, source_target_pairs={{2,0},{4,2},{6,4},{8,6},{10,8},{12,10},{14,12},{16,14},{18,16},{20... | collective-permute-start | bytes 2359304 | tf_op jit(solution)/shard_map/ppermute | solution.py:944
  606.5 74.3 %collective-permute-start.28 = (bf16[512,768]{1,0:T(8,128)(2,1)}, bf16[512,768]{1,0:T(8,128)(2,1)}, u32[]{:S(2)}, u32[]{:S(2)}) collective-permute-start(bf16[512,768]{1,0:T(8,128)(2,1)} %get-tuple-element.180), channel_id=1, source_target_pairs={{0,2},{2,4},{4,6},{6,8},{8,10},{10,12},{12,14},{14,16},{16,18},{18... | collective-permute-start | bytes 2359304 | tf_op jit(solution)/shard_map/ppermute | solution.py:944
  612.0 69.5 %collective-permute-start.29 = (bf16[512,768]{1,0:T(8,128)(2,1)}, bf16[512,768]{1,0:T(8,128)(2,1)}, u32[]{:S(2)}, u32[]{:S(2)}) collective-permute-start(bf16[512,768]{1,0:T(8,128)(2,1)} %get-tuple-element.179), channel_id=1, source_target_pairs={{0,4},{2,6},{4,8},{6,10},{8,12},{10,14},{12,16},{14,18},{16,20},{1... | collective-permute-start | bytes 2359304 | tf_op jit(solution)/shard_map/ppermute | solution.py:944
  648.8 15.6 %copy-start.16 = (f32[6,32,256]{2,1,0:T(8,128)S(1)}, f32[6,32,256]{2,1,0:T(8,128)}, u32[]{:S(2)}) copy-start(f32[6,32,256]{2,1,0:T(8,128)} %broadcast_multiply_fusion) | copy-start | bytes 589828
  648.8 15.8 %copy-start.64 = (f32[8,256]{1,0:T(8,128)S(1)}, f32[8,256]{1,0:T(8,128)}, u32[]{:S(2)}) copy-start(f32[8,256]{1,0:T(8,128)} %get-tuple-element.137) | copy-start | bytes 24580
  664.3 20.3 %collective-permute-start.25 = (bf16[512,768]{1,0:T(8,128)(2,1)}, bf16[512,768]{1,0:T(8,128)(2,1)}, u32[]{:S(2)}, u32[]{:S(2)}) collective-permute-start(bf16[512,768]{1,0:T(8,128)(2,1)} %get-tuple-element.125), channel_id=1, source_target_pairs={{0,1},{1,0},{2,3},{3,2},{4,5},{5,4},{6,7},{7,6},{8,9},{9,8},{10,11... | collective-permute-start | bytes 2359304 | tf_op jit(solution)/shard_map/ppermute | solution.py:948
  689.9 66.2 %collective-permute-start.30 = (f32[512,768]{1,0:T(8,128)}, f32[512,768]{1,0:T(8,128)S(1)}, u32[]{:S(2)}, u32[]{:S(2)}) collective-permute-start(f32[512,768]{1,0:T(8,128)} %convert_add_fusion), channel_id=1, source_target_pairs={{0,1},{1,0},{2,3},{3,2},{4,5},{5,4},{6,7},{7,6},{8,9},{9,8},{10,11... | collective-permute-start | bytes 4718600 | tf_op jit(solution)/shard_map/ppermute | solution.py:948
  (63 other events, 417.0 us)
Sparse Core Ops, SparseCore 0:
  286.0 251.5 all-reduce.7
